TPU v7x, 256 devices: a whole 4x4x8 slice. The times are simulated.
256 devices in a mesh: samp: 64 (over z, y, core), var: 4 (over x).
Axes of the slice: x: 4, y: 4, z: 8, core: 2. Of those that a mesh axis runs over, the one named last changes fastest.
Arguments:
- dosage: bfloat16 [16384, 40960], P('samp', 'var'), may hold values from 0 to 2
- centers: float32 [40960], replicated, may hold values from 0.4 to 1.34
- scales: float32 [40960], replicated, may hold values from 1.6 to 2.2
- phenotype: float32 [16384], P('samp'), may hold values from -6 to 6
- fold_ids: int32 [16384], P('samp'), may hold values from 0 to 3
- strong_blocks: int32 [32], replicated, may hold values from 0 to 319, as said below
- warm_start: float32 [4096, 32], replicated, may hold values from -4 to 4
- penalty: float32 [8], replicated, may hold values from 0.05 to 0.5
- step_size: float32 [32], replicated, may hold values from 0.2 to 0.6
Outputs:
- margin: float32 [40960], P('var')
- coefficients: float32 [4096, 32], P('var')
Inputs may be any that keep to these rules, and one draw needn't show every extreme that they name: `strong_blocks`: 32 different block numbers.
All inputs are finite; a program needn't handle non-finite values.
Results may differ from a plain program's by a relative error of at most 0.0075.
Values may be sent and summed in bfloat16 or wider, within the bound.
No kernel may reach another device: no remote copies, remote signals or barrier semaphores. Data moves between devices by JAX's collectives and lax.ppermute only.
A program may use at most 64 MiB of HBM per device.

v0:
```python
import math

import jax
import jax.numpy as jnp
from jax import lax
from jax.sharding import PartitionSpec as P

BLOCK = 128
NS = 4096
LAMBDAS = 8
FOLDS = 4
ITERS = 3


exact_mode = lax.Precision.HIGHEST


def shards(
    dosage, centers, scales, phenotype, fold_ids, strong_blocks, warm_start, penalty, step_size
):
    rows, local_width = dosage.shape
    groups = lax.axis_size("var")
    place = lax.axis_index("var")
    fit_total = LAMBDAS * FOLDS
    fit_folds = jnp.arange(fit_total, dtype=jnp.int32) % FOLDS
    weights = (fold_ids[:, None] != fit_folds[None, :]).astype(jnp.float32)
    counts = lax.psum(jnp.sum(weights, axis=0), "samp")
    fit_penalty = jnp.repeat(penalty, FOLDS)
    threshold = step_size * fit_penalty
    local_blocks = local_width // BLOCK
    relative = strong_blocks - place * local_blocks
    owned = (relative >= 0) & (relative < local_blocks)
    picked = jnp.take(
        dosage.reshape(rows, local_blocks, BLOCK), jnp.clip(relative, 0, local_blocks - 1), axis=1
    )
    masked = (picked * owned.astype(jnp.bfloat16)[None, :, None]).reshape(rows, NS)
    columns = (
        strong_blocks[:, None] * BLOCK + jnp.arange(BLOCK, dtype=jnp.int32)[None, :]
    ).reshape(NS)
    strong_centers = centers[columns]
    strong_scales = scales[columns]
    owned_columns = jnp.repeat(owned.astype(jnp.float32), BLOCK)
    share = NS // groups
    point = warm_start
    part_centers = strong_centers * owned_columns
    part_threshold = threshold[None, :]

    def residual_of(coef):
        scaled = (strong_scales[:, None] * coef).astype(jnp.bfloat16)
        partial_fit = jnp.dot(masked, scaled, preferred_element_type=jnp.float32)
        partial_fit = (
            partial_fit - jnp.dot(part_centers * strong_scales, coef, precision=exact_mode)[None, :]
        )
        fitted = lax.psum(partial_fit.astype(jnp.bfloat16), "var").astype(jnp.float32)
        return (weights * (phenotype[:, None] - fitted)).astype(jnp.bfloat16)

    rounded = residual_of(point)
    column_sums = jnp.sum(rounded.astype(jnp.float32), axis=0)
    local_centers = lax.dynamic_slice_in_dim(centers, place * local_width, local_width, 0)
    local_scales = lax.dynamic_slice_in_dim(scales, place * local_width, local_width, 0)
    cross = lax.dot_general(
        dosage, rounded, (((0,), (0,)), ((), ())), preferred_element_type=jnp.float32
    )
    total = lax.psum(cross - local_centers[:, None] * column_sums[None, :], "samp")
    margin = jnp.max(
        jnp.abs(local_scales[:, None] * total / counts[None, :]) / fit_penalty[None, :], axis=1
    )
    momentum = 1.0
    previous = point
    for sweep in range(ITERS):
        if sweep > 0:
            rounded = residual_of(point)
            column_sums = jnp.sum(rounded.astype(jnp.float32), axis=0)
        gradient_cross = lax.dot_general(
            masked, rounded, (((0,), (0,)), ((), ())), preferred_element_type=jnp.float32
        )
        gradient_cross = gradient_cross - part_centers[:, None] * column_sums[None, :]
        gradient_total = lax.psum(gradient_cross, ("samp", "var"))
        moved = point + step_size[None, :] * (
            strong_scales[:, None] * gradient_total / counts[None, :]
        )
        current = moved - jnp.clip(moved, -part_threshold, part_threshold)
        following = (1.0 + math.sqrt(1.0 + 4.0 * momentum * momentum)) / 2.0
        point = current + (momentum - 1.0) / following * (current - previous)
        previous = current
        momentum = following
    coefficients = lax.dynamic_slice_in_dim(previous, place * share, share, 0)
    return (margin, coefficients)


def solution(mesh):
    return jax.shard_map(
        shards,
        mesh=mesh,
        in_specs=(P("samp", "var"), P(), P(), P("samp"), P("samp"), P(), P(), P(), P()),
        out_specs=(P("var"), P("var", None)),
        check_vma=False,
    )
```

profile of v0, /device:TPU:1, one launch (start us, length us, event | category | flops | bytes accessed | tf_op | source)
XLA Modules:
  0.0 1087.3 jit_solution(17105678928884932665)
XLA Ops:
  7.2 7.9 copy.11
  15.2 7.9 copy.12
  23.1 3.4 gather_fusion
  26.6 2.9 copy.13
  29.8 23.0 %gather_fusion.1 = f32[4096]{0:T(1024)S(1)} fusion(f32[40960]{0:T(1024)S(1)} %copy-done.1, s32[4096]{0:T(1024)S(1)} %broadcast_clamp_fusion), kind=kCustom, calls=%fused_computation.1 | custom fusion | bytes 49152 | tf_op jit(solution)/shard_map/gather | solution.py:41
  52.9 23.0 %gather_fusion.2 = f32[4096]{0:T(1024)S(1)} fusion(f32[40960]{0:T(1024)S(1)} %copy-done, s32[4096]{0:T(1024)S(1)} %broadcast_clamp_fusion), kind=kCustom, calls=%fused_computation.2 | custom fusion | bytes 49152 | tf_op jit(solution)/shard_map/gather | solution.py:40
  76.0 0.5 convolution_bitcast_fusion.3
  76.5 3.2 fusion.1
  79.7 0.4 fusion.3
  80.2 14.3 %psum.56 = bf16[256,32]{0,1:T(8,128)(2,1)S(1)} all-reduce(bf16[256,32]{0,1:T(8,128)(2,1)S(1)} %fusion.3), channel_id=1, replica_groups=mesh['samp'=64,'var'=4] {'var'}, use_global_device_ids=true, to_apply=%region_0.1 | all-reduce | flops 8192 | bytes 32768 | tf_op jit(solution)/shard_map/psum | solution.py:54
  94.5 0.2 fusion.11
  94.7 1.5 convolution_subtract_fusion.2
  96.4 131.0 %psum.58 = f32[32]{0:T(128)S(1)} all-reduce(f32[32]{0:T(128)S(1)} %get-tuple-element.2), channel_id=1, replica_groups=mesh['samp'=64,'var'=4] {'samp'}, use_global_device_ids=true, to_apply=%region_4.5 | all-reduce | flops 32 | bytes 256 | tf_op jit(solution)/shard_map/psum | solution.py:27
  227.5 128.0 %all-reduce.7.cloned.1.call-done = f32[4096,32]{0,1:T(8,128)} async-done(((f32[4096,32]{0,1:T(8,128)}), f32[4096,32]{0,1:T(8,128)}) %all-reduce.7.cloned.1.call-update) | async-done | bytes 524304 | tf_op jit(solution)/shard_map/psum | solution.py:78
  355.4 1.8 convolution_bitcast_fusion.2
  357.2 0.5 fusion.4
  357.8 13.0 %psum.60 = bf16[256,32]{0,1:T(8,128)(2,1)S(1)} all-reduce(bf16[256,32]{0,1:T(8,128)(2,1)S(1)} %fusion.4), channel_id=1, replica_groups=mesh['samp'=64,'var'=4] {'var'}, use_global_device_ids=true, to_apply=%region_7.8 | all-reduce | flops 8192 | bytes 32768 | tf_op jit(solution)/shard_map/psum | solution.py:54
  370.8 0.2 convert_reduce_fusion.1
  371.0 1.5 convolution_subtract_fusion.1
  372.7 4.6 fusion
  377.4 251.2 %all-reduce.9.cloned.1.call-done = f32[4096,32]{0,1:T(8,128)} async-done(((f32[4096,32]{0,1:T(8,128)}), f32[4096,32]{0,1:T(8,128)}) %all-reduce.9.cloned.1.call-update) | async-done | bytes 524304 | tf_op jit(solution)/shard_map/psum | solution.py:78
  628.6 1.6 multiply_add_fusion
  630.2 0.5 convolution_bitcast_fusion.1
  630.7 0.4 fusion.5
  631.2 12.9 %psum.62 = bf16[256,32]{0,1:T(8,128)(2,1)S(1)} all-reduce(bf16[256,32]{0,1:T(8,128)(2,1)S(1)} %fusion.5), channel_id=1, replica_groups=mesh['samp'=64,'var'=4] {'var'}, use_global_device_ids=true, to_apply=%region_10.11 | all-reduce | flops 8192 | bytes 32768 | tf_op jit(solution)/shard_map/psum | solution.py:54
  644.1 0.2 convert_reduce_fusion
  644.3 1.5 convolution_subtract_fusion
  645.8 173.4 %all-reduce.5.cloned.1.call-done = f32[10240,32]{0,1:T(8,128)} async-done(((f32[10240,32]{0,1:T(8,128)}), f32[10240,32]{0,1:T(8,128)}) %all-reduce.5.cloned.1.call-update) | async-done | bytes 1310736 | tf_op jit(solution)/shard_map/psum | solution.py:64
  819.2 2.3 fusion.2
  821.5 257.4 %all-reduce.11.cloned.1.call-done = f32[4096,32]{0,1:T(8,128)} async-done(((f32[4096,32]{0,1:T(8,128)}), f32[4096,32]{0,1:T(8,128)}) %all-reduce.11.cloned.1.call-update) | async-done | bytes 524304 | tf_op jit(solution)/shard_map/psum | solution.py:78
  1078.9 1.1 broadcast_multiply_fusion
  1080.0 0.8 minimum_subtract_fusion.1
  (48 shorter events, 0.8 us)
Async XLA Ops:
  7.2 348.3 %all-reduce.7.cloned.1.call-start = ((), (), s32[]{:S(2)}) async-start(), calls=%async_computation.1 | async-start | bytes 1048576 | tf_op jit(solution)/shard_map/psum | solution.py:78
  15.2 7.9 copy-start.10
  26.6 3.2 copy-start.1
  29.8 23.1 %copy-start = (f32[40960]{0:T(1024)S(1)}, f32[40960]{0:T(1024)}, u32[]{:S(2)}) copy-start(f32[40960]{0:T(1024)} %param.10) | copy-start | bytes 491524
  52.8 23.1 %copy-start.2 = (f32[4096,32]{0,1:T(8,128)S(1)}, f32[4096,32]{0,1:T(8,128)}, u32[]{:S(2)}) copy-start(f32[4096,32]{0,1:T(8,128)} %param.15) | copy-start | bytes 1572868
  79.7 14.8 %copy-start.4 = (s32[256]{0:T(256)S(1)}, s32[256]{0:T(256)}, u32[]{:S(2)}) copy-start(s32[256]{0:T(256)} %param.13) | copy-start | bytes 3076
  79.7 14.8 %copy-start.5 = (f32[256]{0:T(256)S(1)}, f32[256]{0:T(256)}, u32[]{:S(2)}) copy-start(f32[256]{0:T(256)} %param.12) | copy-start | bytes 3076
  80.1 16.1 %copy-start.9 = (f32[8]{0:T(128)S(1)}, f32[8]{0:T(128)}, u32[]{:S(2)}) copy-start(f32[8]{0:T(128)} %param.16) | copy-start | bytes 100
  80.2 147.3 %copy-start.6 = (f32[32]{0:T(128)S(1)}, f32[32]{0:T(128)}, u32[]{:S(2)}) copy-start(f32[32]{0:T(128)} %param.17) | copy-start | bytes 388
  94.7 132.8 %copy-start.7 = (f32[32]{0:T(128)}, f32[32]{0:T(128)S(1)}, u32[]{:S(2)}) copy-start(f32[32]{0:T(128)S(1)} %get-tuple-element.3) | copy-start | bytes 388
  96.2 532.4 %all-reduce.9.cloned.1.call-start = ((), (), s32[]{:S(2)}) async-start(), calls=%async_computation.2 | async-start | bytes 1048576 | tf_op jit(solution)/shard_map/psum | solution.py:78
  355.4 1.8 copy-start.3
  357.8 14.9 %dynamic-slice-start = ((f32[40960]{0:T(1024)}, s32[]{:T(128)}), f32[10240]{0:T(1024)S(1)}, s32[]{:S(2)}) async-start(f32[40960]{0:T(1024)} %param.10, s32[]{:T(128)} %select_n.39), calls=%async_computation.4 | async-start | bytes 82432 | tf_op jit(solution)/shard_map/dynamic_slice | solution.py:59
  357.8 14.9 %copy-start.8 = (f32[32]{0:T(128)S(1)}, f32[32]{0:T(128)}, u32[]{:S(2)}) copy-start(f32[32]{0:T(128)} %copy-done.7) | copy-start | bytes 388
  372.6 446.6 %all-reduce.5.cloned.1.call-start = ((), (), s32[]{:S(2)}) async-start(), calls=%async_computation | async-start | bytes 2621440 | tf_op jit(solution)/shard_map/psum | solution.py:64
  377.3 701.6 %all-reduce.11.cloned.1.call-start = ((), (), s32[]{:S(2)}) async-start(), calls=%async_computation.3 | async-start | bytes 1048576 | tf_op jit(solution)/shard_map/psum | solution.py:78
  631.2 188.0 %dynamic-slice-start.1 = ((f32[40960]{0:T(1024)}, s32[]{:T(128)}), f32[10240]{0:T(1024)S(1)}, s32[]{:S(2)}) async-start(f32[40960]{0:T(1024)} %param.11, s32[]{:T(128)} %select_n.39), calls=%async_computation.5 | async-start | bytes 82432 | tf_op jit(solution)/shard_map/dynamic_slice | solution.py:60
Sparse Core Ops, SparseCore 0:
  96.3 259.0 all-reduce.6
  372.7 255.8 all-reduce.8
  632.0 187.1 all-reduce.4
  824.5 254.2 all-reduce.10
where the time goes:
time: 1090 us
  waiting for transfers between devices  810 us (74%)
  blocking collectives  171 us (16%)
  local copies, waits for them, and re-layouts  68.7 us (6%)
  between operations  14 us (1%)
  matrix products  13.4 us (1%)
    psum x3, waiting for transfers between devices, shards(): gradient_total = lax.psum(gradient_cross, ('samp', 'var'))  637 us
    psum x1, waiting for transfers between devices, shards(): lax.psum(cross - local_centers[:, None] * column_sums[None, :], 'samp')  173 us
    psum x1, blocking collectives, shards(): counts = lax.psum(jnp.sum(weights, axis=0), 'samp')  131 us
    psum x3, blocking collectives, residual_of(): lax.psum(partial_fit.astype(jnp.bfloat16), 'var').astype(jnp.float32)  40.2 us
    gather x1, local copies, waits for them, and re-layouts, shards(): strong_scales = scales[columns]  23 us
    gather x1, local copies, waits for them, and re-layouts, shards(): strong_centers = centers[columns]  23 us
  transfers between devices with their start and end apart: 4, of which 4 were waited for; matrix products, arithmetic and copies ran while one was open for 1% of the time, Pallas kernels for 0%

commit v1 on v0

v1 whole, which is shorter than its diff:
```python
import functools
import math

import jax
import jax.numpy as jnp
from jax import lax
from jax.experimental import pallas as pl
from jax.experimental.pallas import tpu as pltpu
from jax.sharding import Mesh
from jax.sharding import PartitionSpec as P

BLOCK = 128
SLOTS = 32
NS = SLOTS * BLOCK
LAMBDAS = 8
FOLDS = 4
FITS = LAMBDAS * FOLDS
HALF = FITS // 2
ITERS = 3
PLANE = ("z", "y")
PARTS = 32
MBLK = 3

f32 = jnp.float32
bf16 = jnp.bfloat16
exact_mode = lax.Precision.HIGHEST


def pick_kernel(width, index_ref, source_ref, out_ref, sem):
    def start(slot, carry):
        pltpu.make_async_copy(
            source_ref.at[:, pl.ds(pl.multiple_of(index_ref[slot] * BLOCK, BLOCK), BLOCK)],
            out_ref.at[:, pl.ds(pl.multiple_of(slot * BLOCK, BLOCK), BLOCK)],
            sem,
        ).start()
        return carry

    lax.fori_loop(0, SLOTS, start, 0)
    pltpu.make_async_copy(source_ref.at[:, pl.ds(0, NS)], out_ref, sem).wait()


def pick_blocks(dosage, index):
    rows, width = dosage.shape
    return pl.pallas_call(
        functools.partial(pick_kernel, width),
        grid_spec=pltpu.PrefetchScalarGridSpec(
            num_scalar_prefetch=1,
            grid=(1,),
            in_specs=[pl.BlockSpec(memory_space=pl.ANY)],
            out_specs=pl.BlockSpec((rows, NS), lambda i, s: (0, 0)),
            scratch_shapes=[pltpu.SemaphoreType.DMA],
        ),
        out_shape=jax.ShapeDtypeStruct((rows, NS), bf16),
        name="pick_blocks",
    )(index, dosage)


def spread(payload, axis, count):
    return lax.all_to_all(
        jnp.broadcast_to(payload[None], (count,) + payload.shape), axis, 0, 0, tiled=True
    )


def swap(value):
    return lax.ppermute(value, "core", [(0, 1), (1, 0)])


def pieces(value):
    high = value.astype(bf16)
    rest = value - high.astype(f32)
    middle = rest.astype(bf16)
    low = (rest - middle.astype(f32)).astype(bf16)
    return [high, middle, low]


def lanes(wide):
    return wide.reshape(wide.shape[0], -1, BLOCK).transpose(1, 0, 2)


def shards(
    dosage, centers, scales, phenotype, fold_ids, strong_blocks, warm_start, penalty, step_size
):
    rows, local_width = dosage.shape
    local_blocks = local_width // BLOCK
    core = lax.axis_index("core")
    place = lax.axis_index("x")
    slot = lax.axis_index(PLANE)

    relative = strong_blocks - place * local_blocks
    owned = (relative >= 0) & (relative < local_blocks)
    own_mask = owned.astype(f32)
    mine = pick_blocks(dosage, jnp.clip(relative, 0, local_blocks - 1).astype(jnp.int32))
    other = swap(mine)

    center_rows = centers.reshape(-1, BLOCK)
    scale_rows = scales.reshape(-1, BLOCK)
    strong_centers = center_rows[strong_blocks]
    strong_scales = scale_rows[strong_blocks]
    flat_centers = strong_centers.reshape(1, NS)
    samples = jnp.stack([fold_ids.astype(f32), phenotype])
    samples_other = swap(samples)

    fit_folds = (jnp.arange(FITS, dtype=jnp.int32) % FOLDS).astype(f32)
    weights = (samples[:1] != fit_folds[:, None]).astype(f32)
    warm = warm_start.T
    coef_mask = jnp.repeat(own_mask, BLOCK)[None, :]
    flat_scales = strong_scales.reshape(1, NS)
    scaled = ((flat_scales * warm) * coef_mask).astype(bf16)
    shift = jnp.sum(warm * (flat_centers * flat_scales * coef_mask), axis=1, keepdims=True)
    dims = (((1,), (1,)), ((), ()))
    fit_part = lax.dot_general(scaled, mine, dims, preferred_element_type=f32) - shift
    fitted = jnp.sum(spread(fit_part.astype(bf16), "x", 4).astype(f32), axis=0)
    residual = (weights * (samples[1:] - fitted)).astype(bf16)
    column_sums = jnp.sum(residual.astype(f32), axis=1, keepdims=True)

    local_centers = lax.dynamic_slice_in_dim(centers, place * local_width, local_width, 0)
    local_scales = lax.dynamic_slice_in_dim(
        scale_rows, place * local_blocks, local_blocks, 0
    )
    cross = jnp.dot(residual, dosage, preferred_element_type=f32) - (
        local_centers[None, :] * column_sums
    )
    cross_strong = jnp.dot(residual, mine, preferred_element_type=f32) - (
        flat_centers * column_sums
    )
    both = jnp.concatenate([cross, cross_strong], axis=1)
    keep = lax.dynamic_slice_in_dim(both, core * HALF, HALF, 0)
    give = lax.dynamic_slice_in_dim(both, (1 - core) * HALF, HALF, 0)
    tally = jnp.sum(weights[:FOLDS], axis=1)
    tally_row = jnp.zeros((1, BLOCK), f32).at[0, :FOLDS].set(tally)
    summed = (keep + swap(give.astype(bf16)).astype(f32)).astype(bf16)
    tiles = lanes(summed)
    padded = jnp.concatenate(
        [tiles[:local_blocks], jnp.zeros((PARTS * MBLK - local_blocks, HALF, BLOCK), bf16)], axis=0
    ).reshape(PARTS, MBLK * HALF, BLOCK)
    tally_other = jnp.sum(
        (samples_other[:1] != fit_folds[:FOLDS, None]).astype(f32), axis=1
    )
    tally_rows = jnp.zeros((8, BLOCK), f32)
    tally_rows = tally_rows.at[0, :FOLDS].set(tally).at[1, :FOLDS].set(tally_other)
    message = jnp.concatenate(
        [
            padded,
            tiles[local_blocks:],
            jnp.broadcast_to(tally_rows.astype(bf16)[None], (PARTS, 8, BLOCK)),
        ],
        axis=1,
    )
    first = jnp.sum(lax.all_to_all(message, PLANE, 0, 0, tiled=True).astype(f32), axis=0)
    edge = MBLK * HALF
    totals = first[edge + HALF] + first[edge + HALF + 1]
    counts = jnp.tile(totals[:FOLDS], HALF // FOLDS)[:, None]

    fit_penalty = jnp.repeat(penalty, FOLDS)
    half_penalty = lax.dynamic_slice_in_dim(fit_penalty, core * HALF, HALF, 0)[:, None]
    step = lax.dynamic_slice_in_dim(step_size, core * HALF, HALF, 0)[:, None]
    threshold = step * half_penalty

    margin_scales = jnp.concatenate(
        [local_scales, jnp.zeros((PARTS * MBLK - local_blocks, BLOCK), f32)], axis=0
    )
    margin_scales = lax.dynamic_slice_in_dim(margin_scales, slot * MBLK, MBLK, 0)
    kkt = margin_scales[:, None, :] * first[:edge].reshape(MBLK, HALF, BLOCK) / counts[None]
    peak = jnp.max(jnp.abs(kkt) / half_penalty[None], axis=1)

    slot_scale = lax.dynamic_slice_in_dim(strong_scales, slot, 1, 0)
    slot_center = lax.dynamic_slice_in_dim(strong_centers, slot, 1, 0)
    slot_mask = lax.dynamic_slice_in_dim(own_mask, slot, 1, 0)[:, None]
    point = lax.dynamic_slice(warm, (core * HALF, slot * BLOCK), (HALF, BLOCK))
    previous = point
    gradient = first[edge : edge + HALF]
    near = jnp.concatenate([samples, samples_other], axis=1)
    half_weights = (near[:1] != fit_folds[:HALF, None]).astype(f32)
    momentum = 1.0
    margin = None
    for sweep in range(ITERS):
        if sweep > 0:
            coef = (slot_scale * point * slot_mask).astype(bf16)
            shift = jnp.sum(slot_center * slot_scale * slot_mask * point, axis=1)
            shift_row = jnp.concatenate(pieces(shift) + [jnp.zeros((BLOCK - 3 * HALF,), bf16)])
            parts = [coef, shift_row[None]]
            if sweep == 1:
                parts += pieces(peak)
            used = sum(part.shape[0] for part in parts)
            parts.append(jnp.zeros((-used % 8, BLOCK), bf16))
            got = spread(jnp.concatenate(parts, axis=0), PLANE, PARTS)
            if sweep == 1:
                peaks = got[:, HALF + 1 : HALF + 1 + 3 * MBLK].astype(f32)
                peaks = jnp.sum(peaks.reshape(PARTS, 3, MBLK, BLOCK), axis=1)
                peaks = peaks.reshape(PARTS * MBLK * BLOCK)[:local_width]
                margin = jnp.maximum(peaks, swap(peaks))
            scaled = got[:, :HALF].transpose(1, 0, 2).reshape(HALF, NS)
            shift = jnp.sum(got[:, HALF].astype(f32), axis=0)
            shift = jnp.sum(shift[: 3 * HALF].reshape(3, HALF), axis=0)[:, None]
            fit_part = jnp.concatenate(
                [
                    lax.dot_general(scaled, mine, dims, preferred_element_type=f32),
                    lax.dot_general(scaled, other, dims, preferred_element_type=f32),
                ],
                axis=1,
            )
            fit_part = (fit_part - shift).astype(bf16)
            fitted = jnp.sum(spread(fit_part, "x", 4).astype(f32), axis=0)
            residual = (half_weights * (near[1:] - fitted)).astype(bf16)
            column_sums = jnp.sum(residual.astype(f32), axis=1, keepdims=True)
            cross = jnp.dot(residual[:, :rows], mine, preferred_element_type=f32) + jnp.dot(
                residual[:, rows:], other, preferred_element_type=f32
            )
            cross = (cross - flat_centers * column_sums).astype(bf16)
            gradient = jnp.sum(
                lax.all_to_all(lanes(cross), PLANE, 0, 0, tiled=True).astype(f32), axis=0
            )
        moved = point + step * (slot_scale * gradient / counts)
        current = moved - jnp.clip(moved, -threshold, threshold)
        following = (1.0 + math.sqrt(1.0 + 4.0 * momentum * momentum)) / 2.0
        point = current + (momentum - 1.0) / following * (current - previous)
        previous = current
        momentum = following

    gathered = spread(previous * slot_mask, ("core", "x"), 8)
    whole = jnp.sum(gathered.reshape(2, 4, HALF, BLOCK), axis=1).reshape(FITS, BLOCK)
    everyone = spread(whole, PLANE, PARTS)
    share = SLOTS // 4
    out = lax.dynamic_slice_in_dim(everyone, place * share, share, 0)
    coefficients = out.transpose(0, 2, 1).reshape(share * BLOCK, FITS)
    return (margin, coefficients)


def solution(mesh):
    cube = Mesh(mesh.devices.reshape(8, 4, 2, 4), ("z", "y", "core", "x"))
    samp = ("z", "y", "core")
    return jax.shard_map(
        shards,
        mesh=cube,
        in_specs=(P(samp, "x"), P(), P(), P(samp), P(samp), P(), P(), P(), P()),
        out_specs=(P("x"), P("x", None)),
        check_vma=False,
    )
```

time: 1090 us -> 192 us (0.18)
  waiting for transfers between devices: 810 us -> 59.9 us
  blocking collectives: 171 us -> 48.6 us
  local copies, waits for them, and re-layouts: 68.7 us -> 9.92 us
  starting transfers between devices: 0.16 us -> 38.3 us
  between operations: 14 us -> 1.09 us
    psum x4 -> x0, waiting for transfers between devices: 810 us -> none  [the longest x3 637 us: shards(): gradient_total = lax.psum(gradient_cross, ('samp', 'var'))]
    psum x4 -> x0, blocking collectives: 171 us -> none  [the longest x1 131 us: shards(): counts = lax.psum(jnp.sum(weights, axis=0), 'samp')]
    all_to_all x0 -> x6, waiting for transfers between devices: none -> 57.6 us  [the longest x4 32.9 us: spread(): lax.all_to_all(jnp.broadcast_to(payload[None], (count,) + payload.shape),...]
    gather x4 -> x2, local copies, waits for them, and re-layouts: 52.4 us -> 2.06 us  [the longest x1 1.49 us: shards(): strong_centers = center_rows[strong_blocks]]
    all_to_all x0 -> x4, blocking collectives: none -> 48.6 us  [the longest x3 35.9 us: spread(): lax.all_to_all(jnp.broadcast_to(payload[None], (count,) + payload.shape),...]
    all_to_all x0 -> x6, starting transfers between devices: none -> 34.8 us  [the longest x4 18.7 us: spread(): lax.all_to_all(jnp.broadcast_to(payload[None], (count,) + payload.shape),...]
  transfers between devices with their start and end apart: 4 -> 10, of which waited for: 4 -> 8; matrix products, arithmetic and copies ran while one was open for 1% -> 3% of each run, Pallas kernels for 0% -> 0%
where the time goes in v1:
time: 192 us; the launch traced here: 191 us
  waiting for transfers between devices  59.9 us (31%)
  blocking collectives  48.6 us (25%)
  starting transfers between devices  38.3 us (20%)
  matrix products  17 us (9%)
  other arithmetic  11.9 us (6%)
  local copies, waits for them, and re-layouts  9.92 us (5%)
  Pallas kernels  4.43 us (2%)
    all_to_all x3, blocking collectives, spread(): lax.all_to_all(jnp.broadcast_to(payload[None], (count,) + payload.shape),...  35.9 us
    all_to_all x4, waiting for transfers between devices, spread(): lax.all_to_all(jnp.broadcast_to(payload[None], (count,) + payload.shape),...  32.9 us
    all_to_all x4, starting transfers between devices, spread(): lax.all_to_all(jnp.broadcast_to(payload[None], (count,) + payload.shape),...  18.7 us
    all_to_all x1, waiting for transfers between devices, shards(): lax.all_to_all(message, PLANE, 0, 0, tiled=True).astype(f32)  15.4 us
    all_to_all x1, blocking collectives, shards(): lax.all_to_all(lanes(cross), PLANE, 0, 0, tiled=True).astype(f32)  12.7 us
    all_to_all x1, starting transfers between devices, shards(): lax.all_to_all(message, PLANE, 0, 0, tiled=True).astype(f32)  11.2 us
    all_to_all x1, waiting for transfers between devices, shards(): lax.all_to_all(lanes(cross), PLANE, 0, 0, tiled=True).astype(f32)  9.26 us
    all_to_all x1, starting transfers between devices, shards(): lax.all_to_all(lanes(cross), PLANE, 0, 0, tiled=True).astype(f32)  4.9 us
  transfers between devices with their start and end apart: 10, of which 8 were waited for; matrix products, arithmetic and copies ran while one was open for 3% of the time, Pallas kernels for 0%

profile of v1, /device:TPU:1, one launch (start us, length us, event | category | flops | bytes accessed | tf_op | source)
XLA Modules:
  0.0 191.1 jit_solution(17493789208489807180)
XLA Ops:
  0.7 1.2 subtract_clamp_fusion
  3.1 1.5 gather_fusion.1
  4.7 1.2 multiply_reduce_fusion
  5.9 4.4 %pick_blocks.1 = bf16[256,4096]{1,0:T(8,128)(2,1)} custom-call(s32[32]{0:T(128)} %get-tuple-element.53.index_ref, bf16[256,10240]{1,0:T(8,128)(2,1)} %source_ref.1), custom_call_target="tpu_custom_call" | custom-call | tf_op jit(solution)/shard_map/pick_blocks/pallas_call | solution.py:44
  10.4 2.5 %fusion.6 = bf16[32,256]{1,0:T(8,128)(2,1)S(1)} fusion(bf16[256,4096]{1,0:T(8,128)(2,1)} %pick_blocks.1, f32[4096,32]{0,1:T(8,128)S(1)} %copy-done.3, f32[4096]{0:T(1024)S(1)} %broadcast_bitcast_fusion, f32[4096]{0:T(1024)S(1)} %bitcast.130, f32[32]{0:T(128)S(1)} %multiply_reduce_fusion), kind=kOutput, calls=%fused_computation.18 | convolution fusion | flops 67518464 | bytes 2670720 | tf_op jit(solution)/shard_map/dot_general | solution.py:111
  13.5 6.2 %all-to-all-start = ((bf16[4,32,256]{2,1,0:T(8,128)(2,1)}), bf16[4,32,256]{2,1,0:T(8,128)(2,1)S(1)}, u32[]{:S(2)}, u32[]{:S(2)}) async-start(bf16[4,32,256]{2,1,0:T(8,128)(2,1)} %broadcast_in_dim.34), calls=%async_computation | async-start | bytes 131072 | tf_op jit(solution)/shard_map/all_to_all | solution.py:59
  20.6 3.7 %all-to-all-done = bf16[4,32,256]{2,1,0:T(8,128)(2,1)S(1)} async-done(((bf16[4,32,256]{2,1,0:T(8,128)(2,1)}), bf16[4,32,256]{2,1,0:T(8,128)(2,1)S(1)}, u32[]{:S(2)}, u32[]{:S(2)}) %all-to-all-start) | async-done | bytes 65568 | tf_op jit(solution)/shard_map/all_to_all | solution.py:59
  24.9 3.5 %convolution_subtract_fusion = f32[32,10240]{1,0:T(8,128)S(1)} fusion(bf16[32,256]{1,0:T(8,128)(2,1)S(1)} %get-tuple-element.39, bf16[256,10240]{1,0:T(8,128)(2,1)} %source_ref.1, f32[32]{0:T(128)S(1)} %get-tuple-element.38, f32[10240]{0:T(1024)S(1)} %dynamic_slice.39), kind=kOutput, calls=%fused_computation.2 | convolution fusion | flops 168427520 | bytes 6611072 | tf_op jit(solution)/shard_map/dot_general | solution.py:120
  28.5 1.1 copy-done.2
  30.3 2.1 %collective-permute-start = (bf16[16,14336]{1,0:T(8,128)(2,1)}, bf16[16,14336]{1,0:T(8,128)(2,1)}, u32[]{:S(2)}, u32[]{:S(2)}) collective-permute-start(bf16[16,14336]{1,0:T(8,128)(2,1)} %fusion.8), channel_id=1, source_target_pairs={{0,4},{4,0},{1,5},{5,1},{2,6},{6,2},{3,7},{7,3},{8,12},{12,8},{9,1... | collective-permute-start | bytes 1376264 | tf_op jit(solution)/shard_map/ppermute | solution.py:65
  32.7 1.5 collective-permute-done.1
  34.6 1.3 bitcast_bitcast_fusion
  36.2 0.9 pad_maximum_fusion
  37.0 11.2 %all-to-all-start.1 = ((bf16[32,72,128]{2,1,0:T(8,128)(2,1)}), bf16[32,72,128]{2,1,0:T(8,128)(2,1)S(1)}, u32[]{:S(2)}, u32[]{:S(2)}) async-start(bf16[32,72,128]{2,1,0:T(8,128)(2,1)} %pad_maximum_fusion), calls=%async_computation.1 | async-start | bytes 1179648 | tf_op jit(solution)/shard_map/all_to_all | solution.py:149
  50.5 15.4 %all-to-all-done.1 = bf16[32,72,128]{2,1,0:T(8,128)(2,1)S(1)} async-done(((bf16[32,72,128]{2,1,0:T(8,128)(2,1)}), bf16[32,72,128]{2,1,0:T(8,128)(2,1)S(1)}, u32[]{:S(2)}, u32[]{:S(2)}) %all-to-all-start.1) | async-done | bytes 589856 | tf_op jit(solution)/shard_map/all_to_all | solution.py:149
  68.1 5.3 %all-to-all-start.2 = ((bf16[32,32,128]{2,1,0:T(8,128)(2,1)}), bf16[32,32,128]{2,1,0:T(8,128)(2,1)S(1)}, u32[]{:S(2)}, u32[]{:S(2)}) async-start(bf16[32,32,128]{2,1,0:T(8,128)(2,1)} %broadcast_in_dim.39), calls=%async_computation.2 | async-start | bytes 524288 | tf_op jit(solution)/shard_map/all_to_all | solution.py:59
  73.4 10.4 %all-to-all-done.2 = bf16[32,32,128]{2,1,0:T(8,128)(2,1)S(1)} async-done(((bf16[32,32,128]{2,1,0:T(8,128)(2,1)}), bf16[32,32,128]{2,1,0:T(8,128)(2,1)S(1)}, u32[]{:S(2)}, u32[]{:S(2)}) %all-to-all-start.2) | async-done | bytes 262176 | tf_op jit(solution)/shard_map/all_to_all | solution.py:59
  84.6 2.2 %fusion.19 = f32[16,256]{1,0:T(8,128)S(1)} fusion(bf16[256,4096]{1,0:T(8,128)(2,1)} %collective-permute-done.3, bf16[32,32,128]{2,1,0:T(8,128)(2,1)S(1)} %all-to-all-done.2), kind=kOutput, calls=%fused_computation.40 | convolution fusion | flops 33554432 | bytes 2244608 | tf_op jit(solution)/shard_map/dot_general | solution.py:198
  87.6 3.3 %all-to-all-start.3 = ((bf16[4,16,512]{2,1,0:T(8,128)(2,1)}), bf16[4,16,512]{2,1,0:T(8,128)(2,1)S(1)}, u32[]{:S(2)}, u32[]{:S(2)}) async-start(bf16[4,16,512]{2,1,0:T(8,128)(2,1)} %broadcast_in_dim.40), calls=%async_computation.3 | async-start | bytes 131072 | tf_op jit(solution)/shard_map/all_to_all | solution.py:59
  90.9 4.4 %all-to-all-done.3 = bf16[4,16,512]{2,1,0:T(8,128)(2,1)S(1)} async-done(((bf16[4,16,512]{2,1,0:T(8,128)(2,1)}), bf16[4,16,512]{2,1,0:T(8,128)(2,1)S(1)}, u32[]{:S(2)}, u32[]{:S(2)}) %all-to-all-start.3) | async-done | bytes 65568 | tf_op jit(solution)/shard_map/all_to_all | solution.py:59
  95.9 2.0 %fusion.5 = bf16[2,32,8,128]{3,2,1,0:T(8,128)(2,1)S(1)} fusion(f32[16,4096]{1,0:T(8,128)S(1)} %fusion.38, bf16[256,4096]{1,0:T(8,128)(2,1)} %collective-permute-done.3, f32[16]{0:T(128)S(1)} %get-tuple-element.30, f32[4096]{0:T(1024)S(1)} %bitcast.126, bf16[16,512]{1,0:T(8,128)(2,1)S(1)} %get-tuple-element.31), kind=kOutput, calls=%fused_computation.16 | convolution fusion | flops 33816576 | bytes 2515456 | tf_op jit(solution)/shard_map/dot_general | solution.py:206
  98.6 4.9 %all-to-all-start.4 = ((bf16[32,16,128]{2,1,0:T(8,128)(2,1)}), bf16[32,16,128]{2,1,0:T(8,128)(2,1)S(1)}, u32[]{:S(2)}, u32[]{:S(2)}) async-start(bf16[32,16,128]{2,1,0:T(8,128)(2,1)} %bitcast.116), calls=%async_computation.4 | async-start | bytes 262144 | tf_op jit(solution)/shard_map/all_to_all | solution.py:211
  103.6 9.3 %all-to-all-done.4 = bf16[32,16,128]{2,1,0:T(8,128)(2,1)S(1)} async-done(((bf16[32,16,128]{2,1,0:T(8,128)(2,1)}), bf16[32,16,128]{2,1,0:T(8,128)(2,1)S(1)}, u32[]{:S(2)}, u32[]{:S(2)}) %all-to-all-start.4) | async-done | bytes 131104 | tf_op jit(solution)/shard_map/all_to_all | solution.py:211
  113.9 13.1 %all_to_all.50 = bf16[32,24,128]{2,1,0:T(8,128)(2,1)S(1)} all-to-all(bf16[32,24,128]{2,1,0:T(8,128)(2,1)S(1)} %broadcast_in_dim.43), channel_id=1, replica_groups=mesh['z'=8,'y'=4,'core'=2,'x'=4] {'z','y'}, dimensions={0} | all-to-all | bytes 393216 | tf_op jit(solution)/shard_map/all_to_all | solution.py:59
  127.8 2.2 %fusion.15 = f32[16,256]{1,0:T(8,128)S(1)} fusion(bf16[256,4096]{1,0:T(8,128)(2,1)} %collective-permute-done.3, bf16[32,24,128]{2,1,0:T(8,128)(2,1)S(1)} %all_to_all.50), kind=kOutput, calls=%fused_computation.36 | convolution fusion | flops 33554432 | bytes 2244608 | tf_op jit(solution)/shard_map/dot_general | solution.py:198
  130.2 6.8 %all_to_all.51 = bf16[4,16,512]{2,1,0:T(8,128)(2,1)S(1)} all-to-all(bf16[4,16,512]{2,1,0:T(8,128)(2,1)S(1)} %broadcast_in_dim.44), channel_id=1, replica_groups=mesh['z'=8,'y'=4,'core'=2,'x'=4] {'x'}, dimensions={0} | all-to-all | bytes 131072 | tf_op jit(solution)/shard_map/all_to_all | solution.py:59
  137.6 2.0 %fusion.4 = bf16[2,32,8,128]{3,2,1,0:T(8,128)(2,1)S(1)} fusion(f32[16,4096]{1,0:T(8,128)S(1)} %fusion.35, bf16[256,4096]{1,0:T(8,128)(2,1)} %collective-permute-done.3, f32[16]{0:T(128)S(1)} %get-tuple-element.26, f32[4096]{0:T(1024)S(1)} %bitcast.127, bf16[16,512]{1,0:T(8,128)(2,1)S(1)} %get-tuple-element.27), kind=kOutput, calls=%fused_computation.15 | convolution fusion | flops 33816576 | bytes 2515456 | tf_op jit(solution)/shard_map/dot_general | solution.py:206
  139.6 12.7 %all_to_all.52 = bf16[32,16,128]{2,1,0:T(8,128)(2,1)S(1)} all-to-all(bf16[32,16,128]{2,1,0:T(8,128)(2,1)S(1)} %bitcast.124), channel_id=1, replica_groups=mesh['z'=8,'y'=4,'core'=2,'x'=4] {'z','y'}, dimensions={0} | all-to-all | bytes 262144 | tf_op jit(solution)/shard_map/all_to_all | solution.py:211
  153.1 16.0 %all_to_all.53 = f32[8,16,128]{2,1,0:T(8,128)S(1)} all-to-all(f32[8,16,128]{2,1,0:T(8,128)S(1)} %broadcast_in_dim.45), channel_id=1, replica_groups=mesh['z'=8,'y'=4,'core'=2,'x'=4] {'core','x'}, dimensions={0} | all-to-all | bytes 131072 | tf_op jit(solution)/shard_map/all_to_all | solution.py:59
  169.9 3.9 %all-to-all-start.9 = ((f32[32,32,128]{2,1,0:T(8,128)}), f32[32,32,128]{2,1,0:T(8,128)S(1)}, u32[]{:S(2)}, u32[]{:S(2)}) async-start(f32[32,32,128]{2,1,0:T(8,128)} %broadcast_in_dim.47), calls=%async_computation.9 | async-start | bytes 1048576 | tf_op jit(solution)/shard_map/all_to_all | solution.py:59
  174.5 0.9 collective-permute-done.2
  176.0 14.5 %all-to-all-done.9 = f32[32,32,128]{2,1,0:T(8,128)S(1)} async-done(((f32[32,32,128]{2,1,0:T(8,128)}), f32[32,32,128]{2,1,0:T(8,128)S(1)}, u32[]{:S(2)}, u32[]{:S(2)}) %all-to-all-start.9) | async-done | bytes 524320 | tf_op jit(solution)/shard_map/all_to_all | solution.py:59
  (112 shorter events, 18.6 us)
Async XLA Ops:
  0.6 1.9 copy-start
  5.9 4.5 %copy-start.3 = (f32[4096,32]{0,1:T(8,128)S(1)}, f32[4096,32]{0,1:T(8,128)}, u32[]{:S(2)}) copy-start(f32[4096,32]{0,1:T(8,128)} %param.19) | copy-start | bytes 1572868
  10.4 9.4 %copy-start.5 = (s32[256]{0:T(256)S(1)}, s32[256]{0:T(256)}, u32[]{:S(2)}) copy-start(s32[256]{0:T(256)} %param.17) | copy-start | bytes 3076
  10.4 13.9 %copy-start.4 = (f32[256]{0:T(256)S(1)}, f32[256]{0:T(256)}, u32[]{:S(2)}) copy-start(f32[256]{0:T(256)} %param.16) | copy-start | bytes 3076
  10.4 14.1 %copy-start.1 = (bf16[256,4096]{1,0:T(8,128)(2,1)S(1)}, bf16[256,4096]{1,0:T(8,128)(2,1)}, u32[]{:S(2)}) copy-start(bf16[256,4096]{1,0:T(8,128)(2,1)} %pick_blocks.1) | copy-start | bytes 6291460
  13.5 10.7 %all-to-all-start = ((bf16[4,32,256]{2,1,0:T(8,128)(2,1)}), bf16[4,32,256]{2,1,0:T(8,128)(2,1)S(1)}, u32[]{:S(2)}, u32[]{:S(2)}) async-start(bf16[4,32,256]{2,1,0:T(8,128)(2,1)} %broadcast_in_dim.34), calls=%async_computation | async-start | bytes 131072 | tf_op jit(solution)/shard_map/all_to_all | solution.py:59
  28.5 1.1 copy-start.2
  30.3 5.6 %copy-start.8 = (pred[96]{0:T(512)(128)(4,1)S(1)}, pred[96]{0:T(512)(128)(4,1)}, u32[]{:S(2)}) copy-start(pred[96]{0:T(512)(128)(4,1)} %constant.122.clone.1) | copy-start | bytes 292
  30.3 4.2 %collective-permute-start = (bf16[16,14336]{1,0:T(8,128)(2,1)}, bf16[16,14336]{1,0:T(8,128)(2,1)}, u32[]{:S(2)}, u32[]{:S(2)}) collective-permute-start(bf16[16,14336]{1,0:T(8,128)(2,1)} %fusion.8), channel_id=1, source_target_pairs={{0,4},{4,0},{1,5},{5,1},{2,6},{6,2},{3,7},{7,3},{8,12},{12,8},{9,1... | collective-permute-start | bytes 1376264 | tf_op jit(solution)/shard_map/ppermute | solution.py:65
  32.5 1.8 collective-permute-start.1
  35.9 13.1 %copy-start.6 = (f32[8]{0:T(128)S(1)}, f32[8]{0:T(128)}, u32[]{:S(2)}) copy-start(f32[8]{0:T(128)} %param.20) | copy-start | bytes 100
  35.9 14.5 %copy-start.7 = (f32[32]{0:T(128)S(1)}, f32[32]{0:T(128)}, u32[]{:S(2)}) copy-start(f32[32]{0:T(128)} %param.21) | copy-start | bytes 388
  37.0 28.9 %all-to-all-start.1 = ((bf16[32,72,128]{2,1,0:T(8,128)(2,1)}), bf16[32,72,128]{2,1,0:T(8,128)(2,1)S(1)}, u32[]{:S(2)}, u32[]{:S(2)}) async-start(bf16[32,72,128]{2,1,0:T(8,128)(2,1)} %pad_maximum_fusion), calls=%async_computation.1 | async-start | bytes 1179648 | tf_op jit(solution)/shard_map/all_to_all | solution.py:149
  48.2 36.4 %collective-permute-start.3 = (bf16[256,4096]{1,0:T(8,128)(2,1)S(1)}, bf16[256,4096]{1,0:T(8,128)(2,1)}, u32[]{:S(2)}, u32[]{:S(2)}) collective-permute-start(bf16[256,4096]{1,0:T(8,128)(2,1)S(1)} %copy-done.1), channel_id=1, source_target_pairs={{0,4},{4,0},{1,5},{5,1},{2,6},{6,2},{3,7},{7,3},{8,12},{12,8},{9,1... | collective-permute-start | bytes 6291464 | tf_op jit(solution)/shard_map/ppermute | solution.py:65
  68.1 15.7 %all-to-all-start.2 = ((bf16[32,32,128]{2,1,0:T(8,128)(2,1)}), bf16[32,32,128]{2,1,0:T(8,128)(2,1)S(1)}, u32[]{:S(2)}, u32[]{:S(2)}) async-start(bf16[32,32,128]{2,1,0:T(8,128)(2,1)} %broadcast_in_dim.39), calls=%async_computation.2 | async-start | bytes 524288 | tf_op jit(solution)/shard_map/all_to_all | solution.py:59
  87.6 7.7 %all-to-all-start.3 = ((bf16[4,16,512]{2,1,0:T(8,128)(2,1)}), bf16[4,16,512]{2,1,0:T(8,128)(2,1)S(1)}, u32[]{:S(2)}, u32[]{:S(2)}) async-start(bf16[4,16,512]{2,1,0:T(8,128)(2,1)} %broadcast_in_dim.40), calls=%async_computation.3 | async-start | bytes 131072 | tf_op jit(solution)/shard_map/all_to_all | solution.py:59
  98.6 14.2 %all-to-all-start.4 = ((bf16[32,16,128]{2,1,0:T(8,128)(2,1)}), bf16[32,16,128]{2,1,0:T(8,128)(2,1)S(1)}, u32[]{:S(2)}, u32[]{:S(2)}) async-start(bf16[32,16,128]{2,1,0:T(8,128)(2,1)} %bitcast.116), calls=%async_computation.4 | async-start | bytes 262144 | tf_op jit(solution)/shard_map/all_to_all | solution.py:211
  169.9 20.5 %all-to-all-start.9 = ((f32[32,32,128]{2,1,0:T(8,128)}), f32[32,32,128]{2,1,0:T(8,128)S(1)}, u32[]{:S(2)}, u32[]{:S(2)}) async-start(f32[32,32,128]{2,1,0:T(8,128)} %broadcast_in_dim.47), calls=%async_computation.9 | async-start | bytes 1048576 | tf_op jit(solution)/shard_map/all_to_all | solution.py:59
  174.0 1.4 collective-permute-start.2

commit v2 on v1

v2 whole, which is shorter than its diff:
```python
import functools
import math

import jax
import jax.numpy as jnp
from jax import lax
from jax.experimental import pallas as pl
from jax.experimental.pallas import tpu as pltpu
from jax.sharding import Mesh
from jax.sharding import PartitionSpec as P

BLOCK = 128
SLOTS = 32
NS = SLOTS * BLOCK
LAMBDAS = 8
FOLDS = 4
FITS = LAMBDAS * FOLDS
HALF = FITS // 2
OWN = 4
SHARE = NS // 4
ITERS = 3
PLANE = ("z", "y")
PARTS = 32
MBLK = 3

f32 = jnp.float32
bf16 = jnp.bfloat16
exact_mode = lax.Precision.HIGHEST


def pick_kernel(width, index_ref, source_ref, out_ref, sem):
    def start(slot, carry):
        pltpu.make_async_copy(
            source_ref.at[:, pl.ds(pl.multiple_of(index_ref[slot] * BLOCK, BLOCK), BLOCK)],
            out_ref.at[:, pl.ds(pl.multiple_of(slot * BLOCK, BLOCK), BLOCK)],
            sem,
        ).start()
        return carry

    lax.fori_loop(0, SLOTS, start, 0)
    pltpu.make_async_copy(source_ref.at[:, pl.ds(0, NS)], out_ref, sem).wait()


def pick_blocks(dosage, index):
    rows, width = dosage.shape
    return pl.pallas_call(
        functools.partial(pick_kernel, width),
        grid_spec=pltpu.PrefetchScalarGridSpec(
            num_scalar_prefetch=1,
            grid=(1,),
            in_specs=[pl.BlockSpec(memory_space=pl.ANY)],
            out_specs=pl.BlockSpec((rows, NS), lambda i, s: (0, 0)),
            scratch_shapes=[pltpu.SemaphoreType.DMA],
        ),
        out_shape=jax.ShapeDtypeStruct((rows, NS), bf16),
        name="pick_blocks",
    )(index, dosage)


def spread(payload, axis, count):
    return lax.all_to_all(
        jnp.broadcast_to(payload[None], (count,) + payload.shape), axis, 0, 0, tiled=True
    )


def swap(value):
    return lax.ppermute(value, "core", [(0, 1), (1, 0)])


def onward(value):
    return lax.ppermute(value, "x", [(i, (i + 1) % 4) for i in range(4)])


def backward(value):
    return lax.ppermute(value, "x", [(i, (i + 3) % 4) for i in range(4)])


def turned(value, count, axis):
    twice = jnp.concatenate([value, value], axis=axis)
    return lax.dynamic_slice_in_dim(twice, count, value.shape[axis], axis)


def pieces(value):
    high = value.astype(bf16)
    rest = value - high.astype(f32)
    middle = rest.astype(bf16)
    low = (rest - middle.astype(f32)).astype(bf16)
    return [high, middle, low]


def lanes(wide):
    return wide.reshape(wide.shape[0], -1, BLOCK).transpose(1, 0, 2)


def shards(
    dosage, centers, scales, phenotype, fold_ids, strong_blocks, warm_start, penalty, step_size
):
    rows, local_width = dosage.shape
    part = rows // 2
    local_blocks = local_width // BLOCK
    core = lax.axis_index("core")
    place = lax.axis_index("x")
    slot = lax.axis_index(PLANE)

    relative = strong_blocks - place * local_blocks
    owned = (relative >= 0) & (relative < local_blocks)
    own_mask = owned.astype(f32)
    mine = pick_blocks(dosage, jnp.clip(relative, 0, local_blocks - 1).astype(jnp.int32))

    def chunk(ahead):
        return lax.dynamic_slice_in_dim(mine, (place + ahead) % 4 * SHARE, SHARE, 1)

    far = chunk(2)
    from_left = onward(jnp.concatenate([chunk(1), far[:part]], axis=0))
    from_right = backward(jnp.concatenate([chunk(3), far[part:]], axis=0))

    center_rows = centers.reshape(-1, BLOCK)
    scale_rows = scales.reshape(-1, BLOCK)
    strong_centers = center_rows[strong_blocks]
    strong_scales = scale_rows[strong_blocks]
    flat_centers = strong_centers.reshape(1, NS)
    samples = jnp.stack([fold_ids.astype(f32), phenotype])
    samples_other = swap(samples)

    fit_folds = (jnp.arange(FITS, dtype=jnp.int32) % FOLDS).astype(f32)
    weights = (samples[:1] != fit_folds[:, None]).astype(f32)
    warm = warm_start.T
    coef_mask = jnp.repeat(own_mask, BLOCK)[None, :]
    flat_scales = strong_scales.reshape(1, NS)
    scaled = ((flat_scales * warm) * coef_mask).astype(bf16)
    shift = jnp.sum(warm * (flat_centers * flat_scales * coef_mask), axis=1, keepdims=True)
    dims = (((1,), (1,)), ((), ()))
    fit_part = lax.dot_general(scaled, mine, dims, preferred_element_type=f32) - shift
    fitted = jnp.sum(spread(fit_part.astype(bf16), "x", 4).astype(f32), axis=0)
    residual = (weights * (samples[1:] - fitted)).astype(bf16)
    column_sums = jnp.sum(residual.astype(f32), axis=1, keepdims=True)

    local_centers = lax.dynamic_slice_in_dim(centers, place * local_width, local_width, 0)
    local_scales = lax.dynamic_slice_in_dim(scale_rows, place * local_blocks, local_blocks, 0)
    cross = jnp.dot(residual, dosage, preferred_element_type=f32) - (
        local_centers[None, :] * column_sums
    )
    cross_strong = jnp.dot(residual, mine, preferred_element_type=f32) - (
        flat_centers * column_sums
    )
    both = jnp.concatenate([cross, cross_strong], axis=1)
    keep = lax.dynamic_slice_in_dim(both, core * HALF, HALF, 0)
    give = lax.dynamic_slice_in_dim(both, (1 - core) * HALF, HALF, 0)
    summed = (keep + swap(give.astype(bf16)).astype(f32)).astype(bf16)
    tiles = lanes(summed)
    padded = jnp.concatenate(
        [tiles[:local_blocks], jnp.zeros((PARTS * MBLK - local_blocks, HALF, BLOCK), bf16)], axis=0
    ).reshape(PARTS, MBLK * HALF, BLOCK)
    near = jnp.concatenate([samples, samples_other], axis=1)
    half_weights = (near[:1] != fit_folds[:FOLDS, None]).astype(f32)
    tally_rows = jnp.zeros((8, BLOCK), f32)
    tally_rows = tally_rows.at[0, :FOLDS].set(jnp.sum(half_weights[:, :rows], axis=1))
    tally_rows = tally_rows.at[1, :FOLDS].set(jnp.sum(half_weights[:, rows:], axis=1))
    message = jnp.concatenate(
        [
            padded,
            tiles[local_blocks:],
            jnp.broadcast_to(tally_rows.astype(bf16)[None], (PARTS, 8, BLOCK)),
        ],
        axis=1,
    )
    message, from_left, from_right = lax.optimization_barrier((message, from_left, from_right))
    via_left = onward(from_left[rows:])
    via_right = backward(from_right[rows:])
    first = jnp.sum(lax.all_to_all(message, PLANE, 0, 0, tiled=True).astype(f32), axis=0)
    edge = MBLK * HALF
    totals = first[edge + HALF] + first[edge + HALF + 1]
    counts = totals[:FOLDS, None]

    def mine_of(values, start, size):
        return lax.dynamic_slice_in_dim(values, start, size, 0)[:, None]

    fit_penalty = jnp.repeat(penalty, FOLDS)
    half_penalty = mine_of(fit_penalty, core * HALF, HALF)
    step = mine_of(step_size, core * HALF, HALF)
    half_counts = jnp.tile(counts, (HALF // FOLDS, 1))

    margin_scales = jnp.concatenate(
        [local_scales, jnp.zeros((PARTS * MBLK - local_blocks, BLOCK), f32)], axis=0
    )
    margin_scales = lax.dynamic_slice_in_dim(margin_scales, slot * MBLK, MBLK, 0)
    kkt = margin_scales[:, None, :] * first[:edge].reshape(MBLK, HALF, BLOCK) / half_counts[None]
    peak = jnp.max(jnp.abs(kkt) / half_penalty[None], axis=1)

    slot_scale = lax.dynamic_slice_in_dim(strong_scales, slot, 1, 0)
    slot_mask = lax.dynamic_slice_in_dim(own_mask, slot, 1, 0)[:, None]
    point = lax.dynamic_slice(warm, (core * HALF, slot * BLOCK), (HALF, BLOCK))
    moved = point + step * (slot_scale * first[edge : edge + HALF] / half_counts)
    threshold = step * half_penalty
    current = (moved - jnp.clip(moved, -threshold, threshold)) * slot_mask

    current, via_left, via_right = lax.optimization_barrier((current, via_left, via_right))
    owner = jnp.repeat(strong_blocks // local_blocks, BLOCK)
    owner = lax.dynamic_slice_in_dim(owner, place * SHARE, SHARE, 0)[None, :]
    share = jnp.where(owner == (place + 3) % 4, from_left[:rows], chunk(0))
    share = jnp.where(owner == (place + 1) % 4, from_right[:rows], share)
    share = jnp.where(
        owner == (place + 2) % 4, jnp.concatenate([via_left, via_right], axis=0), share
    )
    share_left = onward(share)
    share_right = backward(share)
    share_other = swap(share)
    mixed = lax.all_to_all(current.reshape(4, OWN, BLOCK), "x", 0, 0, tiled=True)
    parts = pieces(jnp.sum(mixed, axis=0)) + pieces(peak)
    used = sum(piece.shape[0] for piece in parts)
    parts.append(jnp.zeros((-used % 8, BLOCK), bf16))
    payload = jnp.concatenate(parts, axis=0)
    payload, share_left, share_right, share_other = lax.optimization_barrier(
        (payload, share_left, share_right, share_other)
    )
    share_far = [onward(share_left[:part]), backward(share_right[part:])]
    left_other, right_other = swap(share_left), swap(share_right)
    got = spread(payload, PLANE, PARTS)
    peaks = got[:, 3 * OWN : 3 * OWN + 3 * MBLK].astype(f32)
    peaks = jnp.sum(peaks.reshape(PARTS, 3, MBLK, BLOCK), axis=1)
    peaks = peaks.reshape(PARTS * MBLK * BLOCK)[:local_width]
    margin = jnp.maximum(peaks, swap(peaks))
    current = jnp.sum(got[:, : 3 * OWN].astype(f32).reshape(PARTS, 3, OWN, BLOCK), axis=1)
    ahead = place * (SLOTS // 4)
    current = turned(current, ahead, 0).transpose(1, 0, 2).reshape(OWN, NS)
    wide_scale = turned(strong_scales, ahead, 0).reshape(1, NS)
    wide_center = turned(strong_centers, ahead, 0).reshape(1, NS)
    far_other = [swap(piece) for piece in share_far]
    strong = jnp.concatenate(
        [
            jnp.concatenate([share, share_right, jnp.concatenate(share_far, axis=0), share_left], axis=1),
            jnp.concatenate(
                [share_other, right_other, jnp.concatenate(far_other, axis=0), left_other], axis=1
            ),
        ],
        axis=0,
    )

    first_fit = core * HALF + place * OWN
    step = mine_of(step_size, first_fit, OWN)
    threshold = step * mine_of(fit_penalty, first_fit, OWN)
    point = current
    previous = current
    momentum = (1.0 + math.sqrt(5.0)) / 2.0
    for sweep in range(1, ITERS):
        scaled = (wide_scale * point).astype(bf16)
        shift = jnp.sum(wide_center * wide_scale * point, axis=1, keepdims=True)
        fitted = lax.dot_general(scaled, strong, dims, preferred_element_type=f32) - shift
        residual = (half_weights * (near[1:] - fitted)).astype(bf16)
        column_sums = jnp.sum(residual.astype(f32), axis=1, keepdims=True)
        cross = jnp.dot(residual, strong, preferred_element_type=f32) - wide_center * column_sums
        cross = jnp.sum(spread(cross.astype(bf16), "y", 4).astype(f32), axis=0)
        cross = jnp.sum(spread(cross.astype(bf16), "z", 8).astype(f32), axis=0)
        moved = point + step * (wide_scale * cross / counts)
        current = moved - jnp.clip(moved, -threshold, threshold)
        following = (1.0 + math.sqrt(1.0 + 4.0 * momentum * momentum)) / 2.0
        point = current + (momentum - 1.0) / following * (current - previous)
        previous = current
        momentum = following

    leaving = previous.reshape(OWN, 4, SHARE).transpose(1, 0, 2)
    leaving = turned(leaving, (4 - place) % 4, 0)
    landed = lax.all_to_all(
        jnp.concatenate([leaving, leaving], axis=0), ("core", "x"), 0, 0, tiled=True
    )
    coefficients = landed.reshape(FITS, SHARE).T
    return (margin, coefficients)


def solution(mesh):
    cube = Mesh(mesh.devices.reshape(8, 4, 2, 4), ("z", "y", "core", "x"))
    samp = ("z", "y", "core")
    return jax.shard_map(
        shards,
        mesh=cube,
        in_specs=(P(samp, "x"), P(), P(), P(samp), P(samp), P(), P(), P(), P()),
        out_specs=(P("x"), P("x", None)),
        check_vma=False,
    )
```

time: 192 us -> 224 us (1.17)
  other arithmetic: 11.9 us -> 53.5 us
  starting transfers between devices: 38.3 us -> 76.4 us
  blocking collectives: 48.6 us -> 16.1 us
  waiting for transfers between devices: 59.9 us -> 43.9 us
  matrix products: 17 us -> 11.1 us
  local copies, waits for them, and re-layouts: 9.92 us -> 14.3 us
    concatenate x1 -> x5, other arithmetic: 0.08 us -> 43 us  [the longest x1 40.4 us: shards(): jnp.concatenate([jnp.concatenate([share, share_right, jnp.concatenate(sha...]
    all_to_all x3 -> x2, blocking collectives: 35.9 us -> 16.1 us  [spread(): lax.all_to_all(jnp.broadcast_to(payload[None], (count,) + payload.shape),...]
    ppermute x4 -> x8, starting transfers between devices: 3.42 us -> 20.3 us  [swap(): return lax.ppermute(value, 'core', [(0, 1), (1, 0)])]
    all_to_all x1 -> x0, blocking collectives: 12.7 us -> none  [shards(): lax.all_to_all(lanes(cross), PLANE, 0, 0, tiled=True).astype(f32)]
    all_to_all x4, waiting for transfers between devices: 32.9 us -> 20.7 us  [spread(): lax.all_to_all(jnp.broadcast_to(payload[None], (count,) + payload.shape),...]
    ppermute x0 -> x8, starting transfers between devices: none -> 11.7 us  [the longest x4 5.86 us: backward(): return lax.ppermute(value, 'x', [(i, (i + 3) % 4) for i in range(4)])]
    all_to_all x1 -> x2, starting transfers between devices: 4.9 us -> 13.6 us  [the longest x1 10.4 us: shards(): lax.all_to_all(jnp.concatenate([leaving, leaving], axis=0), ('core', 'x')...]
    slice x4 -> x9, local copies, waits for them, and re-layouts: 0.05 us -> 5.93 us  [the longest x1 1.68 us: shards(): via_left = onward(from_left[rows:])]
  transfers between devices with their start and end apart: 10 -> 23, of which waited for: 8 -> 11; matrix products, arithmetic and copies ran while one was open for 3% -> 10% of each run, Pallas kernels for 0% -> 0%
where the time goes in v2:
time: 224 us; the launch traced here: 223 us
  starting transfers between devices  76.4 us (34%)
  other arithmetic  53.5 us (24%)
  waiting for transfers between devices  43.9 us (20%)
  blocking collectives  16.1 us (7%)
  local copies, waits for them, and re-layouts  14.3 us (6%)
  matrix products  11.1 us (5%)
  Pallas kernels  6.1 us (3%)
    concatenate x1, other arithmetic, shards(): jnp.concatenate([jnp.concatenate([share, share_right, jnp.concatenate(sha...  40.4 us
    all_to_all x4, waiting for transfers between devices, spread(): lax.all_to_all(jnp.broadcast_to(payload[None], (count,) + payload.shape),...  20.7 us
    ppermute x8, starting transfers between devices, swap(): return lax.ppermute(value, 'core', [(0, 1), (1, 0)])  20.3 us
    all_to_all x4, starting transfers between devices, spread(): lax.all_to_all(jnp.broadcast_to(payload[None], (count,) + payload.shape),...  19.5 us
    all_to_all x2, blocking collectives, spread(): lax.all_to_all(jnp.broadcast_to(payload[None], (count,) + payload.shape),...  16.1 us
    all_to_all x1, starting transfers between devices, shards(): lax.all_to_all(message, PLANE, 0, 0, tiled=True).astype(f32)  11.2 us
    all_to_all x1, waiting for transfers between devices, shards(): lax.all_to_all(message, PLANE, 0, 0, tiled=True).astype(f32)  10.4 us
    all_to_all x1, starting transfers between devices, shards(): lax.all_to_all(jnp.concatenate([leaving, leaving], axis=0), ('core', 'x')...  10.4 us
  transfers between devices with their start and end apart: 23, of which 11 were waited for; matrix products, arithmetic and copies ran while one was open for 10% of the time, Pallas kernels for 0%

profile of v2, /device:TPU:1, one launch (start us, length us, event | category | flops | bytes accessed | tf_op | source)
XLA Modules:
  0.0 222.6 jit_solution(17194554509701121446)
XLA Ops:
  1.9 6.1 %pick_blocks.1 = bf16[256,4096]{1,0:T(8,128)(2,1)} custom-call(s32[32]{0:T(128)} %get-tuple-element.78.index_ref, bf16[256,10240]{1,0:T(8,128)(2,1)} %source_ref.1), custom_call_target="tpu_custom_call" | custom-call | tf_op jit(solution)/shard_map/pick_blocks/pallas_call | solution.py:46
  11.5 1.6 collective-permute-start.2
  18.4 3.3 %all-to-all-start = ((bf16[4,32,256]{2,1,0:T(8,128)(2,1)}), bf16[4,32,256]{2,1,0:T(8,128)(2,1)S(1)}, u32[]{:S(2)}, u32[]{:S(2)}) async-start(bf16[4,32,256]{2,1,0:T(8,128)(2,1)} %broadcast_in_dim.44), calls=%async_computation | async-start | bytes 131072 | tf_op jit(solution)/shard_map/all_to_all | solution.py:61
  21.7 3.5 %collective-permute-start.1 = (f32[2,256]{1,0:T(2,128)S(1)}, f32[2,256]{1,0:T(2,128)S(1)}, u32[]{:S(2)}, u32[]{:S(2)}) collective-permute-start(f32[2,256]{1,0:T(2,128)S(1)} %pad_maximum_fusion.5), channel_id=1, source_target_pairs={{0,4},{4,0},{1,5},{5,1},{2,6},{6,2},{3,7},{7,3},{8,12},{12,8},{9,1... | collective-permute-start | bytes 6152 | tf_op jit(solution)/shard_map/ppermute | solution.py:67
  26.0 7.3 %all-to-all-done = bf16[4,32,256]{2,1,0:T(8,128)(2,1)S(1)} async-done(((bf16[4,32,256]{2,1,0:T(8,128)(2,1)}), bf16[4,32,256]{2,1,0:T(8,128)(2,1)S(1)}, u32[]{:S(2)}, u32[]{:S(2)}) %all-to-all-start) | async-done | bytes 65568 | tf_op jit(solution)/shard_map/all_to_all | solution.py:61
  33.5 3.5 %convolution_subtract_fusion = f32[32,10240]{1,0:T(8,128)S(1)} fusion(bf16[32,256]{1,0:T(8,128)(2,1)S(1)} %get-tuple-element.60, bf16[256,10240]{1,0:T(8,128)(2,1)} %source_ref.1, f32[32]{0:T(128)S(1)} %get-tuple-element.59, f32[10240]{0:T(1024)S(1)} %dynamic_slice.66), kind=kOutput, calls=%fused_computation.2 | convolution fusion | flops 168427520 | bytes 6611072 | tf_op jit(solution)/shard_map/dot_general | solution.py:140
  38.9 1.8 collective-permute-start
  44.9 11.2 %all-to-all-start.1 = ((bf16[32,72,128]{2,1,0:T(8,128)(2,1)}), bf16[32,72,128]{2,1,0:T(8,128)(2,1)S(1)}, u32[]{:S(2)}, u32[]{:S(2)}) async-start(bf16[32,72,128]{2,1,0:T(8,128)(2,1)} %pad_maximum_fusion.2), calls=%async_computation.1 | async-start | bytes 1179648 | tf_op jit(solution)/shard_map/all_to_all | solution.py:170
  57.1 1.7 slice.122
  58.8 1.8 collective-permute-start.4
  60.6 1.7 slice.123
  63.4 10.4 %all-to-all-done.1 = bf16[32,72,128]{2,1,0:T(8,128)(2,1)S(1)} async-done(((bf16[32,72,128]{2,1,0:T(8,128)(2,1)}), bf16[32,72,128]{2,1,0:T(8,128)(2,1)S(1)}, u32[]{:S(2)}, u32[]{:S(2)}) %all-to-all-start.1) | async-done | bytes 589856 | tf_op jit(solution)/shard_map/all_to_all | solution.py:170
  75.4 1.7 maximum_select_fusion
  77.1 1.9 collective-permute-start.6
  80.2 2.6 %collective-permute-start.8 = (bf16[256,1024]{1,0:T(8,128)(2,1)S(1)}, bf16[256,1024]{1,0:T(8,128)(2,1)S(1)}, u32[]{:S(2)}, u32[]{:S(2)}) collective-permute-start(bf16[256,1024]{1,0:T(8,128)(2,1)S(1)} %maximum_select_fusion), channel_id=1, source_target_pairs={{0,4},{4,0},{1,5},{5,1},{2,6},{6,2},{3,7},{7,3},{8,12},{12,8},{9,1... | collective-permute-start | bytes 1572872 | tf_op jit(solution)/shard_map/ppermute | solution.py:67
  82.8 3.2 %all-to-all-start.2 = ((f32[4,4,128]{2,1,0:T(4,128)}), f32[4,4,128]{2,1,0:T(4,128)S(1)}, u32[]{:S(2)}, u32[]{:S(2)}) async-start(f32[4,4,128]{2,1,0:T(4,128)} %bitcast.16), calls=%async_computation.2 | async-start | bytes 16384 | tf_op jit(solution)/shard_map/all_to_all | solution.py:208
  86.2 4.6 %all-to-all-done.2 = f32[4,4,128]{2,1,0:T(4,128)S(1)} async-done(((f32[4,4,128]{2,1,0:T(4,128)}), f32[4,4,128]{2,1,0:T(4,128)S(1)}, u32[]{:S(2)}, u32[]{:S(2)}) %all-to-all-start.2) | async-done | bytes 8224 | tf_op jit(solution)/shard_map/all_to_all | solution.py:208
  91.7 6.5 %all-to-all-start.3 = ((bf16[32,24,128]{2,1,0:T(8,128)(2,1)}), bf16[32,24,128]{2,1,0:T(8,128)(2,1)S(1)}, u32[]{:S(2)}, u32[]{:S(2)}) async-start(bf16[32,24,128]{2,1,0:T(8,128)(2,1)} %broadcast_in_dim.52), calls=%async_computation.3 | async-start | bytes 393216 | tf_op jit(solution)/shard_map/all_to_all | solution.py:61
  100.2 2.1 collective-permute-start.11
  102.3 3.2 %collective-permute-start.12 = (bf16[256,1024]{1,0:T(8,128)(2,1)S(1)}, bf16[256,1024]{1,0:T(8,128)(2,1)S(1)}, u32[]{:S(2)}, u32[]{:S(2)}) collective-permute-start(bf16[256,1024]{1,0:T(8,128)(2,1)S(1)} %collective-permute-done.7), channel_id=1, source_target_pairs={{0,4},{4,0},{1,5},{5,1},{2,6},{6,2},{3,7},{7,3},{8,12},{12,8},{9,1... | collective-permute-start | bytes 1572872 | tf_op jit(solution)/shard_map/ppermute | solution.py:67
  105.6 3.7 %collective-permute-start.13 = (bf16[128,1024]{1,0:T(8,128)(2,1)}, bf16[128,1024]{1,0:T(8,128)(2,1)}, u32[]{:S(2)}, u32[]{:S(2)}) collective-permute-start(bf16[128,1024]{1,0:T(8,128)(2,1)} %collective-permute-done.10), channel_id=1, source_target_pairs={{0,4},{4,0},{1,5},{5,1},{2,6},{6,2},{3,7},{7,3},{8,12},{12,8},{9,1... | collective-permute-start | bytes 786440 | tf_op jit(solution)/shard_map/ppermute | solution.py:67
  111.5 40.4 %maximum_maximum_fusion = bf16[512,4096]{1,0:T(8,128)(2,1)S(1)} fusion(bf16[256,1024]{1,0:T(8,128)(2,1)} %collective-permute-done.15, bf16[128,1024]{1,0:T(8,128)(2,1)} %collective-permute-done.14, bf16[128,1024]{1,0:T(8,128)(2,1)} %collective-permute-done.13, bf16[256,1024]{1,0:T(8,128)(2,1)S(1)} %collective-permute-done.12, ...), kind=kLoop, calls=%fused_computation.8 | loop fusion | flops 41943040 | bytes 8388608 | tf_op jit(solution)/shard_map/concatenate | solution.py:229
  154.0 8.9 %all_to_all.45 = bf16[4,4,4096]{2,1,0:T(4,128)(2,1)S(1)} all-to-all(bf16[4,4,4096]{2,1,0:T(4,128)(2,1)S(1)} %broadcast_in_dim.53), channel_id=1, replica_groups=mesh['z'=8,'y'=4,'core'=2,'x'=4] {'y'}, dimensions={0} | all-to-all | bytes 262144 | tf_op jit(solution)/shard_map/all_to_all | solution.py:61
  163.7 6.4 %all-to-all-start.5 = ((bf16[8,4,4096]{2,1,0:T(4,128)(2,1)}), bf16[8,4,4096]{2,1,0:T(4,128)(2,1)S(1)}, u32[]{:S(2)}, u32[]{:S(2)}) async-start(bf16[8,4,4096]{2,1,0:T(4,128)(2,1)} %broadcast_in_dim.54), calls=%async_computation.5 | async-start | bytes 524288 | tf_op jit(solution)/shard_map/all_to_all | solution.py:61
  170.2 9.1 %all-to-all-done.5 = bf16[8,4,4096]{2,1,0:T(4,128)(2,1)S(1)} async-done(((bf16[8,4,4096]{2,1,0:T(4,128)(2,1)}), bf16[8,4,4096]{2,1,0:T(4,128)(2,1)S(1)}, u32[]{:S(2)}, u32[]{:S(2)}) %all-to-all-start.5) | async-done | bytes 262176 | tf_op jit(solution)/shard_map/all_to_all | solution.py:61
  179.9 3.8 %convert_reduce_fusion.7 = (f32[4]{0:T(128)S(1)}, bf16[4,512]{1,0:T(4,128)(2,1)S(1)}) fusion(f32[4]{0:T(128)S(1)} %multiply_reduce_fusion.1, bf16[512,4096]{1,0:T(8,128)(2,1)} %copy-done.1, f32[4,4096]{1,0:T(4,128)S(1)} %convert_reduce_fusion.2, f32[1,4,32,128]{3,2,1,0:T(8,128)S(1)} %fusion.42, f32[4]{0:T(128)S(1)} %get-tuple-element.48, ...), kind=kOutput, calls=%fused_computation.91 | convolution fusion | flops 16988156 | bytes 4350064 | tf_op jit(solution)/shard_map/dot_general | solution.py:248
  184.4 7.2 %all_to_all.46 = bf16[4,4,4096]{2,1,0:T(4,128)(2,1)S(1)} all-to-all(bf16[4,4,4096]{2,1,0:T(4,128)(2,1)S(1)} %broadcast_in_dim.55), channel_id=1, replica_groups=mesh['z'=8,'y'=4,'core'=2,'x'=4] {'y'}, dimensions={0} | all-to-all | bytes 262144 | tf_op jit(solution)/shard_map/all_to_all | solution.py:61
  192.4 3.4 %all-to-all-start.7 = ((bf16[8,4,4096]{2,1,0:T(4,128)(2,1)}), bf16[8,4,4096]{2,1,0:T(4,128)(2,1)S(1)}, u32[]{:S(2)}, u32[]{:S(2)}) async-start(bf16[8,4,4096]{2,1,0:T(4,128)(2,1)} %broadcast_in_dim.56), calls=%async_computation.7 | async-start | bytes 524288 | tf_op jit(solution)/shard_map/all_to_all | solution.py:61
  196.1 4.8 %collective-permute-start.9 = (f32[10240]{0:T(1024)S(1)}, f32[10240]{0:T(1024)S(1)}, u32[]{:S(2)}, u32[]{:S(2)}) collective-permute-start(f32[10240]{0:T(1024)S(1)} %slice.147), channel_id=1, source_target_pairs={{0,4},{4,0},{1,5},{5,1},{2,6},{6,2},{3,7},{7,3},{8,12},{12,8},{9,1... | collective-permute-start | bytes 122888 | tf_op jit(solution)/shard_map/ppermute | solution.py:67
  200.9 4.2 %all-to-all-done.7 = bf16[8,4,4096]{2,1,0:T(4,128)(2,1)S(1)} async-done(((bf16[8,4,4096]{2,1,0:T(4,128)(2,1)}), bf16[8,4,4096]{2,1,0:T(4,128)(2,1)S(1)}, u32[]{:S(2)}, u32[]{:S(2)}) %all-to-all-start.7) | async-done | bytes 262176 | tf_op jit(solution)/shard_map/all_to_all | solution.py:61
  206.4 10.4 %all-to-all-start.8 = ((f32[8,4,1024]{2,1,0:T(4,128)}), f32[8,4,1024]{2,1,0:T(4,128)S(1)}, u32[]{:S(2)}, u32[]{:S(2)}) async-start(f32[8,4,1024]{2,1,0:T(4,128)} %pad_maximum_fusion.3), calls=%async_computation.8 | async-start | bytes 262144 | tf_op jit(solution)/shard_map/all_to_all | solution.py:263
  217.4 4.6 %all-to-all-done.8 = f32[8,4,1024]{2,1,0:T(4,128)S(1)} async-done(((f32[8,4,1024]{2,1,0:T(4,128)}), f32[8,4,1024]{2,1,0:T(4,128)S(1)}, u32[]{:S(2)}, u32[]{:S(2)}) %all-to-all-start.8) | async-done | bytes 131104 | tf_op jit(solution)/shard_map/all_to_all | solution.py:263
  (139 shorter events, 34.8 us)
Async XLA Ops:
  0.6 14.9 %copy-start = (f32[40960]{0:T(1024)S(1)}, f32[40960]{0:T(1024)}, u32[]{:S(2)}) copy-start(f32[40960]{0:T(1024)} %param.15) | copy-start | bytes 491524
  8.0 7.5 %copy-start.10 = (s32[32]{0:T(128)S(1)}, s32[32]{0:T(128)}, u32[]{:S(2)}) copy-start(s32[32]{0:T(128)} %param.18) | copy-start | bytes 388
  8.0 8.1 %copy-start.6 = (f32[40960]{0:T(1024)S(1)}, f32[40960]{0:T(1024)}, u32[]{:S(2)}) copy-start(f32[40960]{0:T(1024)} %param.14) | copy-start | bytes 491524
  8.0 8.8 %copy-start.5 = (f32[4096,32]{0,1:T(8,128)S(1)}, f32[4096,32]{0,1:T(8,128)}, u32[]{:S(2)}) copy-start(f32[4096,32]{0,1:T(8,128)} %param.19) | copy-start | bytes 1572868
  8.0 9.0 %copy-start.3 = (bf16[256,4096]{1,0:T(8,128)(2,1)S(1)}, bf16[256,4096]{1,0:T(8,128)(2,1)}, u32[]{:S(2)}) copy-start(bf16[256,4096]{1,0:T(8,128)(2,1)} %pick_blocks.1) | copy-start | bytes 6291460
  9.5 12.2 %copy-start.9 = (s32[256]{0:T(256)S(1)}, s32[256]{0:T(256)}, u32[]{:S(2)}) copy-start(s32[256]{0:T(256)} %param.17) | copy-start | bytes 3076
  9.5 12.2 %copy-start.7 = (f32[256]{0:T(256)S(1)}, f32[256]{0:T(256)}, u32[]{:S(2)}) copy-start(f32[256]{0:T(256)} %param.16) | copy-start | bytes 3076
  11.5 33.4 %collective-permute-start.2 = (bf16[384,1024]{1,0:T(8,128)(2,1)}, bf16[384,1024]{1,0:T(8,128)(2,1)}, u32[]{:S(2)}, u32[]{:S(2)}) collective-permute-start(bf16[384,1024]{1,0:T(8,128)(2,1)} %pad_maximum_fusion), channel_id=1, source_target_pairs={{0,1},{1,2},{2,3},{3,0},{4,5},{5,6},{6,7},{7,4},{8,9},{9,10},{10,1... | collective-permute-start | bytes 2359304 | tf_op jit(solution)/shard_map/ppermute | solution.py:71
  14.1 30.9 %collective-permute-start.3 = (bf16[384,1024]{1,0:T(8,128)(2,1)}, bf16[384,1024]{1,0:T(8,128)(2,1)}, u32[]{:S(2)}, u32[]{:S(2)}) collective-permute-start(bf16[384,1024]{1,0:T(8,128)(2,1)} %pad_maximum_fusion.1), channel_id=1, source_target_pairs={{0,3},{1,0},{2,1},{3,2},{4,7},{5,4},{6,5},{7,6},{8,11},{9,8},{10,9... | collective-permute-start | bytes 2359304 | tf_op jit(solution)/shard_map/ppermute | solution.py:75
  18.4 14.9 %all-to-all-start = ((bf16[4,32,256]{2,1,0:T(8,128)(2,1)}), bf16[4,32,256]{2,1,0:T(8,128)(2,1)S(1)}, u32[]{:S(2)}, u32[]{:S(2)}) async-start(bf16[4,32,256]{2,1,0:T(8,128)(2,1)} %broadcast_in_dim.44), calls=%async_computation | async-start | bytes 131072 | tf_op jit(solution)/shard_map/all_to_all | solution.py:61
  21.7 4.3 %collective-permute-start.1 = (f32[2,256]{1,0:T(2,128)S(1)}, f32[2,256]{1,0:T(2,128)S(1)}, u32[]{:S(2)}, u32[]{:S(2)}) collective-permute-start(f32[2,256]{1,0:T(2,128)S(1)} %pad_maximum_fusion.5), channel_id=1, source_target_pairs={{0,4},{4,0},{1,5},{5,1},{2,6},{6,2},{3,7},{7,3},{8,12},{12,8},{9,1... | collective-permute-start | bytes 6152 | tf_op jit(solution)/shard_map/ppermute | solution.py:67
  38.1 18.7 %copy-start.11 = (f32[8]{0:T(128)S(1)}, f32[8]{0:T(128)}, u32[]{:S(2)}) copy-start(f32[8]{0:T(128)} %param.20) | copy-start | bytes 100
  38.1 18.8 %copy-start.8 = (f32[32]{0:T(128)S(1)}, f32[32]{0:T(128)}, u32[]{:S(2)}) copy-start(f32[32]{0:T(128)} %param.21) | copy-start | bytes 388
  38.9 3.6 %collective-permute-start = (bf16[16,14336]{1,0:T(8,128)(2,1)}, bf16[16,14336]{1,0:T(8,128)(2,1)}, u32[]{:S(2)}, u32[]{:S(2)}) collective-permute-start(bf16[16,14336]{1,0:T(8,128)(2,1)} %fusion.10), channel_id=1, source_target_pairs={{0,4},{4,0},{1,5},{5,1},{2,6},{6,2},{3,7},{7,3},{8,12},{12,8},{9,1... | collective-permute-start | bytes 1376264 | tf_op jit(solution)/shard_map/ppermute | solution.py:67
  44.9 28.9 %all-to-all-start.1 = ((bf16[32,72,128]{2,1,0:T(8,128)(2,1)}), bf16[32,72,128]{2,1,0:T(8,128)(2,1)S(1)}, u32[]{:S(2)}, u32[]{:S(2)}) async-start(bf16[32,72,128]{2,1,0:T(8,128)(2,1)} %pad_maximum_fusion.2), calls=%async_computation.1 | async-start | bytes 1179648 | tf_op jit(solution)/shard_map/all_to_all | solution.py:170
  58.8 16.6 %collective-permute-start.4 = (bf16[128,1024]{1,0:T(8,128)(2,1)}, bf16[128,1024]{1,0:T(8,128)(2,1)}, u32[]{:S(2)}, u32[]{:S(2)}) collective-permute-start(bf16[128,1024]{1,0:T(8,128)(2,1)} %slice.122), channel_id=1, source_target_pairs={{0,1},{1,2},{2,3},{3,0},{4,5},{5,6},{6,7},{7,4},{8,9},{9,10},{10,1... | collective-permute-start | bytes 786440 | tf_op jit(solution)/shard_map/ppermute | solution.py:71
  62.3 13.1 %collective-permute-start.5 = (bf16[128,1024]{1,0:T(8,128)(2,1)}, bf16[128,1024]{1,0:T(8,128)(2,1)}, u32[]{:S(2)}, u32[]{:S(2)}) collective-permute-start(bf16[128,1024]{1,0:T(8,128)(2,1)} %slice.123), channel_id=1, source_target_pairs={{0,3},{1,0},{2,1},{3,2},{4,7},{5,4},{6,5},{7,6},{8,11},{9,8},{10,9... | collective-permute-start | bytes 786440 | tf_op jit(solution)/shard_map/ppermute | solution.py:75
  77.1 13.8 %collective-permute-start.6 = (bf16[256,1024]{1,0:T(8,128)(2,1)S(1)}, bf16[256,1024]{1,0:T(8,128)(2,1)S(1)}, u32[]{:S(2)}, u32[]{:S(2)}) collective-permute-start(bf16[256,1024]{1,0:T(8,128)(2,1)S(1)} %maximum_select_fusion), channel_id=1, source_target_pairs={{0,1},{1,2},{2,3},{3,0},{4,5},{5,6},{6,7},{7,4},{8,9},{9,10},{10,1... | collective-permute-start | bytes 1572872 | tf_op jit(solution)/shard_map/ppermute | solution.py:71
  79.0 12.0 %collective-permute-start.7 = (bf16[256,1024]{1,0:T(8,128)(2,1)S(1)}, bf16[256,1024]{1,0:T(8,128)(2,1)S(1)}, u32[]{:S(2)}, u32[]{:S(2)}) collective-permute-start(bf16[256,1024]{1,0:T(8,128)(2,1)S(1)} %maximum_select_fusion), channel_id=1, source_target_pairs={{0,3},{1,0},{2,1},{3,2},{4,7},{5,4},{6,5},{7,6},{8,11},{9,8},{10,9... | collective-permute-start | bytes 1572872 | tf_op jit(solution)/shard_map/ppermute | solution.py:75
  80.2 10.8 %collective-permute-start.8 = (bf16[256,1024]{1,0:T(8,128)(2,1)S(1)}, bf16[256,1024]{1,0:T(8,128)(2,1)S(1)}, u32[]{:S(2)}, u32[]{:S(2)}) collective-permute-start(bf16[256,1024]{1,0:T(8,128)(2,1)S(1)} %maximum_select_fusion), channel_id=1, source_target_pairs={{0,4},{4,0},{1,5},{5,1},{2,6},{6,2},{3,7},{7,3},{8,12},{12,8},{9,1... | collective-permute-start | bytes 1572872 | tf_op jit(solution)/shard_map/ppermute | solution.py:67
  82.8 8.0 %all-to-all-start.2 = ((f32[4,4,128]{2,1,0:T(4,128)}), f32[4,4,128]{2,1,0:T(4,128)S(1)}, u32[]{:S(2)}, u32[]{:S(2)}) async-start(f32[4,4,128]{2,1,0:T(4,128)} %bitcast.16), calls=%async_computation.2 | async-start | bytes 16384 | tf_op jit(solution)/shard_map/all_to_all | solution.py:208
  91.7 18.4 %all-to-all-start.3 = ((bf16[32,24,128]{2,1,0:T(8,128)(2,1)}), bf16[32,24,128]{2,1,0:T(8,128)(2,1)S(1)}, u32[]{:S(2)}, u32[]{:S(2)}) async-start(bf16[32,24,128]{2,1,0:T(8,128)(2,1)} %broadcast_in_dim.52), calls=%async_computation.3 | async-start | bytes 393216 | tf_op jit(solution)/shard_map/all_to_all | solution.py:61
  98.9 6.7 %collective-permute-start.10 = (bf16[128,1024]{1,0:T(8,128)(2,1)}, bf16[128,1024]{1,0:T(8,128)(2,1)}, u32[]{:S(2)}, u32[]{:S(2)}) collective-permute-start(bf16[128,1024]{1,0:T(8,128)(2,1)} %slice.131), channel_id=1, source_target_pairs={{0,1},{1,2},{2,3},{3,0},{4,5},{5,6},{6,7},{7,4},{8,9},{9,10},{10,1... | collective-permute-start | bytes 786440 | tf_op jit(solution)/shard_map/ppermute | solution.py:71
  100.2 9.2 %collective-permute-start.11 = (bf16[128,1024]{1,0:T(8,128)(2,1)}, bf16[128,1024]{1,0:T(8,128)(2,1)}, u32[]{:S(2)}, u32[]{:S(2)}) collective-permute-start(bf16[128,1024]{1,0:T(8,128)(2,1)} %slice.132), channel_id=1, source_target_pairs={{0,3},{1,0},{2,1},{3,2},{4,7},{5,4},{6,5},{7,6},{8,11},{9,8},{10,9... | collective-permute-start | bytes 786440 | tf_op jit(solution)/shard_map/ppermute | solution.py:75
  102.3 9.3 %collective-permute-start.12 = (bf16[256,1024]{1,0:T(8,128)(2,1)S(1)}, bf16[256,1024]{1,0:T(8,128)(2,1)S(1)}, u32[]{:S(2)}, u32[]{:S(2)}) collective-permute-start(bf16[256,1024]{1,0:T(8,128)(2,1)S(1)} %collective-permute-done.7), channel_id=1, source_target_pairs={{0,4},{4,0},{1,5},{5,1},{2,6},{6,2},{3,7},{7,3},{8,12},{12,8},{9,1... | collective-permute-start | bytes 1572872 | tf_op jit(solution)/shard_map/ppermute | solution.py:67
  105.4 6.1 %collective-permute-start.15 = (bf16[256,1024]{1,0:T(8,128)(2,1)S(1)}, bf16[256,1024]{1,0:T(8,128)(2,1)}, u32[]{:S(2)}, u32[]{:S(2)}) collective-permute-start(bf16[256,1024]{1,0:T(8,128)(2,1)S(1)} %collective-permute-done.6), channel_id=1, source_target_pairs={{0,4},{4,0},{1,5},{5,1},{2,6},{6,2},{3,7},{7,3},{8,12},{12,8},{9,1... | collective-permute-start | bytes 1572872 | tf_op jit(solution)/shard_map/ppermute | solution.py:67
  105.6 5.2 %collective-permute-start.13 = (bf16[128,1024]{1,0:T(8,128)(2,1)}, bf16[128,1024]{1,0:T(8,128)(2,1)}, u32[]{:S(2)}, u32[]{:S(2)}) collective-permute-start(bf16[128,1024]{1,0:T(8,128)(2,1)} %collective-permute-done.10), channel_id=1, source_target_pairs={{0,4},{4,0},{1,5},{5,1},{2,6},{6,2},{3,7},{7,3},{8,12},{12,8},{9,1... | collective-permute-start | bytes 786440 | tf_op jit(solution)/shard_map/ppermute | solution.py:67
  109.4 2.2 collective-permute-start.14
  163.7 15.6 %all-to-all-start.5 = ((bf16[8,4,4096]{2,1,0:T(4,128)(2,1)}), bf16[8,4,4096]{2,1,0:T(4,128)(2,1)S(1)}, u32[]{:S(2)}, u32[]{:S(2)}) async-start(bf16[8,4,4096]{2,1,0:T(4,128)(2,1)} %broadcast_in_dim.54), calls=%async_computation.5 | async-start | bytes 524288 | tf_op jit(solution)/shard_map/all_to_all | solution.py:61
  192.4 12.8 %all-to-all-start.7 = ((bf16[8,4,4096]{2,1,0:T(4,128)(2,1)}), bf16[8,4,4096]{2,1,0:T(4,128)(2,1)S(1)}, u32[]{:S(2)}, u32[]{:S(2)}) async-start(bf16[8,4,4096]{2,1,0:T(4,128)(2,1)} %broadcast_in_dim.56), calls=%async_computation.7 | async-start | bytes 524288 | tf_op jit(solution)/shard_map/all_to_all | solution.py:61
  196.1 20.7 %collective-permute-start.9 = (f32[10240]{0:T(1024)S(1)}, f32[10240]{0:T(1024)S(1)}, u32[]{:S(2)}, u32[]{:S(2)}) collective-permute-start(f32[10240]{0:T(1024)S(1)} %slice.147), channel_id=1, source_target_pairs={{0,4},{4,0},{1,5},{5,1},{2,6},{6,2},{3,7},{7,3},{8,12},{12,8},{9,1... | collective-permute-start | bytes 122888 | tf_op jit(solution)/shard_map/ppermute | solution.py:67
  206.4 15.6 %all-to-all-start.8 = ((f32[8,4,1024]{2,1,0:T(4,128)}), f32[8,4,1024]{2,1,0:T(4,128)S(1)}, u32[]{:S(2)}, u32[]{:S(2)}) async-start(f32[8,4,1024]{2,1,0:T(4,128)} %pad_maximum_fusion.3), calls=%async_computation.8 | async-start | bytes 262144 | tf_op jit(solution)/shard_map/all_to_all | solution.py:263
  (4 other events, 14.2 us)

commit v3 on v0

v3 whole, which is shorter than its diff:
```python
import functools
import math

import jax
import jax.numpy as jnp
from jax import lax
from jax.experimental import pallas as pl
from jax.experimental.pallas import tpu as pltpu
from jax.sharding import Mesh
from jax.sharding import PartitionSpec as P

BLOCK = 128
SLOTS = 32
NS = SLOTS * BLOCK
LAMBDAS = 8
FOLDS = 4
FITS = LAMBDAS * FOLDS
HALF = FITS // 2
OWN = 4
SHARE = NS // 4
EACH = SHARE // BLOCK
ITERS = 3
PLANE = ("z", "y")
PARTS = 32
MBLK = 3
ROWS = 256
PART = ROWS // 2
PEAK = MBLK * BLOCK

f32 = jnp.float32
bf16 = jnp.bfloat16
LAST = (((1,), (1,)), ((), ()))
WHOLE = pl.BlockSpec(memory_space=pltpu.VMEM)


def pick_kernel(
    index_ref, source_ref, scaled_ref, shift_ref, own, right, far_a, far_b, left, fit_ref, sem
):
    moves = (
        (own, 0, 0, ROWS),
        (right, 1, 0, ROWS),
        (far_a, 2, 0, PART),
        (far_b, 2, PART, PART),
        (left, 3, 0, ROWS),
    )
    copies = []
    for target, turn, first, height in moves:
        for i in range(EACH):
            block = index_ref[turn * EACH + i]
            copies.append(
                pltpu.make_async_copy(
                    source_ref.at[
                        pl.ds(first, height), pl.ds(pl.multiple_of(block * BLOCK, BLOCK), BLOCK)
                    ],
                    target.at[:, pl.ds(i * BLOCK, BLOCK)],
                    sem.at[len(copies)],
                )
            )
    for copy in copies:
        copy.start()
    for copy in copies:
        copy.wait()
    place = index_ref[SLOTS]

    def dot(ahead, piece):
        start = pl.multiple_of(lax.rem(place + ahead, 4) * SHARE, SHARE)
        return lax.dot_general(
            scaled_ref[:, pl.ds(start, SHARE)], piece[...], LAST, preferred_element_type=f32
        )

    far = jnp.concatenate([dot(2, far_a), dot(2, far_b)], axis=1)
    fit = (dot(0, own) + dot(1, right) + far + dot(3, left) - shift_ref[...]).astype(bf16)
    for x in range(4):
        fit_ref[x] = fit


def pick_blocks(index, dosage, scaled, shift):
    tall = jax.ShapeDtypeStruct((ROWS, SHARE), bf16)
    flat = jax.ShapeDtypeStruct((PART, SHARE), bf16)
    return pl.pallas_call(
        pick_kernel,
        in_specs=[
            pl.BlockSpec(memory_space=pltpu.SMEM),
            pl.BlockSpec(memory_space=pl.ANY),
            WHOLE,
            WHOLE,
        ],
        out_specs=[WHOLE] * 6,
        out_shape=[tall, tall, flat, flat, tall, jax.ShapeDtypeStruct((4, FITS, ROWS), bf16)],
        scratch_shapes=[pltpu.SemaphoreType.DMA((5 * EACH,))],
        name="pick_blocks",
    )(index, dosage, scaled, shift)


def send_gradient(residual, center_ref, pieces, extra_ref, out_ref):
    sums = jnp.sum(residual.astype(f32), axis=1, keepdims=True)

    def dot(piece, first, height):
        return jnp.dot(
            residual[:, first : first + height], piece[...], preferred_element_type=f32
        )

    def half(group, first):
        own, right, far_a, far_b, left = group
        far = dot(far_a, first, PART) + dot(far_b, first + PART, PART)
        return [dot(own, first, ROWS), dot(right, first, ROWS), far, dot(left, first, ROWS)]

    both = zip(half(pieces[:5], 0), half(pieces[5:], ROWS))
    for j, (near, other) in enumerate(both):
        lane = pl.ds(j * SHARE, SHARE)
        piece = (near + other - center_ref[:, lane] * sums).astype(bf16)
        for y in range(4):
            out_ref[y, :, lane] = piece
    if extra_ref is not None:
        for y in range(4):
            out_ref[y, :, NS:] = extra_ref[...]


def first_kernel(residual_ref, center_ref, *refs):
    send_gradient(residual_ref[...], center_ref, refs[:10], None, refs[10])


def first_sweep(residual, center, pieces):
    return pl.pallas_call(
        first_kernel,
        in_specs=[WHOLE] * 12,
        out_specs=WHOLE,
        out_shape=jax.ShapeDtypeStruct((4, OWN, NS), bf16),
        name="first_sweep",
    )(residual, center, *pieces)


def middle_kernel(got_ref, out_ref):
    total = got_ref[0, :, :NS].astype(f32)
    for y in range(1, 4):
        total = total + got_ref[y, :, :NS].astype(f32)
    total = total.astype(bf16)
    for z in range(8):
        out_ref[z, :, :NS] = total
        if got_ref.shape[2] > NS:
            for y in range(4):
                out_ref[z, :, NS + y * PEAK : NS + (y + 1) * PEAK] = got_ref[y, :, NS:]


def middle(got):
    width = NS + 4 * (got.shape[2] - NS)
    return pl.pallas_call(
        middle_kernel,
        in_specs=[WHOLE],
        out_specs=WHOLE,
        out_shape=jax.ShapeDtypeStruct((8, OWN, width), bf16),
        name="middle",
    )(got)


def prox(got_ref, point, previous, scale, column_ref, factor):
    total = got_ref[0, :, :NS].astype(f32)
    for z in range(1, 8):
        total = total + got_ref[z, :, :NS].astype(f32)
    step, threshold, counts = (column_ref[:, i : i + 1] for i in range(3))
    moved = point + step * (scale * total / counts)
    current = moved - jnp.clip(moved, -threshold, threshold)
    return current + factor * (current - previous), current


def sweep_kernel(factor, has_extra, *refs):
    got_ref, point_ref, previous_ref, scale_ref, center_ref, column_ref, near_ref = refs[:7]
    pieces = refs[7:17]
    extra_ref = refs[17] if has_extra else None
    out_ref, next_ref, current_ref = refs[-3:]
    scale = scale_ref[...]
    point, current = prox(got_ref, point_ref[...], previous_ref[...], scale, column_ref, factor)
    next_ref[...] = point
    current_ref[...] = current
    weighted = scale * point
    shift = jnp.sum(center_ref[...] * weighted, axis=1, keepdims=True)
    scaled = weighted.astype(bf16)

    def dot(turn, piece):
        return lax.dot_general(
            scaled[:, turn * SHARE : (turn + 1) * SHARE],
            piece[...],
            LAST,
            preferred_element_type=f32,
        )

    def half(group):
        own, right, far_a, far_b, left = group
        far = jnp.concatenate([dot(2, far_a), dot(2, far_b)], axis=1)
        return dot(0, own) + dot(1, right) + far + dot(3, left)

    fitted = jnp.concatenate([half(pieces[:5]), half(pieces[5:])], axis=1) - shift
    residual = (near_ref[1:] * (near_ref[:1] - fitted)).astype(bf16)
    send_gradient(residual, center_ref, pieces, extra_ref, out_ref)


def sweep(factor, extra, *operands):
    width = NS if extra is None else NS + PEAK
    state = jax.ShapeDtypeStruct((OWN, NS), f32)
    more = () if extra is None else (extra,)
    return pl.pallas_call(
        functools.partial(sweep_kernel, factor, extra is not None),
        in_specs=[WHOLE] * (len(operands) + len(more)),
        out_specs=[WHOLE] * 3,
        out_shape=[jax.ShapeDtypeStruct((4, OWN, width), bf16), state, state],
        name="sweep",
    )(*operands, *more)


def last_kernel(got_ref, point_ref, previous_ref, scale_ref, column_ref, out_ref):
    current = prox(got_ref, point_ref[...], previous_ref[...], scale_ref[...], column_ref, 0.0)[1]
    for turn in range(4):
        piece = current[:, turn * SHARE : (turn + 1) * SHARE]
        out_ref[turn] = piece
        out_ref[turn + 4] = piece


def last(got, point, previous, scale, columns):
    return pl.pallas_call(
        last_kernel,
        in_specs=[WHOLE] * 5,
        out_specs=WHOLE,
        out_shape=jax.ShapeDtypeStruct((8, OWN, SHARE), f32),
        name="last",
    )(got, point, previous, scale, columns)


def exchange(value, axis):
    return lax.all_to_all(value, axis, 0, 0, tiled=True)


def swap(value):
    return lax.ppermute(value, "core", [(0, 1), (1, 0)])


def onward(value):
    return lax.ppermute(value, "x", [(i, (i + 1) % 4) for i in range(4)])


def backward(value):
    return lax.ppermute(value, "x", [(i, (i + 3) % 4) for i in range(4)])


def turned(value, count, axis):
    twice = jnp.concatenate([value, value], axis=axis)
    return lax.dynamic_slice_in_dim(twice, count, value.shape[axis], axis)


def lanes(wide):
    return wide.reshape(wide.shape[0], -1, BLOCK).transpose(1, 0, 2)


def shards(
    dosage, centers, scales, phenotype, fold_ids, strong_blocks, warm_start, penalty, step_size
):
    rows, local_width = dosage.shape
    local_blocks = local_width // BLOCK
    core = lax.axis_index("core")
    place = lax.axis_index("x")
    slot = lax.axis_index(PLANE)
    first_fit = core * HALF + place * OWN
    other_fit = (1 - core) * HALF + place * OWN
    ahead = place * EACH

    relative = strong_blocks - place * local_blocks
    owned = (relative >= 0) & (relative < local_blocks)
    center_rows = centers.reshape(-1, BLOCK)
    scale_rows = scales.reshape(-1, BLOCK)
    strong_centers = center_rows[strong_blocks]
    strong_scales = scale_rows[strong_blocks]
    flat_scales = strong_scales.reshape(1, NS)
    coef_mask = jnp.repeat(owned.astype(f32), BLOCK)[None, :]
    warm = warm_start.T
    masked = (flat_scales * warm) * coef_mask
    scaled = masked.astype(bf16)
    shift = jnp.sum(strong_centers.reshape(1, NS) * masked, axis=1, keepdims=True)
    index = jnp.clip(turned(relative, ahead, 0), 0, local_blocks - 1).astype(jnp.int32)
    index = jnp.concatenate([index, place.astype(jnp.int32)[None]])
    own, right, far_a, far_b, left, fit_part = pick_blocks(index, dosage, scaled, shift)

    samples = jnp.stack([phenotype, fold_ids.astype(f32)])
    samples_other = swap(samples)
    fit_part, far_a, far_b = lax.optimization_barrier((fit_part, far_a, far_b))
    via_left = onward(far_a)
    via_right = backward(far_b)
    fitted = exchange(fit_part, "x")
    fitted, via_left, via_right, right, left = lax.optimization_barrier(
        (fitted, via_left, via_right, right, left)
    )
    from_left = onward(right)
    from_right = backward(left)
    far_a = onward(via_left)
    far_b = backward(via_right)

    fit_folds = (jnp.arange(FITS, dtype=jnp.int32) % FOLDS).astype(f32)
    weights = (samples[1:] != fit_folds[:, None]).astype(f32)
    fitted = jnp.sum(fitted.astype(f32), axis=0)
    residual = (weights * (samples[:1] - fitted)).astype(bf16)
    column_sums = jnp.sum(residual.astype(f32), axis=1, keepdims=True)
    residual_own = lax.dynamic_slice_in_dim(residual, first_fit, OWN, 0)
    residual_other = swap(lax.dynamic_slice_in_dim(residual, other_fit, OWN, 0))
    residual_near = jnp.concatenate([residual_own, residual_other], axis=1)

    local_centers = lax.dynamic_slice_in_dim(centers, place * local_width, local_width, 0)
    local_scales = lax.dynamic_slice_in_dim(scale_rows, place * local_blocks, local_blocks, 0)
    cross = jnp.dot(residual, dosage, preferred_element_type=f32) - (
        local_centers[None, :] * column_sums
    )
    keep = lax.dynamic_slice_in_dim(cross, core * HALF, HALF, 0)
    give = lax.dynamic_slice_in_dim(cross, (1 - core) * HALF, HALF, 0)
    summed = (keep + swap(give.astype(bf16)).astype(f32)).astype(bf16)
    padded = jnp.concatenate(
        [lanes(summed), jnp.zeros((PARTS * MBLK - local_blocks, HALF, BLOCK), bf16)], axis=0
    ).reshape(PARTS, MBLK * HALF, BLOCK)
    near = jnp.concatenate([samples, samples_other], axis=1)
    near_weights = (near[1:] != fit_folds[:FOLDS, None]).astype(f32)
    tally_rows = jnp.zeros((8, BLOCK), f32)
    tally_rows = tally_rows.at[0, :FOLDS].set(jnp.sum(near_weights[:, :rows], axis=1))
    tally_rows = tally_rows.at[1, :FOLDS].set(jnp.sum(near_weights[:, rows:], axis=1))
    message = jnp.concatenate(
        [padded, jnp.broadcast_to(tally_rows.astype(bf16)[None], (PARTS, 8, BLOCK))], axis=1
    )
    owner = jnp.repeat(turned(strong_blocks, ahead, 0)[:EACH] // local_blocks, BLOCK)[None, :]
    wide_scale = turned(strong_scales, ahead, 0).reshape(1, NS)
    wide_center = turned(strong_centers, ahead, 0).reshape(1, NS)
    arrived = exchange(message, PLANE)

    share = jnp.where(owner == (place + 3) % 4, from_left, own)
    share = jnp.where(owner == (place + 1) % 4, from_right, share)
    share = jnp.where(
        owner == (place + 2) % 4, jnp.concatenate([far_a, far_b], axis=0), share
    )
    share_left = onward(share)
    share_right = backward(share)
    share_other = swap(share)
    far_a = onward(share_left[:PART])
    far_b = backward(share_right[PART:])
    strong = [share, share_right, far_a, far_b, share_left]
    strong += [share_other] + [swap(piece) for piece in strong[1:]]
    strong = lax.optimization_barrier(tuple(strong))

    first = jnp.sum(arrived.astype(f32), axis=0)
    edge = MBLK * HALF
    counts = (first[edge] + first[edge + 1])[:FOLDS, None]
    fit_penalty = jnp.repeat(penalty, FOLDS)
    half_penalty = lax.dynamic_slice_in_dim(fit_penalty, core * HALF, HALF, 0)[:, None]
    margin_scales = jnp.concatenate(
        [local_scales, jnp.zeros((PARTS * MBLK - local_blocks, BLOCK), f32)], axis=0
    )
    margin_scales = lax.dynamic_slice_in_dim(margin_scales, slot * MBLK, MBLK, 0)
    kkt = margin_scales[:, None, :] * first[:edge].reshape(MBLK, HALF, BLOCK)
    kkt = kkt / jnp.tile(counts, (HALF // FOLDS, 1))[None]
    peak = jnp.max(jnp.abs(kkt) / half_penalty[None], axis=1).reshape(1, PEAK)
    peak_high = peak.astype(bf16)
    peak_low = (peak - peak_high.astype(f32)).astype(bf16)
    extra = jnp.concatenate([peak_high, peak_low, jnp.zeros((2, PEAK), bf16)], axis=0)

    step = lax.dynamic_slice_in_dim(step_size, first_fit, OWN, 0)[:, None]
    threshold = step * lax.dynamic_slice_in_dim(fit_penalty, first_fit, OWN, 0)[:, None]
    columns = jnp.concatenate([step, threshold, counts], axis=1)
    near = jnp.concatenate([near[:1], near_weights], axis=0)
    start = lax.dynamic_slice_in_dim(warm, first_fit, OWN, 0).reshape(OWN, SLOTS, BLOCK)
    point = turned(start, ahead, 1).reshape(OWN, NS)
    previous = point

    sent = first_sweep(residual_near, wide_center, strong)
    got = exchange(middle(exchange(sent, "y")), "z")
    momentum = 1.0
    margin = None
    for round in range(1, ITERS):
        following = (1.0 + math.sqrt(1.0 + 4.0 * momentum * momentum)) / 2.0
        factor = (momentum - 1.0) / following
        sent, point, previous = sweep(
            factor,
            extra if round == 1 else None,
            got,
            point,
            previous,
            wide_scale,
            wide_center,
            columns,
            near,
            *strong,
        )
        got = exchange(middle(exchange(sent, "y")), "z")
        momentum = following
        if round == 1:
            peaks = got[:, :2, NS:].astype(f32)
            peaks = jnp.sum(peaks, axis=1).reshape(PARTS * PEAK)[:local_width]
            margin = jnp.maximum(peaks, swap(peaks))
    leaving = last(got, point, previous, wide_scale, columns)
    leaving = turned(leaving[:4], (4 - place) % 4, 0)
    landed = exchange(jnp.concatenate([leaving, leaving], axis=0), ("core", "x"))
    return (margin, landed.reshape(FITS, SHARE).T)


def solution(mesh):
    cube = Mesh(mesh.devices.reshape(8, 4, 2, 4), ("z", "y", "core", "x"))
    samp = ("z", "y", "core")
    return jax.shard_map(
        shards,
        mesh=cube,
        in_specs=(P(samp, "x"), P(), P(), P(samp), P(samp), P(), P(), P(), P()),
        out_specs=(P("x"), P("x", None)),
        check_vma=False,
    )
```

time: 1090 us -> 198 us (0.18)
  waiting for transfers between devices: 810 us -> 32.3 us
  blocking collectives: 171 us -> 32.3 us
  starting transfers between devices: 0.16 us -> 72.6 us
  local copies, waits for them, and re-layouts: 68.7 us -> 13.1 us
  Pallas kernels: 0 us -> 26.7 us
  between operations: 14 us -> 1.08 us
    psum x4 -> x0, waiting for transfers between devices: 810 us -> none  [the longest x3 637 us: shards(): gradient_total = lax.psum(gradient_cross, ('samp', 'var'))]
    psum x4 -> x0, blocking collectives: 171 us -> none  [the longest x1 131 us: shards(): counts = lax.psum(jnp.sum(weights, axis=0), 'samp')]
    gather x4 -> x2, local copies, waits for them, and re-layouts: 52.4 us -> 2.06 us  [the longest x1 1.49 us: shards(): strong_centers = center_rows[strong_blocks]]
    all_to_all x0 -> x6, starting transfers between devices: none -> 40.1 us  [exchange(): return lax.all_to_all(value, axis, 0, 0, tiled=True)]
    ppermute x0 -> x19, starting transfers between devices: none -> 32.5 us  [the longest x9 19.5 us: swap(): return lax.ppermute(value, 'core', [(0, 1), (1, 0)])]
    all_to_all x0 -> x3, blocking collectives: none -> 32.3 us  [exchange(): return lax.all_to_all(value, axis, 0, 0, tiled=True)]
    pallas_call x0 -> x8, Pallas kernels: none -> 26.7 us  [the longest x2 9.68 us: sweep(): pl.pallas_call(functools.partial(sweep_kernel, factor, extra is not None)...]
    all_to_all x0 -> x6, waiting for transfers between devices: none -> 18.3 us  [exchange(): return lax.all_to_all(value, axis, 0, 0, tiled=True)]
  transfers between devices with their start and end apart: 4 -> 25, of which waited for: 4 -> 8; matrix products, arithmetic and copies ran while one was open for 1% -> 8% of each run, Pallas kernels for 0% -> 1%
where the time goes in v3:
time: 198 us; the launch traced here: 196 us
  starting transfers between devices  72.6 us (37%)
  waiting for transfers between devices  32.3 us (16%)
  blocking collectives  32.3 us (16%)
  Pallas kernels  26.7 us (13%)
  other arithmetic  14.9 us (8%)
  local copies, waits for them, and re-layouts  13.1 us (7%)
  matrix products  3.49 us (2%)
    all_to_all x6, starting transfers between devices, exchange(): return lax.all_to_all(value, axis, 0, 0, tiled=True)  40.1 us
    all_to_all x3, blocking collectives, exchange(): return lax.all_to_all(value, axis, 0, 0, tiled=True)  32.3 us
    ppermute x9, starting transfers between devices, swap(): return lax.ppermute(value, 'core', [(0, 1), (1, 0)])  19.5 us
    all_to_all x6, waiting for transfers between devices, exchange(): return lax.all_to_all(value, axis, 0, 0, tiled=True)  18.3 us
    ppermute x5, waiting for transfers between devices, onward(): return lax.ppermute(value, 'x', [(i, (i + 1) % 4) for i in range(4)])  12.6 us
    ppermute x5, starting transfers between devices, backward(): return lax.ppermute(value, 'x', [(i, (i + 3) % 4) for i in range(4)])  10.4 us
    pallas_call x2, Pallas kernels, sweep(): pl.pallas_call(functools.partial(sweep_kernel, factor, extra is not None)...  9.68 us
    pallas_call x1, Pallas kernels, pick_blocks(): pl.pallas_call(pick_kernel, in_specs=[pl.BlockSpec(memory_space=pltpu.SME...  6.83 us
  transfers between devices with their start and end apart: 25, of which 8 were waited for; matrix products, arithmetic and copies ran while one was open for 8% of the time, Pallas kernels for 1%

profile of v3, /device:TPU:1, one launch (start us, length us, event | category | flops | bytes accessed | tf_op | source)
XLA Modules:
  0.0 196.4 jit_solution(719733617032475048)
XLA Ops:
  5.0 1.9 multiply_reduce_fusion
  8.3 6.8 %pick_blocks.1 = (bf16[256,1024]{1,0:T(8,128)(2,1)}, bf16[256,1024]{1,0:T(8,128)(2,1)}, bf16[128,1024]{1,0:T(8,128)(2,1)}, bf16[128,1024]{1,0:T(8,128)(2,1)}, bf...) custom-call(s32[33]{0:T(128)} %pad_add_fusion.1.index_ref, bf16[256,10240]{1,0:T(8,128)(2,1)} %source_ref.1, ...), custom_call_target="tpu_custom_call" | custom-call | tf_op jit(solution)/shard_map/pick_blocks/pallas_call | solution.py:80
  16.7 1.8 collective-permute-start.1
  18.5 3.3 %all-to-all-start = ((bf16[4,32,256]{2,1,0:T(8,128)(2,1)}), bf16[4,32,256]{2,1,0:T(8,128)(2,1)S(1)}, u32[]{:S(2)}, u32[]{:S(2)}) async-start(bf16[4,32,256]{2,1,0:T(8,128)(2,1)} %get-tuple-element.59), calls=%async_computation | async-start | bytes 131072 | tf_op jit(solution)/shard_map/all_to_all | solution.py:229
  21.8 3.3 %collective-permute-start.17 = (f32[2,256]{1,0:T(2,128)S(1)}, f32[2,256]{1,0:T(2,128)S(1)}, u32[]{:S(2)}, u32[]{:S(2)}) collective-permute-start(f32[2,256]{1,0:T(2,128)S(1)} %pad_maximum_fusion.5), channel_id=1, source_target_pairs={{0,4},{4,0},{1,5},{5,1},{2,6},{6,2},{3,7},{7,3},{8,12},{12,8},{9,1... | collective-permute-start | bytes 6152 | tf_op jit(solution)/shard_map/ppermute | solution.py:233
  29.3 3.5 %convolution_subtract_fusion = f32[32,10240]{1,0:T(8,128)S(1)} fusion(bf16[32,256]{1,0:T(8,128)(2,1)S(1)} %get-tuple-element.89, bf16[256,10240]{1,0:T(8,128)(2,1)} %source_ref.1, f32[32]{0:T(128)S(1)} %get-tuple-element.88, f32[10240]{0:T(1024)S(1)} %dynamic_slice.61), kind=kOutput, calls=%fused_computation.2 | convolution fusion | flops 168427520 | bytes 6611072 | tf_op jit(solution)/shard_map/dot_general | solution.py:306
  32.9 2.1 %collective-permute-start.16 = (bf16[16,10240]{1,0:T(8,128)(2,1)S(1)}, bf16[16,10240]{1,0:T(8,128)(2,1)S(1)}, u32[]{:S(2)}, u32[]{:S(2)}) collective-permute-start(bf16[16,10240]{1,0:T(8,128)(2,1)S(1)} %dynamic-slice_convert_fusion), channel_id=1, source_target_pairs={{0,4},{4,0},{1,5},{5,1},{2,6},{6,2},{3,7},{7,3},{8,12},{12,8},{9,1... | collective-permute-start | bytes 983048 | tf_op jit(solution)/shard_map/ppermute | solution.py:233
  37.2 2.4 %collective-permute-start.4 = (bf16[128,1024]{1,0:T(8,128)(2,1)}, bf16[128,1024]{1,0:T(8,128)(2,1)}, u32[]{:S(2)}, u32[]{:S(2)}) collective-permute-start(bf16[128,1024]{1,0:T(8,128)(2,1)} %copy-done.16), channel_id=1, source_target_pairs={{0,3},{1,0},{2,1},{3,2},{4,7},{5,4},{6,5},{7,6},{8,11},{9,8},{10,9... | collective-permute-start | bytes 786440 | tf_op jit(solution)/shard_map/ppermute | solution.py:241
  40.6 9.6 %all-to-all-start.3 = ((bf16[32,56,128]{2,1,0:T(8,128)(2,1)}), bf16[32,56,128]{2,1,0:T(8,128)(2,1)}, u32[]{:S(2)}, u32[]{:S(2)}) async-start(bf16[32,56,128]{2,1,0:T(8,128)(2,1)} %pad_maximum_fusion), calls=%async_computation.3 | async-start | bytes 917504 | tf_op jit(solution)/shard_map/all_to_all | solution.py:229
  50.2 5.6 %collective-permute-done.3 = bf16[128,1024]{1,0:T(8,128)(2,1)S(1)} collective-permute-done((bf16[128,1024]{1,0:T(8,128)(2,1)}, bf16[128,1024]{1,0:T(8,128)(2,1)S(1)}, u32[]{:S(2)}, u32[]{:S(2)}) %collective-permute-start.3) | collective-permute-done | bytes 262176 | tf_op jit(solution)/shard_map/ppermute | solution.py:237
  57.2 2.7 %collective-permute-start.7 = (bf16[256,1024]{1,0:T(8,128)(2,1)S(1)}, bf16[256,1024]{1,0:T(8,128)(2,1)S(1)}, u32[]{:S(2)}, u32[]{:S(2)}) collective-permute-start(bf16[256,1024]{1,0:T(8,128)(2,1)S(1)} %maximum_select_fusion.refs_0_.refs_7_), channel_id=1, source_target_pairs={{0,3},{1,0},{2,1},{3,2},{4,7},{5,4},{6,5},{7,6},{8,11},{9,8},{10,9... | collective-permute-start | bytes 1572872 | tf_op jit(solution)/shard_map/ppermute | solution.py:241
  61.1 2.2 %collective-permute-start.2 = (bf16[4,256]{1,0:T(4,128)(2,1)S(1)}, bf16[4,256]{1,0:T(4,128)(2,1)S(1)}, u32[]{:S(2)}, u32[]{:S(2)}) collective-permute-start(bf16[4,256]{1,0:T(4,128)(2,1)S(1)} %get-tuple-element.97), channel_id=1, source_target_pairs={{0,4},{4,0},{1,5},{5,1},{2,6},{6,2},{3,7},{7,3},{8,12},{12,8},{9,1... | collective-permute-start | bytes 6152 | tf_op jit(solution)/shard_map/ppermute | solution.py:233
  63.3 7.0 %collective-permute-done.8.refs_4_.refs_11_ = bf16[256,1024]{1,0:T(8,128)(2,1)S(1)} collective-permute-done((bf16[256,1024]{1,0:T(8,128)(2,1)S(1)}, bf16[256,1024]{1,0:T(8,128)(2,1)S(1)}, u32[]{:S(2)}, u32[]{:S(2)}) %collective-permute-start.8) | collective-permute-done | bytes 524320 | tf_op jit(solution)/shard_map/ppermute | solution.py:237
  71.9 2.7 %collective-permute-start.10 = (bf16[128,1024]{1,0:T(8,128)(2,1)}, bf16[128,1024]{1,0:T(8,128)(2,1)}, u32[]{:S(2)}, u32[]{:S(2)}) collective-permute-start(bf16[128,1024]{1,0:T(8,128)(2,1)} %slice.104), channel_id=1, source_target_pairs={{0,3},{1,0},{2,1},{3,2},{4,7},{5,4},{6,5},{7,6},{8,11},{9,8},{10,9... | collective-permute-start | bytes 786440 | tf_op jit(solution)/shard_map/ppermute | solution.py:241
  75.8 3.0 %collective-permute-start.11 = (bf16[256,1024]{1,0:T(8,128)(2,1)S(1)}, bf16[256,1024]{1,0:T(8,128)(2,1)S(1)}, u32[]{:S(2)}, u32[]{:S(2)}) collective-permute-start(bf16[256,1024]{1,0:T(8,128)(2,1)S(1)} %maximum_select_fusion.refs_0_.refs_7_), channel_id=1, source_target_pairs={{0,4},{4,0},{1,5},{5,1},{2,6},{6,2},{3,7},{7,3},{8,12},{12,8},{9,1... | collective-permute-start | bytes 1572872 | tf_op jit(solution)/shard_map/ppermute | solution.py:233
  84.3 3.5 %first_sweep.1 = bf16[4,4,4096]{2,1,0:T(4,128)(2,1)} custom-call(bf16[4,512]{1,0:T(4,128)(2,1)} %pad_maximum_fusion.3.residual_ref, f32[1,4096]{1,0:T(1,128)} %bitcast.70, bf16[256,1024]{1,0:T(8,128)(2,1)} %copy-done.1, bf16[256,1024]{1,0:T(8,128)(2,1)} %copy-done.3, bf16[128,1024]{1,0:T(8,128)(2,1)} %collective-permute-done.9.refs_2_.refs_9_, ...), custom_call_target="tpu_custom_call" | custom-call | tf_op jit(solution)/shard_map/first_sweep/pallas_call | solution.py:124
  87.8 3.3 %all-to-all-start.1 = ((bf16[4,4,4096]{2,1,0:T(4,128)(2,1)}), bf16[4,4,4096]{2,1,0:T(4,128)(2,1)S(1)}, u32[]{:S(2)}, u32[]{:S(2)}) async-start(bf16[4,4,4096]{2,1,0:T(4,128)(2,1)} %first_sweep.1), calls=%async_computation.1 | async-start | bytes 262144 | tf_op jit(solution)/shard_map/all_to_all | solution.py:229
  91.2 4.7 %all-to-all-done.1.got_ref = bf16[4,4,4096]{2,1,0:T(4,128)(2,1)S(1)} async-done(((bf16[4,4,4096]{2,1,0:T(4,128)(2,1)}), bf16[4,4,4096]{2,1,0:T(4,128)(2,1)S(1)}, u32[]{:S(2)}, u32[]{:S(2)}) %all-to-all-start.1) | async-done | bytes 131104 | tf_op jit(solution)/shard_map/all_to_all | solution.py:229
  98.2 7.5 %all-to-all-start.2 = ((bf16[8,4,4096]{2,1,0:T(4,128)(2,1)}), bf16[8,4,4096]{2,1,0:T(4,128)(2,1)S(1)}, u32[]{:S(2)}, u32[]{:S(2)}) async-start(bf16[8,4,4096]{2,1,0:T(4,128)(2,1)} %middle.3), calls=%async_computation.2 | async-start | bytes 524288 | tf_op jit(solution)/shard_map/all_to_all | solution.py:229
  107.0 7.9 %all-to-all-done.2.refs_0_ = bf16[8,4,4096]{2,1,0:T(4,128)(2,1)S(1)} async-done(((bf16[8,4,4096]{2,1,0:T(4,128)(2,1)}), bf16[8,4,4096]{2,1,0:T(4,128)(2,1)S(1)}, u32[]{:S(2)}, u32[]{:S(2)}) %all-to-all-start.2) | async-done | bytes 262176 | tf_op jit(solution)/shard_map/all_to_all | solution.py:229
  115.6 4.8 %sweep.2 = (bf16[4,4,4480]{2,1,0:T(4,128)(2,1)}, f32[4,4096]{1,0:T(4,128)}, f32[4,4096]{1,0:T(4,128)}) custom-call(bf16[8,4,4096]{2,1,0:T(4,128)(2,1)} %copy-done.7, f32[4,4096]{1,0:T(4,128)} %bitcast.68, f32[4,4096]{1,0:T(4,128)} %bitcast.69, f32[1,4096]{1,0:T(1,128)} %bitcast.73, f32[1,4096]{1,0:T(1,128)} %bitcast.71, ...), custom_call_target="tpu_custom_call" | custom-call | tf_op jit(solution)/shard_map/sweep/pallas_call | solution.py:201
  120.4 8.9 %all_to_all.45.got_ref = bf16[4,4,4480]{2,1,0:T(4,128)(2,1)} all-to-all(bf16[4,4,4480]{2,1,0:T(4,128)(2,1)} %get-tuple-element.80), channel_id=1, replica_groups=mesh['z'=8,'y'=4,'core'=2,'x'=4] {'y'}, dimensions={0} | all-to-all | bytes 286720 | tf_op jit(solution)/shard_map/all_to_all | solution.py:229
  129.3 1.7 middle.4
  131.0 14.6 %all_to_all.46.refs_0_ = bf16[8,4,5632]{2,1,0:T(4,128)(2,1)} all-to-all(bf16[8,4,5632]{2,1,0:T(4,128)(2,1)} %middle.4), channel_id=1, replica_groups=mesh['z'=8,'y'=4,'core'=2,'x'=4] {'z'}, dimensions={0} | all-to-all | bytes 720896 | tf_op jit(solution)/shard_map/all_to_all | solution.py:229
  145.6 4.9 %sweep.3 = (bf16[4,4,4096]{2,1,0:T(4,128)(2,1)}, f32[4,4096]{1,0:T(4,128)}, f32[4,4096]{1,0:T(4,128)}) custom-call(bf16[8,4,5632]{2,1,0:T(4,128)(2,1)} %all_to_all.46.refs_0_, f32[4,4096]{1,0:T(4,128)} %get-tuple-element.81.refs_1_, f32[4,4096]{1,0:T(4,128)} %get-tuple-element.82.refs_2_, f32[1,4096]{1,0:T(1,128)} %bitcast.74, f32[1,4096]{1,0:T(1,128)} %bitcast.72, ...), custom_call_target="tpu_custom_call" | custom-call | tf_op jit(solution)/shard_map/sweep/pallas_call | solution.py:201
  150.4 8.8 %all_to_all.47.got_ref = bf16[4,4,4096]{2,1,0:T(4,128)(2,1)} all-to-all(bf16[4,4,4096]{2,1,0:T(4,128)(2,1)} %get-tuple-element.83), channel_id=1, replica_groups=mesh['z'=8,'y'=4,'core'=2,'x'=4] {'y'}, dimensions={0} | all-to-all | bytes 262144 | tf_op jit(solution)/shard_map/all_to_all | solution.py:229
  159.2 1.6 middle.5
  160.9 3.4 %all-to-all-start.7 = ((bf16[8,4,4096]{2,1,0:T(4,128)(2,1)}), bf16[8,4,4096]{2,1,0:T(4,128)(2,1)S(1)}, u32[]{:S(2)}, u32[]{:S(2)}) async-start(bf16[8,4,4096]{2,1,0:T(4,128)(2,1)} %middle.5), calls=%async_computation.7 | async-start | bytes 524288 | tf_op jit(solution)/shard_map/all_to_all | solution.py:229
  165.4 7.0 %collective-permute-start.18 = (f32[10240]{0:T(1024)S(1)}, f32[10240]{0:T(1024)S(1)}, u32[]{:S(2)}, u32[]{:S(2)}) collective-permute-start(f32[10240]{0:T(1024)S(1)} %slice.113), channel_id=1, source_target_pairs={{0,4},{4,0},{1,5},{5,1},{2,6},{6,2},{3,7},{7,3},{8,12},{12,8},{9,1... | collective-permute-start | bytes 122888 | tf_op jit(solution)/shard_map/ppermute | solution.py:233
  174.2 1.8 last.1
  177.6 13.0 %all-to-all-start.8 = ((f32[8,4,1024]{2,1,0:T(4,128)}), f32[8,4,1024]{2,1,0:T(4,128)S(1)}, u32[]{:S(2)}, u32[]{:S(2)}) async-start(f32[8,4,1024]{2,1,0:T(4,128)} %pad_maximum_fusion.1), calls=%async_computation.8 | async-start | bytes 262144 | tf_op jit(solution)/shard_map/all_to_all | solution.py:229
  191.2 4.6 %all-to-all-done.8 = f32[8,4,1024]{2,1,0:T(4,128)S(1)} async-done(((f32[8,4,1024]{2,1,0:T(4,128)}), f32[8,4,1024]{2,1,0:T(4,128)S(1)}, u32[]{:S(2)}, u32[]{:S(2)}) %all-to-all-start.8) | async-done | bytes 131104 | tf_op jit(solution)/shard_map/all_to_all | solution.py:229
  (139 shorter events, 35.6 us)
Async XLA Ops:
  8.3 13.5 %copy-start.12 = (s32[256]{0:T(256)S(1)}, s32[256]{0:T(256)}, u32[]{:S(2)}) copy-start(s32[256]{0:T(256)} %param.17) | copy-start | bytes 3076
  8.3 13.5 %copy-start.11 = (f32[256]{0:T(256)S(1)}, f32[256]{0:T(256)}, u32[]{:S(2)}) copy-start(f32[256]{0:T(256)} %param.16) | copy-start | bytes 3076
  8.3 16.8 %copy-start.13 = (f32[8]{0:T(128)S(1)}, f32[8]{0:T(128)}, u32[]{:S(2)}) copy-start(f32[8]{0:T(128)} %param.20) | copy-start | bytes 100
  8.3 18.3 %copy-start.14 = (f32[32]{0:T(128)S(1)}, f32[32]{0:T(128)}, u32[]{:S(2)}) copy-start(f32[32]{0:T(128)} %param.21) | copy-start | bytes 388
  15.2 13.3 %collective-permute-start = (bf16[128,1024]{1,0:T(8,128)(2,1)}, bf16[128,1024]{1,0:T(8,128)(2,1)S(1)}, u32[]{:S(2)}, u32[]{:S(2)}) collective-permute-start(bf16[128,1024]{1,0:T(8,128)(2,1)} %get-tuple-element.60), channel_id=1, source_target_pairs={{0,1},{1,2},{2,3},{3,0},{4,5},{5,6},{6,7},{7,4},{8,9},{9,10},{10,1... | collective-permute-start | bytes 786440 | tf_op jit(solution)/shard_map/ppermute | solution.py:237
  16.7 11.8 %collective-permute-start.1 = (bf16[128,1024]{1,0:T(8,128)(2,1)}, bf16[128,1024]{1,0:T(8,128)(2,1)S(1)}, u32[]{:S(2)}, u32[]{:S(2)}) collective-permute-start(bf16[128,1024]{1,0:T(8,128)(2,1)} %get-tuple-element.61), channel_id=1, source_target_pairs={{0,3},{1,0},{2,1},{3,2},{4,7},{5,4},{6,5},{7,6},{8,11},{9,8},{10,9... | collective-permute-start | bytes 786440 | tf_op jit(solution)/shard_map/ppermute | solution.py:241
  18.5 10.0 %all-to-all-start = ((bf16[4,32,256]{2,1,0:T(8,128)(2,1)}), bf16[4,32,256]{2,1,0:T(8,128)(2,1)S(1)}, u32[]{:S(2)}, u32[]{:S(2)}) async-start(bf16[4,32,256]{2,1,0:T(8,128)(2,1)} %get-tuple-element.59), calls=%async_computation | async-start | bytes 131072 | tf_op jit(solution)/shard_map/all_to_all | solution.py:229
  21.8 6.6 %collective-permute-start.17 = (f32[2,256]{1,0:T(2,128)S(1)}, f32[2,256]{1,0:T(2,128)S(1)}, u32[]{:S(2)}, u32[]{:S(2)}) collective-permute-start(f32[2,256]{1,0:T(2,128)S(1)} %pad_maximum_fusion.5), channel_id=1, source_target_pairs={{0,4},{4,0},{1,5},{5,1},{2,6},{6,2},{3,7},{7,3},{8,12},{12,8},{9,1... | collective-permute-start | bytes 6152 | tf_op jit(solution)/shard_map/ppermute | solution.py:233
  32.9 6.8 %collective-permute-start.16 = (bf16[16,10240]{1,0:T(8,128)(2,1)S(1)}, bf16[16,10240]{1,0:T(8,128)(2,1)S(1)}, u32[]{:S(2)}, u32[]{:S(2)}) collective-permute-start(bf16[16,10240]{1,0:T(8,128)(2,1)S(1)} %dynamic-slice_convert_fusion), channel_id=1, source_target_pairs={{0,4},{4,0},{1,5},{5,1},{2,6},{6,2},{3,7},{7,3},{8,12},{12,8},{9,1... | collective-permute-start | bytes 983048 | tf_op jit(solution)/shard_map/ppermute | solution.py:233
  35.0 20.8 %collective-permute-start.5 = (bf16[256,1024]{1,0:T(8,128)(2,1)}, bf16[256,1024]{1,0:T(8,128)(2,1)S(1)}, u32[]{:S(2)}, u32[]{:S(2)}) collective-permute-start(bf16[256,1024]{1,0:T(8,128)(2,1)} %get-tuple-element.67), channel_id=1, source_target_pairs={{0,3},{1,0},{2,1},{3,2},{4,7},{5,4},{6,5},{7,6},{8,11},{9,8},{10,9... | collective-permute-start | bytes 1572872 | tf_op jit(solution)/shard_map/ppermute | solution.py:241
  35.9 19.8 %collective-permute-start.6 = (bf16[256,1024]{1,0:T(8,128)(2,1)}, bf16[256,1024]{1,0:T(8,128)(2,1)S(1)}, u32[]{:S(2)}, u32[]{:S(2)}) collective-permute-start(bf16[256,1024]{1,0:T(8,128)(2,1)} %get-tuple-element.68), channel_id=1, source_target_pairs={{0,1},{1,2},{2,3},{3,0},{4,5},{5,6},{6,7},{7,4},{8,9},{9,10},{10,1... | collective-permute-start | bytes 1572872 | tf_op jit(solution)/shard_map/ppermute | solution.py:237
  36.8 18.9 %collective-permute-start.3 = (bf16[128,1024]{1,0:T(8,128)(2,1)}, bf16[128,1024]{1,0:T(8,128)(2,1)S(1)}, u32[]{:S(2)}, u32[]{:S(2)}) collective-permute-start(bf16[128,1024]{1,0:T(8,128)(2,1)} %copy-done.15), channel_id=1, source_target_pairs={{0,1},{1,2},{2,3},{3,0},{4,5},{5,6},{6,7},{7,4},{8,9},{9,10},{10,1... | collective-permute-start | bytes 786440 | tf_op jit(solution)/shard_map/ppermute | solution.py:237
  37.2 18.5 %collective-permute-start.4 = (bf16[128,1024]{1,0:T(8,128)(2,1)}, bf16[128,1024]{1,0:T(8,128)(2,1)}, u32[]{:S(2)}, u32[]{:S(2)}) collective-permute-start(bf16[128,1024]{1,0:T(8,128)(2,1)} %copy-done.16), channel_id=1, source_target_pairs={{0,3},{1,0},{2,1},{3,2},{4,7},{5,4},{6,5},{7,6},{8,11},{9,8},{10,9... | collective-permute-start | bytes 786440 | tf_op jit(solution)/shard_map/ppermute | solution.py:241
  39.7 16.1 %copy-start.10 = (bf16[256,1024]{1,0:T(8,128)(2,1)S(1)}, bf16[256,1024]{1,0:T(8,128)(2,1)}, u32[]{:S(2)}) copy-start(bf16[256,1024]{1,0:T(8,128)(2,1)} %get-tuple-element.69) | copy-start | bytes 1572868
  40.6 38.7 %all-to-all-start.3 = ((bf16[32,56,128]{2,1,0:T(8,128)(2,1)}), bf16[32,56,128]{2,1,0:T(8,128)(2,1)}, u32[]{:S(2)}, u32[]{:S(2)}) async-start(bf16[32,56,128]{2,1,0:T(8,128)(2,1)} %pad_maximum_fusion), calls=%async_computation.3 | async-start | bytes 917504 | tf_op jit(solution)/shard_map/all_to_all | solution.py:229
  57.1 26.2 %copy-start.1 = (bf16[256,1024]{1,0:T(8,128)(2,1)}, bf16[256,1024]{1,0:T(8,128)(2,1)S(1)}, u32[]{:S(2)}) copy-start(bf16[256,1024]{1,0:T(8,128)(2,1)S(1)} %maximum_select_fusion.refs_0_.refs_7_) | copy-start | bytes 1572868
  57.1 13.2 %collective-permute-start.8 = (bf16[256,1024]{1,0:T(8,128)(2,1)S(1)}, bf16[256,1024]{1,0:T(8,128)(2,1)S(1)}, u32[]{:S(2)}, u32[]{:S(2)}) collective-permute-start(bf16[256,1024]{1,0:T(8,128)(2,1)S(1)} %maximum_select_fusion.refs_0_.refs_7_), channel_id=1, source_target_pairs={{0,1},{1,2},{2,3},{3,0},{4,5},{5,6},{6,7},{7,4},{8,9},{9,10},{10,1... | collective-permute-start | bytes 1572872 | tf_op jit(solution)/shard_map/ppermute | solution.py:237
  57.2 13.9 %collective-permute-start.7 = (bf16[256,1024]{1,0:T(8,128)(2,1)S(1)}, bf16[256,1024]{1,0:T(8,128)(2,1)S(1)}, u32[]{:S(2)}, u32[]{:S(2)}) collective-permute-start(bf16[256,1024]{1,0:T(8,128)(2,1)S(1)} %maximum_select_fusion.refs_0_.refs_7_), channel_id=1, source_target_pairs={{0,3},{1,0},{2,1},{3,2},{4,7},{5,4},{6,5},{7,6},{8,11},{9,8},{10,9... | collective-permute-start | bytes 1572872 | tf_op jit(solution)/shard_map/ppermute | solution.py:241
  61.1 14.0 %collective-permute-start.2 = (bf16[4,256]{1,0:T(4,128)(2,1)S(1)}, bf16[4,256]{1,0:T(4,128)(2,1)S(1)}, u32[]{:S(2)}, u32[]{:S(2)}) collective-permute-start(bf16[4,256]{1,0:T(4,128)(2,1)S(1)} %get-tuple-element.97), channel_id=1, source_target_pairs={{0,4},{4,0},{1,5},{5,1},{2,6},{6,2},{3,7},{7,3},{8,12},{12,8},{9,1... | collective-permute-start | bytes 6152 | tf_op jit(solution)/shard_map/ppermute | solution.py:233
  70.3 13.0 %copy-start.2 = (bf16[256,1024]{1,0:T(8,128)(2,1)}, bf16[256,1024]{1,0:T(8,128)(2,1)S(1)}, u32[]{:S(2)}) copy-start(bf16[256,1024]{1,0:T(8,128)(2,1)S(1)} %collective-permute-done.8.refs_4_.refs_11_) | copy-start | bytes 1572868
  71.1 9.3 %collective-permute-start.9 = (bf16[128,1024]{1,0:T(8,128)(2,1)}, bf16[128,1024]{1,0:T(8,128)(2,1)}, u32[]{:S(2)}, u32[]{:S(2)}) collective-permute-start(bf16[128,1024]{1,0:T(8,128)(2,1)} %slice.103), channel_id=1, source_target_pairs={{0,1},{1,2},{2,3},{3,0},{4,5},{5,6},{6,7},{7,4},{8,9},{9,10},{10,1... | collective-permute-start | bytes 786440 | tf_op jit(solution)/shard_map/ppermute | solution.py:237
  71.9 9.5 %collective-permute-start.10 = (bf16[128,1024]{1,0:T(8,128)(2,1)}, bf16[128,1024]{1,0:T(8,128)(2,1)}, u32[]{:S(2)}, u32[]{:S(2)}) collective-permute-start(bf16[128,1024]{1,0:T(8,128)(2,1)} %slice.104), channel_id=1, source_target_pairs={{0,3},{1,0},{2,1},{3,2},{4,7},{5,4},{6,5},{7,6},{8,11},{9,8},{10,9... | collective-permute-start | bytes 786440 | tf_op jit(solution)/shard_map/ppermute | solution.py:241
  75.8 6.2 %collective-permute-start.11 = (bf16[256,1024]{1,0:T(8,128)(2,1)S(1)}, bf16[256,1024]{1,0:T(8,128)(2,1)S(1)}, u32[]{:S(2)}, u32[]{:S(2)}) collective-permute-start(bf16[256,1024]{1,0:T(8,128)(2,1)S(1)} %maximum_select_fusion.refs_0_.refs_7_), channel_id=1, source_target_pairs={{0,4},{4,0},{1,5},{5,1},{2,6},{6,2},{3,7},{7,3},{8,12},{12,8},{9,1... | collective-permute-start | bytes 1572872 | tf_op jit(solution)/shard_map/ppermute | solution.py:233
  78.7 4.6 %collective-permute-start.12 = (bf16[256,1024]{1,0:T(8,128)(2,1)S(1)}, bf16[256,1024]{1,0:T(8,128)(2,1)S(1)}, u32[]{:S(2)}, u32[]{:S(2)}) collective-permute-start(bf16[256,1024]{1,0:T(8,128)(2,1)S(1)} %collective-permute-done.7.refs_1_.refs_8_), channel_id=1, source_target_pairs={{0,4},{4,0},{1,5},{5,1},{2,6},{6,2},{3,7},{7,3},{8,12},{12,8},{9,1... | collective-permute-start | bytes 1572872 | tf_op jit(solution)/shard_map/ppermute | solution.py:233
  78.7 4.6 %collective-permute-start.15 = (bf16[256,1024]{1,0:T(8,128)(2,1)S(1)}, bf16[256,1024]{1,0:T(8,128)(2,1)S(1)}, u32[]{:S(2)}, u32[]{:S(2)}) collective-permute-start(bf16[256,1024]{1,0:T(8,128)(2,1)S(1)} %collective-permute-done.8.refs_4_.refs_11_), channel_id=1, source_target_pairs={{0,4},{4,0},{1,5},{5,1},{2,6},{6,2},{3,7},{7,3},{8,12},{12,8},{9,1... | collective-permute-start | bytes 1572872 | tf_op jit(solution)/shard_map/ppermute | solution.py:233
  80.4 2.6 %collective-permute-start.13 = (bf16[128,1024]{1,0:T(8,128)(2,1)}, bf16[128,1024]{1,0:T(8,128)(2,1)}, u32[]{:S(2)}, u32[]{:S(2)}) collective-permute-start(bf16[128,1024]{1,0:T(8,128)(2,1)} %collective-permute-done.9.refs_2_.refs_9_), channel_id=1, source_target_pairs={{0,4},{4,0},{1,5},{5,1},{2,6},{6,2},{3,7},{7,3},{8,12},{12,8},{9,1... | collective-permute-start | bytes 786440 | tf_op jit(solution)/shard_map/ppermute | solution.py:233
  81.4 1.9 collective-permute-start.14
  87.8 8.1 %all-to-all-start.1 = ((bf16[4,4,4096]{2,1,0:T(4,128)(2,1)}), bf16[4,4,4096]{2,1,0:T(4,128)(2,1)S(1)}, u32[]{:S(2)}, u32[]{:S(2)}) async-start(bf16[4,4,4096]{2,1,0:T(4,128)(2,1)} %first_sweep.1), calls=%async_computation.1 | async-start | bytes 262144 | tf_op jit(solution)/shard_map/all_to_all | solution.py:229
  98.2 16.7 %all-to-all-start.2 = ((bf16[8,4,4096]{2,1,0:T(4,128)(2,1)}), bf16[8,4,4096]{2,1,0:T(4,128)(2,1)S(1)}, u32[]{:S(2)}, u32[]{:S(2)}) async-start(bf16[8,4,4096]{2,1,0:T(4,128)(2,1)} %middle.3), calls=%async_computation.2 | async-start | bytes 524288 | tf_op jit(solution)/shard_map/all_to_all | solution.py:229
  160.9 12.7 %all-to-all-start.7 = ((bf16[8,4,4096]{2,1,0:T(4,128)(2,1)}), bf16[8,4,4096]{2,1,0:T(4,128)(2,1)S(1)}, u32[]{:S(2)}, u32[]{:S(2)}) async-start(bf16[8,4,4096]{2,1,0:T(4,128)(2,1)} %middle.5), calls=%async_computation.7 | async-start | bytes 524288 | tf_op jit(solution)/shard_map/all_to_all | solution.py:229
  165.4 25.2 %collective-permute-start.18 = (f32[10240]{0:T(1024)S(1)}, f32[10240]{0:T(1024)S(1)}, u32[]{:S(2)}, u32[]{:S(2)}) collective-permute-start(f32[10240]{0:T(1024)S(1)} %slice.113), channel_id=1, source_target_pairs={{0,4},{4,0},{1,5},{5,1},{2,6},{6,2},{3,7},{7,3},{8,12},{12,8},{9,1... | collective-permute-start | bytes 122888 | tf_op jit(solution)/shard_map/ppermute | solution.py:233
  177.6 18.2 %all-to-all-start.8 = ((f32[8,4,1024]{2,1,0:T(4,128)}), f32[8,4,1024]{2,1,0:T(4,128)S(1)}, u32[]{:S(2)}, u32[]{:S(2)}) async-start(f32[8,4,1024]{2,1,0:T(4,128)} %pad_maximum_fusion.1), calls=%async_computation.8 | async-start | bytes 262144 | tf_op jit(solution)/shard_map/all_to_all | solution.py:229
  (10 other events, 21.2 us)

commit v4 on v3

--- a/solution.py
+++ b/solution.py
@@ -31,11 +31,36 @@
 bf16 = jnp.bfloat16
 LAST = (((1,), (1,)), ((), ()))
 WHOLE = pl.BlockSpec(memory_space=pltpu.VMEM)
+ROOM = pltpu.CompilerParams(vmem_limit_bytes=12 * 2**20)
 
 
 def pick_kernel(
-    index_ref, source_ref, scaled_ref, shift_ref, own, right, far_a, far_b, left, fit_ref, sem
+    block_ref,
+    source_ref,
+    centers_ref,
+    scales_ref,
+    warm_ref,
+    own,
+    right,
+    far_a,
+    far_b,
+    left,
+    fit_ref,
+    wide_scale_ref,
+    wide_center_ref,
+    scale_rows,
+    center_rows,
+    scaled_ref,
+    sem,
 ):
+    place = block_ref[SLOTS]
+    local_blocks = source_ref.shape[1] // BLOCK
+    slots = [lax.rem(place * EACH + r, SLOTS) for r in range(SLOTS)]
+    blocks = [block_ref[slot] for slot in slots]
+    for r, block in enumerate(blocks):
+        pltpu.make_async_copy(scales_ref.at[block], scale_rows.at[r], sem.at[0]).start()
+        pltpu.make_async_copy(centers_ref.at[block], center_rows.at[r], sem.at[1]).start()
+    relative = [block - place * local_blocks for block in blocks]
     moves = (
         (own, 0, 0, ROWS),
         (right, 1, 0, ROWS),
@@ -43,53 +68,78 @@
         (far_b, 2, PART, PART),
         (left, 3, 0, ROWS),
     )
-    copies = []
-    for target, turn, first, height in moves:
+    for k, (target, turn, first, height) in enumerate(moves):
         for i in range(EACH):
-            block = index_ref[turn * EACH + i]
-            copies.append(
-                pltpu.make_async_copy(
-                    source_ref.at[
-                        pl.ds(first, height), pl.ds(pl.multiple_of(block * BLOCK, BLOCK), BLOCK)
-                    ],
-                    target.at[:, pl.ds(i * BLOCK, BLOCK)],
-                    sem.at[len(copies)],
-                )
-            )
-    for copy in copies:
-        copy.start()
-    for copy in copies:
-        copy.wait()
-    place = index_ref[SLOTS]
-
-    def dot(ahead, piece):
-        start = pl.multiple_of(lax.rem(place + ahead, 4) * SHARE, SHARE)
+            local = jnp.clip(relative[turn * EACH + i], 0, local_blocks - 1)
+            pltpu.make_async_copy(
+                source_ref.at[
+                    pl.ds(first, height), pl.ds(pl.multiple_of(local * BLOCK, BLOCK), BLOCK)
+                ],
+                target.at[:, pl.ds(i * BLOCK, BLOCK)],
+                sem.at[2 + k],
+            ).start()
+    pltpu.make_async_copy(scales_ref.at[pl.ds(0, SLOTS)], scale_rows, sem.at[0]).wait()
+    pltpu.make_async_copy(centers_ref.at[pl.ds(0, SLOTS)], center_rows, sem.at[1]).wait()
+    moments = jnp.zeros((FITS, BLOCK), f32)
+    for r in range(SLOTS):
+        lane = pl.ds(r * BLOCK, BLOCK)
+        scale = scale_rows[r]
+        center = center_rows[r]
+        wide_scale_ref[:, lane] = scale
+        wide_center_ref[:, lane] = center
+        mine = (relative[r] >= 0) & (relative[r] < local_blocks)
+        coef = warm_ref[:, pl.ds(pl.multiple_of(slots[r] * BLOCK, BLOCK), BLOCK)]
+        coef = scale * coef * jnp.where(mine, 1.0, 0.0)
+        moments = moments + center * coef
+        scaled_ref[:, lane] = coef.astype(bf16)
+    shift = jnp.sum(moments, axis=1, keepdims=True)
+    for k, (target, turn, first, height) in enumerate(moves):
+        pltpu.make_async_copy(
+            source_ref.at[pl.ds(0, height), pl.ds(0, SHARE)], target, sem.at[2 + k]
+        ).wait()
+
+    def dot(turn, piece):
         return lax.dot_general(
-            scaled_ref[:, pl.ds(start, SHARE)], piece[...], LAST, preferred_element_type=f32
+            scaled_ref[:, turn * SHARE : (turn + 1) * SHARE],
+            piece[...],
+            LAST,
+            preferred_element_type=f32,
         )
 
     far = jnp.concatenate([dot(2, far_a), dot(2, far_b)], axis=1)
-    fit = (dot(0, own) + dot(1, right) + far + dot(3, left) - shift_ref[...]).astype(bf16)
+    fit = (dot(0, own) + dot(1, right) + far + dot(3, left) - shift).astype(bf16)
     for x in range(4):
         fit_ref[x] = fit
 
 
-def pick_blocks(index, dosage, scaled, shift):
+def pick_blocks(blocks, dosage, centers, scales, warm):
     tall = jax.ShapeDtypeStruct((ROWS, SHARE), bf16)
     flat = jax.ShapeDtypeStruct((PART, SHARE), bf16)
+    wide = jax.ShapeDtypeStruct((1, NS), f32)
+    anywhere = pl.BlockSpec(memory_space=pl.ANY)
     return pl.pallas_call(
         pick_kernel,
-        in_specs=[
-            pl.BlockSpec(memory_space=pltpu.SMEM),
-            pl.BlockSpec(memory_space=pl.ANY),
-            WHOLE,
-            WHOLE,
+        in_specs=[pl.BlockSpec(memory_space=pltpu.SMEM), anywhere, anywhere, anywhere, WHOLE],
+        out_specs=[WHOLE] * 8,
+        out_shape=[
+            tall,
+            tall,
+            flat,
+            flat,
+            tall,
+            jax.ShapeDtypeStruct((4, FITS, ROWS), bf16),
+            wide,
+            wide,
         ],
-        out_specs=[WHOLE] * 6,
-        out_shape=[tall, tall, flat, flat, tall, jax.ShapeDtypeStruct((4, FITS, ROWS), bf16)],
-        scratch_shapes=[pltpu.SemaphoreType.DMA((5 * EACH,))],
+        scratch_shapes=[
+            pltpu.VMEM((SLOTS, 1, BLOCK), f32),
+            pltpu.VMEM((SLOTS, 1, BLOCK), f32),
+            pltpu.VMEM((FITS, NS), bf16),
+            pltpu.SemaphoreType.DMA((7,)),
+        ],
+        compiler_params=ROOM,
         name="pick_blocks",
-    )(index, dosage, scaled, shift)
+    )(blocks, dosage, centers, scales, warm)
 
 
 def send_gradient(residual, center_ref, pieces, extra_ref, out_ref):
@@ -126,6 +176,7 @@
         in_specs=[WHOLE] * 12,
         out_specs=WHOLE,
         out_shape=jax.ShapeDtypeStruct((4, OWN, NS), bf16),
+        compiler_params=ROOM,
         name="first_sweep",
     )(residual, center, *pieces)
 
@@ -149,6 +200,7 @@
         in_specs=[WHOLE],
         out_specs=WHOLE,
         out_shape=jax.ShapeDtypeStruct((8, OWN, width), bf16),
+        compiler_params=ROOM,
         name="middle",
     )(got)
 
@@ -203,26 +255,29 @@
         in_specs=[WHOLE] * (len(operands) + len(more)),
         out_specs=[WHOLE] * 3,
         out_shape=[jax.ShapeDtypeStruct((4, OWN, width), bf16), state, state],
+        compiler_params=ROOM,
         name="sweep",
     )(*operands, *more)
 
 
-def last_kernel(got_ref, point_ref, previous_ref, scale_ref, column_ref, out_ref):
+def last_kernel(place_ref, got_ref, point_ref, previous_ref, scale_ref, column_ref, out_ref):
     current = prox(got_ref, point_ref[...], previous_ref[...], scale_ref[...], column_ref, 0.0)[1]
     for turn in range(4):
         piece = current[:, turn * SHARE : (turn + 1) * SHARE]
-        out_ref[turn] = piece
-        out_ref[turn + 4] = piece
-
-
-def last(got, point, previous, scale, columns):
+        spot = lax.rem(place_ref[0] + turn, 4)
+        out_ref[spot] = piece
+        out_ref[spot + 4] = piece
+
+
+def last(place, got, point, previous, scale, columns):
     return pl.pallas_call(
         last_kernel,
-        in_specs=[WHOLE] * 5,
+        in_specs=[pl.BlockSpec(memory_space=pltpu.SMEM)] + [WHOLE] * 5,
         out_specs=WHOLE,
         out_shape=jax.ShapeDtypeStruct((8, OWN, SHARE), f32),
+        compiler_params=ROOM,
         name="last",
-    )(got, point, previous, scale, columns)
+    )(place, got, point, previous, scale, columns)
 
 
 def exchange(value, axis):
@@ -262,33 +317,25 @@
     other_fit = (1 - core) * HALF + place * OWN
     ahead = place * EACH
 
-    relative = strong_blocks - place * local_blocks
-    owned = (relative >= 0) & (relative < local_blocks)
-    center_rows = centers.reshape(-1, BLOCK)
     scale_rows = scales.reshape(-1, BLOCK)
-    strong_centers = center_rows[strong_blocks]
-    strong_scales = scale_rows[strong_blocks]
-    flat_scales = strong_scales.reshape(1, NS)
-    coef_mask = jnp.repeat(owned.astype(f32), BLOCK)[None, :]
     warm = warm_start.T
-    masked = (flat_scales * warm) * coef_mask
-    scaled = masked.astype(bf16)
-    shift = jnp.sum(strong_centers.reshape(1, NS) * masked, axis=1, keepdims=True)
-    index = jnp.clip(turned(relative, ahead, 0), 0, local_blocks - 1).astype(jnp.int32)
-    index = jnp.concatenate([index, place.astype(jnp.int32)[None]])
-    own, right, far_a, far_b, left, fit_part = pick_blocks(index, dosage, scaled, shift)
+    spot = place.astype(jnp.int32)[None]
+    own, right, far_a, far_b, left, fit_part, wide_scale, wide_center = pick_blocks(
+        jnp.concatenate([strong_blocks, spot]),
+        dosage,
+        centers.reshape(-1, 1, BLOCK),
+        scales.reshape(-1, 1, BLOCK),
+        warm,
+    )
 
     samples = jnp.stack([phenotype, fold_ids.astype(f32)])
     samples_other = swap(samples)
-    fit_part, far_a, far_b = lax.optimization_barrier((fit_part, far_a, far_b))
     via_left = onward(far_a)
     via_right = backward(far_b)
-    fitted = exchange(fit_part, "x")
-    fitted, via_left, via_right, right, left = lax.optimization_barrier(
-        (fitted, via_left, via_right, right, left)
-    )
     from_left = onward(right)
     from_right = backward(left)
+    fitted = exchange(fit_part, "x")
+    fitted, via_left, via_right = lax.optimization_barrier((fitted, via_left, via_right))
     far_a = onward(via_left)
     far_b = backward(via_right)
 
@@ -321,15 +368,13 @@
         [padded, jnp.broadcast_to(tally_rows.astype(bf16)[None], (PARTS, 8, BLOCK))], axis=1
     )
     owner = jnp.repeat(turned(strong_blocks, ahead, 0)[:EACH] // local_blocks, BLOCK)[None, :]
-    wide_scale = turned(strong_scales, ahead, 0).reshape(1, NS)
-    wide_center = turned(strong_centers, ahead, 0).reshape(1, NS)
-    arrived = exchange(message, PLANE)
-
     share = jnp.where(owner == (place + 3) % 4, from_left, own)
     share = jnp.where(owner == (place + 1) % 4, from_right, share)
     share = jnp.where(
         owner == (place + 2) % 4, jnp.concatenate([far_a, far_b], axis=0), share
     )
+    message, share = lax.optimization_barrier((message, share))
+    arrived = exchange(message, PLANE)
     share_left = onward(share)
     share_right = backward(share)
     share_other = swap(share)
@@ -388,9 +433,8 @@
             peaks = got[:, :2, NS:].astype(f32)
             peaks = jnp.sum(peaks, axis=1).reshape(PARTS * PEAK)[:local_width]
             margin = jnp.maximum(peaks, swap(peaks))
-    leaving = last(got, point, previous, wide_scale, columns)
-    leaving = turned(leaving[:4], (4 - place) % 4, 0)
-    landed = exchange(jnp.concatenate([leaving, leaving], axis=0), ("core", "x"))
+    leaving = last(spot, got, point, previous, wide_scale, columns)
+    landed = exchange(leaving, ("core", "x"))
     return (margin, landed.reshape(FITS, SHARE).T)
 
 

time: 198 us -> 177 us (0.89)
  Pallas kernels: 26.7 us -> 13.6 us
  local copies, waits for them, and re-layouts: 13.1 us -> 19.5 us
  blocking collectives: 32.3 us -> 27.4 us
  other arithmetic: 14.9 us -> 11.1 us
  waiting for transfers between devices: 32.3 us -> 29.3 us
  starting transfers between devices: 72.6 us -> 69.8 us
    all_to_all x3, blocking collectives: 32.3 us -> 27.4 us  [exchange(): return lax.all_to_all(value, axis, 0, 0, tiled=True)]
    pallas_call x1, Pallas kernels: 6.83 us -> 3.18 us  [pick_blocks(): pl.pallas_call(pick_kernel, in_specs=[pl.BlockSpec(memory_space=pltpu.SME...]
    pallas_call x2, Pallas kernels: 9.68 us -> 6.15 us  [sweep(): pl.pallas_call(functools.partial(sweep_kernel, factor, extra is not None)...]
    unnamed x38 -> x42, local copies, waits for them, and re-layouts: 5.19 us -> 8.57 us
    pallas_call x3, Pallas kernels: 4.92 us -> 1.71 us  [middle(): pl.pallas_call(middle_kernel, in_specs=[WHOLE], out_specs=WHOLE, out_shap...]
    ppermute x5, waiting for transfers between devices: 12.6 us -> 10 us  [onward(): return lax.ppermute(value, 'x', [(i, (i + 1) % 4) for i in range(4)])]
    gather x2 -> x0, local copies, waits for them, and re-layouts: 2.06 us -> none  [the longest x1 1.49 us: shards(): strong_centers = center_rows[strong_blocks]]
    concatenate x4 -> x1, other arithmetic: 2.07 us -> 0.07 us  [turned(): twice = jnp.concatenate([value, value], axis=axis)]
  transfers between devices with their start and end apart: 25 -> 25, of which waited for: 8 -> 8; matrix products, arithmetic and copies ran while one was open for 8% -> 13% of each run, Pallas kernels for 1% -> 2%
where the time goes in v4:
time: 177 us; the launch traced here: 175 us
  starting transfers between devices  69.8 us (39%)
  waiting for transfers between devices  29.3 us (17%)
  blocking collectives  27.4 us (15%)
  local copies, waits for them, and re-layouts  19.5 us (11%)
  Pallas kernels  13.6 us (8%)
  other arithmetic  11.1 us (6%)
  matrix products  3.5 us (2%)
    all_to_all x6, starting transfers between devices, exchange(): return lax.all_to_all(value, axis, 0, 0, tiled=True)  39.5 us
    all_to_all x3, blocking collectives, exchange(): return lax.all_to_all(value, axis, 0, 0, tiled=True)  27.4 us
    all_to_all x6, waiting for transfers between devices, exchange(): return lax.all_to_all(value, axis, 0, 0, tiled=True)  18.5 us
    ppermute x9, starting transfers between devices, swap(): return lax.ppermute(value, 'core', [(0, 1), (1, 0)])  17.7 us
    ppermute x5, starting transfers between devices, backward(): return lax.ppermute(value, 'x', [(i, (i + 3) % 4) for i in range(4)])  10.2 us
    ppermute x5, waiting for transfers between devices, onward(): return lax.ppermute(value, 'x', [(i, (i + 1) % 4) for i in range(4)])  10 us
    unnamed x42, local copies, waits for them, and re-layouts  8.57 us
    pallas_call x2, Pallas kernels, sweep(): pl.pallas_call(functools.partial(sweep_kernel, factor, extra is not None)...  6.15 us
  transfers between devices with their start and end apart: 25, of which 8 were waited for; matrix products, arithmetic and copies ran while one was open for 13% of the time, Pallas kernels for 2%

profile of v4, /device:TPU:1, one launch (start us, length us, event | category | flops | bytes accessed | tf_op | source)
XLA Modules:
  0.0 175.2 jit_solution(17352151903278444031)
XLA Ops:
  2.0 3.2 %collective-permute-start.4 = (f32[2,256]{1,0:T(2,128)S(1)}, f32[2,256]{1,0:T(2,128)S(1)}, u32[]{:S(2)}, u32[]{:S(2)}) collective-permute-start(f32[2,256]{1,0:T(2,128)S(1)} %pad_maximum_fusion.4), channel_id=1, source_target_pairs={{0,4},{4,0},{1,5},{5,1},{2,6},{6,2},{3,7},{7,3},{8,12},{12,8},{9,1... | collective-permute-start | bytes 6152 | tf_op jit(solution)/shard_map/ppermute | solution.py:288
  5.9 2.5 %copy-done = bf16[256,10240]{1,0:T(8,128)(2,1)S(1)} copy-done((bf16[256,10240]{1,0:T(8,128)(2,1)S(1)}, bf16[256,10240]{1,0:T(8,128)(2,1)}, u32[]{:S(2)}) %copy-start) | copy-done | bytes 5242904
  11.3 3.2 %pick_blocks.1 = (bf16[256,1024]{1,0:T(8,128)(2,1)S(1)}, bf16[256,1024]{1,0:T(8,128)(2,1)S(1)}, bf16[128,1024]{1,0:T(8,128)(2,1)S(1)}, bf16[128,1024]{1,0:T(8,12...) custom-call(s32[33]{0:T(128)S(1)} %pad_add_fusion.block_ref, ...), custom_call_target="tpu_custom_call" | custom-call | tf_op jit(solution)/shard_map/pick_blocks/pallas_call | solution.py:120
  14.5 3.3 %all-to-all-start = ((bf16[4,32,256]{2,1,0:T(8,128)(2,1)}), bf16[4,32,256]{2,1,0:T(8,128)(2,1)S(1)}, u32[]{:S(2)}, u32[]{:S(2)}) async-start(bf16[4,32,256]{2,1,0:T(8,128)(2,1)} %get-tuple-element.55), calls=%async_computation | async-start | bytes 131072 | tf_op jit(solution)/shard_map/all_to_all | solution.py:284
  17.8 1.4 collective-permute-start
  20.5 1.4 collective-permute-start.7
  25.7 2.2 %collective-permute-done = bf16[128,1024]{1,0:T(8,128)(2,1)} collective-permute-done((bf16[128,1024]{1,0:T(8,128)(2,1)S(1)}, bf16[128,1024]{1,0:T(8,128)(2,1)}, u32[]{:S(2)}, u32[]{:S(2)}) %collective-permute-start) | collective-permute-done | bytes 262176 | tf_op jit(solution)/shard_map/ppermute | solution.py:292
  28.4 2.4 %collective-permute-start.6 = (bf16[128,1024]{1,0:T(8,128)(2,1)}, bf16[128,1024]{1,0:T(8,128)(2,1)}, u32[]{:S(2)}, u32[]{:S(2)}) collective-permute-start(bf16[128,1024]{1,0:T(8,128)(2,1)} %collective-permute-done.1), channel_id=1, source_target_pairs={{0,3},{1,0},{2,1},{3,2},{4,7},{5,4},{6,5},{7,6},{8,11},{9,8},{10,9... | collective-permute-start | bytes 786440 | tf_op jit(solution)/shard_map/ppermute | solution.py:296
  30.8 3.5 %convolution_subtract_fusion = f32[32,10240]{1,0:T(8,128)S(1)} fusion(bf16[32,256]{1,0:T(8,128)(2,1)S(1)} %get-tuple-element.89, bf16[256,10240]{1,0:T(8,128)(2,1)} %source_ref.1, f32[32]{0:T(128)S(1)} %get-tuple-element.88, f32[10240]{0:T(1024)S(1)} %dynamic_slice.41), kind=kOutput, calls=%fused_computation | convolution fusion | flops 168427520 | bytes 6611072 | tf_op jit(solution)/shard_map/dot_general | solution.py:353
  35.1 1.9 %collective-permute-start.3 = (bf16[16,10240]{1,0:T(8,128)(2,1)}, bf16[16,10240]{1,0:T(8,128)(2,1)}, u32[]{:S(2)}, u32[]{:S(2)}) collective-permute-start(bf16[16,10240]{1,0:T(8,128)(2,1)} %dynamic-slice_convert_fusion), channel_id=1, source_target_pairs={{0,4},{4,0},{1,5},{5,1},{2,6},{6,2},{3,7},{7,3},{8,12},{12,8},{9,1... | collective-permute-start | bytes 983048 | tf_op jit(solution)/shard_map/ppermute | solution.py:288
  37.3 7.4 %collective-permute-done.5 = bf16[128,1024]{1,0:T(8,128)(2,1)} collective-permute-done((bf16[128,1024]{1,0:T(8,128)(2,1)}, bf16[128,1024]{1,0:T(8,128)(2,1)}, u32[]{:S(2)}, u32[]{:S(2)}) %collective-permute-start.5) | collective-permute-done | bytes 262176 | tf_op jit(solution)/shard_map/ppermute | solution.py:292
  44.7 1.6 maximum_select_fusion.refs_0_.refs_7_
  48.6 2.4 %collective-permute-start.9 = (bf16[256,1024]{1,0:T(8,128)(2,1)S(1)}, bf16[256,1024]{1,0:T(8,128)(2,1)S(1)}, u32[]{:S(2)}, u32[]{:S(2)}) collective-permute-start(bf16[256,1024]{1,0:T(8,128)(2,1)S(1)} %maximum_select_fusion.refs_0_.refs_7_), channel_id=1, source_target_pairs={{0,3},{1,0},{2,1},{3,2},{4,7},{5,4},{6,5},{7,6},{8,11},{9,8},{10,9... | collective-permute-start | bytes 1572872 | tf_op jit(solution)/shard_map/ppermute | solution.py:296
  50.9 10.2 %all-to-all-start.3 = ((bf16[32,56,128]{2,1,0:T(8,128)(2,1)}), bf16[32,56,128]{2,1,0:T(8,128)(2,1)}, u32[]{:S(2)}, u32[]{:S(2)}) async-start(bf16[32,56,128]{2,1,0:T(8,128)(2,1)} %pad_maximum_fusion), calls=%async_computation.3 | async-start | bytes 917504 | tf_op jit(solution)/shard_map/all_to_all | solution.py:284
  66.0 2.7 %collective-permute-start.12 = (bf16[128,1024]{1,0:T(8,128)(2,1)S(1)}, bf16[128,1024]{1,0:T(8,128)(2,1)}, u32[]{:S(2)}, u32[]{:S(2)}) collective-permute-start(bf16[128,1024]{1,0:T(8,128)(2,1)S(1)} %slice.99), channel_id=1, source_target_pairs={{0,3},{1,0},{2,1},{3,2},{4,7},{5,4},{6,5},{7,6},{8,11},{9,8},{10,9... | collective-permute-start | bytes 786440 | tf_op jit(solution)/shard_map/ppermute | solution.py:296
  68.7 2.5 %collective-permute-start.2 = (bf16[4,256]{1,0:T(4,128)(2,1)S(1)}, bf16[4,256]{1,0:T(4,128)(2,1)S(1)}, u32[]{:S(2)}, u32[]{:S(2)}) collective-permute-start(bf16[4,256]{1,0:T(4,128)(2,1)S(1)} %get-tuple-element.91), channel_id=1, source_target_pairs={{0,4},{4,0},{1,5},{5,1},{2,6},{6,2},{3,7},{7,3},{8,12},{12,8},{9,1... | collective-permute-start | bytes 6152 | tf_op jit(solution)/shard_map/ppermute | solution.py:288
  73.3 2.6 %collective-permute-start.15 = (bf16[128,1024]{1,0:T(8,128)(2,1)S(1)}, bf16[128,1024]{1,0:T(8,128)(2,1)}, u32[]{:S(2)}, u32[]{:S(2)}) collective-permute-start(bf16[128,1024]{1,0:T(8,128)(2,1)S(1)} %collective-permute-done.11.refs_2_.refs_9_), channel_id=1, source_target_pairs={{0,4},{4,0},{1,5},{5,1},{2,6},{6,2},{3,7},{7,3},{8,12},{12,8},{9,1... | collective-permute-start | bytes 786440 | tf_op jit(solution)/shard_map/ppermute | solution.py:288
  79.5 1.8 %first_sweep.1 = bf16[4,4,4096]{2,1,0:T(4,128)(2,1)S(1)} custom-call(bf16[4,512]{1,0:T(4,128)(2,1)S(1)} %pad_maximum_fusion.2.residual_ref, f32[1,4096]{1,0:T(1,128)S(1)} %get-tuple-element.59.center_ref.refs_4_, bf16[256,1024]{1,0:T(8,128)(2,1)S(1)} %maximum_select_fusion.refs_0_.refs_7_, bf16[256,1024]{1,0:T(8,128)(2,1)S(1)} %collective-permute-done.9.refs_1_.refs_8_, ...), custom_call_target="tpu_custom_call" | custom-call | tf_op jit(solution)/shard_map/first_sweep/pallas_call | solution.py:174
  81.9 3.9 %all-to-all-start.1 = ((bf16[4,4,4096]{2,1,0:T(4,128)(2,1)}), bf16[4,4,4096]{2,1,0:T(4,128)(2,1)}, u32[]{:S(2)}, u32[]{:S(2)}) async-start(bf16[4,4,4096]{2,1,0:T(4,128)(2,1)} %copy-done.4), calls=%async_computation.1 | async-start | bytes 262144 | tf_op jit(solution)/shard_map/all_to_all | solution.py:284
  86.7 4.1 %all-to-all-done.1.got_ref = bf16[4,4,4096]{2,1,0:T(4,128)(2,1)} async-done(((bf16[4,4,4096]{2,1,0:T(4,128)(2,1)}), bf16[4,4,4096]{2,1,0:T(4,128)(2,1)}, u32[]{:S(2)}, u32[]{:S(2)}) %all-to-all-start.1) | async-done | bytes 131104 | tf_op jit(solution)/shard_map/all_to_all | solution.py:284
  92.4 6.4 %all-to-all-start.2 = ((bf16[8,4,4096]{2,1,0:T(4,128)(2,1)}), bf16[8,4,4096]{2,1,0:T(4,128)(2,1)}, u32[]{:S(2)}, u32[]{:S(2)}) async-start(bf16[8,4,4096]{2,1,0:T(4,128)(2,1)} %copy-done.2), calls=%async_computation.2 | async-start | bytes 524288 | tf_op jit(solution)/shard_map/all_to_all | solution.py:284
  100.2 8.2 %all-to-all-done.2.refs_0_ = bf16[8,4,4096]{2,1,0:T(4,128)(2,1)} async-done(((bf16[8,4,4096]{2,1,0:T(4,128)(2,1)}), bf16[8,4,4096]{2,1,0:T(4,128)(2,1)}, u32[]{:S(2)}, u32[]{:S(2)}) %all-to-all-start.2) | async-done | bytes 262176 | tf_op jit(solution)/shard_map/all_to_all | solution.py:284
  108.5 3.0 %sweep.2 = (bf16[4,4,4480]{2,1,0:T(4,128)(2,1)S(1)}, f32[4,4096]{1,0:T(4,128)S(1)}, f32[4,4096]{1,0:T(4,128)S(1)}) custom-call(bf16[8,4,4096]{2,1,0:T(4,128)(2,1)} %all-to-all-done.2.refs_0_, f32[4,4096]{1,0:T(4,128)S(1)} %bitcast.59, f32[4,4096]{1,0:T(4,128)S(1)} %bitcast.60, f32[1,4096]{1,0:T(1,128)S(1)} %get-tuple-element.76.refs_3_.scale_ref, ...), custom_call_target="tpu_custom_call" | custom-call | tf_op jit(solution)/shard_map/sweep/pallas_call | solution.py:253
  111.5 7.3 %all_to_all.45.got_ref = bf16[4,4,4480]{2,1,0:T(4,128)(2,1)S(1)} all-to-all(bf16[4,4,4480]{2,1,0:T(4,128)(2,1)S(1)} %get-tuple-element.78), channel_id=1, replica_groups=mesh['z'=8,'y'=4,'core'=2,'x'=4] {'y'}, dimensions={0} | all-to-all | bytes 286720 | tf_op jit(solution)/shard_map/all_to_all | solution.py:284
  118.9 12.9 %all_to_all.46.refs_0_ = bf16[8,4,5632]{2,1,0:T(4,128)(2,1)S(1)} all-to-all(bf16[8,4,5632]{2,1,0:T(4,128)(2,1)S(1)} %middle.4), channel_id=1, replica_groups=mesh['z'=8,'y'=4,'core'=2,'x'=4] {'z'}, dimensions={0} | all-to-all | bytes 720896 | tf_op jit(solution)/shard_map/all_to_all | solution.py:284
  131.7 3.1 %sweep.3 = (bf16[4,4,4096]{2,1,0:T(4,128)(2,1)S(1)}, f32[4,4096]{1,0:T(4,128)S(1)}, f32[4,4096]{1,0:T(4,128)S(1)}) custom-call(bf16[8,4,5632]{2,1,0:T(4,128)(2,1)S(1)} %all_to_all.46.refs_0_, f32[4,4096]{1,0:T(4,128)S(1)} %get-tuple-element.79.refs_1_, f32[4,4096]{1,0:T(4,128)S(1)} %get-tuple-element.80.refs_2_, ...), custom_call_target="tpu_custom_call" | custom-call | tf_op jit(solution)/shard_map/sweep/pallas_call | solution.py:253
  134.8 7.2 %all_to_all.47.got_ref = bf16[4,4,4096]{2,1,0:T(4,128)(2,1)S(1)} all-to-all(bf16[4,4,4096]{2,1,0:T(4,128)(2,1)S(1)} %get-tuple-element.81), channel_id=1, replica_groups=mesh['z'=8,'y'=4,'core'=2,'x'=4] {'y'}, dimensions={0} | all-to-all | bytes 262144 | tf_op jit(solution)/shard_map/all_to_all | solution.py:284
  142.8 3.4 %all-to-all-start.7 = ((bf16[8,4,4096]{2,1,0:T(4,128)(2,1)}), bf16[8,4,4096]{2,1,0:T(4,128)(2,1)S(1)}, u32[]{:S(2)}, u32[]{:S(2)}) async-start(bf16[8,4,4096]{2,1,0:T(4,128)(2,1)} %middle.5), calls=%async_computation.7 | async-start | bytes 524288 | tf_op jit(solution)/shard_map/all_to_all | solution.py:284
  147.3 6.7 %collective-permute-start.18 = (f32[10240]{0:T(1024)S(1)}, f32[10240]{0:T(1024)S(1)}, u32[]{:S(2)}, u32[]{:S(2)}) collective-permute-start(f32[10240]{0:T(1024)S(1)} %slice.105), channel_id=1, source_target_pairs={{0,4},{4,0},{1,5},{5,1},{2,6},{6,2},{3,7},{7,3},{8,12},{12,8},{9,1... | collective-permute-start | bytes 122888 | tf_op jit(solution)/shard_map/ppermute | solution.py:288
  154.0 1.5 all-to-all-done.7.got_ref
  157.1 12.2 %all-to-all-start.8 = ((f32[8,4,1024]{2,1,0:T(4,128)}), f32[8,4,1024]{2,1,0:T(4,128)S(1)}, u32[]{:S(2)}, u32[]{:S(2)}) async-start(f32[8,4,1024]{2,1,0:T(4,128)} %last.1), calls=%async_computation.8 | async-start | bytes 262144 | tf_op jit(solution)/shard_map/all_to_all | solution.py:284
  169.9 4.6 %all-to-all-done.8 = f32[8,4,1024]{2,1,0:T(4,128)S(1)} async-done(((f32[8,4,1024]{2,1,0:T(4,128)}), f32[8,4,1024]{2,1,0:T(4,128)S(1)}, u32[]{:S(2)}, u32[]{:S(2)}) %all-to-all-start.8) | async-done | bytes 131104 | tf_op jit(solution)/shard_map/all_to_all | solution.py:284
  (129 shorter events, 33.6 us)
Async XLA Ops:
  2.0 23.0 %collective-permute-start.4 = (f32[2,256]{1,0:T(2,128)S(1)}, f32[2,256]{1,0:T(2,128)S(1)}, u32[]{:S(2)}, u32[]{:S(2)}) collective-permute-start(f32[2,256]{1,0:T(2,128)S(1)} %pad_maximum_fusion.4), channel_id=1, source_target_pairs={{0,4},{4,0},{1,5},{5,1},{2,6},{6,2},{3,7},{7,3},{8,12},{12,8},{9,1... | collective-permute-start | bytes 6152 | tf_op jit(solution)/shard_map/ppermute | solution.py:288
  11.3 13.7 %copy-start.9 = (f32[256]{0:T(256)S(1)}, f32[256]{0:T(256)}, u32[]{:S(2)}) copy-start(f32[256]{0:T(256)} %param.16) | copy-start | bytes 3076
  14.5 11.2 %all-to-all-start = ((bf16[4,32,256]{2,1,0:T(8,128)(2,1)}), bf16[4,32,256]{2,1,0:T(8,128)(2,1)S(1)}, u32[]{:S(2)}, u32[]{:S(2)}) async-start(bf16[4,32,256]{2,1,0:T(8,128)(2,1)} %get-tuple-element.55), calls=%async_computation | async-start | bytes 131072 | tf_op jit(solution)/shard_map/all_to_all | solution.py:284
  17.8 10.0 %collective-permute-start = (bf16[128,1024]{1,0:T(8,128)(2,1)S(1)}, bf16[128,1024]{1,0:T(8,128)(2,1)}, u32[]{:S(2)}, u32[]{:S(2)}) collective-permute-start(bf16[128,1024]{1,0:T(8,128)(2,1)S(1)} %get-tuple-element.56), channel_id=1, source_target_pairs={{0,1},{1,2},{2,3},{3,0},{4,5},{5,6},{6,7},{7,4},{8,9},{9,10},{10,1... | collective-permute-start | bytes 786440 | tf_op jit(solution)/shard_map/ppermute | solution.py:292
  19.2 8.6 %collective-permute-start.1 = (bf16[128,1024]{1,0:T(8,128)(2,1)S(1)}, bf16[128,1024]{1,0:T(8,128)(2,1)}, u32[]{:S(2)}, u32[]{:S(2)}) collective-permute-start(bf16[128,1024]{1,0:T(8,128)(2,1)S(1)} %get-tuple-element.57), channel_id=1, source_target_pairs={{0,3},{1,0},{2,1},{3,2},{4,7},{5,4},{6,5},{7,6},{8,11},{9,8},{10,9... | collective-permute-start | bytes 786440 | tf_op jit(solution)/shard_map/ppermute | solution.py:296
  20.5 24.2 %collective-permute-start.7 = (bf16[256,1024]{1,0:T(8,128)(2,1)S(1)}, bf16[256,1024]{1,0:T(8,128)(2,1)S(1)}, u32[]{:S(2)}, u32[]{:S(2)}) collective-permute-start(bf16[256,1024]{1,0:T(8,128)(2,1)S(1)} %get-tuple-element.62), channel_id=1, source_target_pairs={{0,3},{1,0},{2,1},{3,2},{4,7},{5,4},{6,5},{7,6},{8,11},{9,8},{10,9... | collective-permute-start | bytes 1572872 | tf_op jit(solution)/shard_map/ppermute | solution.py:296
  21.9 22.8 %collective-permute-start.8 = (bf16[256,1024]{1,0:T(8,128)(2,1)S(1)}, bf16[256,1024]{1,0:T(8,128)(2,1)}, u32[]{:S(2)}, u32[]{:S(2)}) collective-permute-start(bf16[256,1024]{1,0:T(8,128)(2,1)S(1)} %get-tuple-element.63), channel_id=1, source_target_pairs={{0,1},{1,2},{2,3},{3,0},{4,5},{5,6},{6,7},{7,4},{8,9},{9,10},{10,1... | collective-permute-start | bytes 1572872 | tf_op jit(solution)/shard_map/ppermute | solution.py:292
  28.0 16.7 %collective-permute-start.5 = (bf16[128,1024]{1,0:T(8,128)(2,1)}, bf16[128,1024]{1,0:T(8,128)(2,1)}, u32[]{:S(2)}, u32[]{:S(2)}) collective-permute-start(bf16[128,1024]{1,0:T(8,128)(2,1)} %collective-permute-done), channel_id=1, source_target_pairs={{0,1},{1,2},{2,3},{3,0},{4,5},{5,6},{6,7},{7,4},{8,9},{9,10},{10,1... | collective-permute-start | bytes 786440 | tf_op jit(solution)/shard_map/ppermute | solution.py:292
  28.4 16.3 %collective-permute-start.6 = (bf16[128,1024]{1,0:T(8,128)(2,1)}, bf16[128,1024]{1,0:T(8,128)(2,1)}, u32[]{:S(2)}, u32[]{:S(2)}) collective-permute-start(bf16[128,1024]{1,0:T(8,128)(2,1)} %collective-permute-done.1), channel_id=1, source_target_pairs={{0,3},{1,0},{2,1},{3,2},{4,7},{5,4},{6,5},{7,6},{8,11},{9,8},{10,9... | collective-permute-start | bytes 786440 | tf_op jit(solution)/shard_map/ppermute | solution.py:296
  30.8 13.9 %copy-start.11 = (pred[1024]{0:T(1024)(128)(4,1)S(1)}, pred[1024]{0:T(1024)(128)(4,1)}, u32[]{:S(2)}) copy-start(pred[1024]{0:T(1024)(128)(4,1)} %get-tuple-element.100) | copy-start | bytes 3076
  30.8 13.9 %copy-start.12 = (pred[1024]{0:T(1024)(128)(4,1)S(1)}, pred[1024]{0:T(1024)(128)(4,1)}, u32[]{:S(2)}) copy-start(pred[1024]{0:T(1024)(128)(4,1)} %get-tuple-element.101) | copy-start | bytes 3076
  30.8 13.9 %copy-start.15 = (pred[1024]{0:T(1024)(128)(4,1)S(1)}, pred[1024]{0:T(1024)(128)(4,1)}, u32[]{:S(2)}) copy-start(pred[1024]{0:T(1024)(128)(4,1)} %broadcast_bitcast_fusion.2) | copy-start | bytes 3076
  35.1 11.2 %collective-permute-start.3 = (bf16[16,10240]{1,0:T(8,128)(2,1)}, bf16[16,10240]{1,0:T(8,128)(2,1)}, u32[]{:S(2)}, u32[]{:S(2)}) collective-permute-start(bf16[16,10240]{1,0:T(8,128)(2,1)} %dynamic-slice_convert_fusion), channel_id=1, source_target_pairs={{0,4},{4,0},{1,5},{5,1},{2,6},{6,2},{3,7},{7,3},{8,12},{12,8},{9,1... | collective-permute-start | bytes 983048 | tf_op jit(solution)/shard_map/ppermute | solution.py:288
  47.4 13.8 %copy-start.14 = (f32[32]{0:T(128)S(1)}, f32[32]{0:T(128)}, u32[]{:S(2)}) copy-start(f32[32]{0:T(128)} %copy-done.13) | copy-start | bytes 388
  47.4 13.8 %copy-start.17 = (f32[32]{0:T(128)S(1)}, f32[32]{0:T(128)}, u32[]{:S(2)}) copy-start(f32[32]{0:T(128)} %param.21) | copy-start | bytes 388
  48.3 22.9 %copy-start.10 = (f32[1,512]{1,0:T(1,128)S(1)}, f32[1,512]{1,0:T(1,128)}, u32[]{:S(2)}) copy-start(f32[1,512]{1,0:T(1,128)} %get-tuple-element.92) | copy-start | bytes 6148
  48.3 17.4 %collective-permute-start.10 = (bf16[256,1024]{1,0:T(8,128)(2,1)S(1)}, bf16[256,1024]{1,0:T(8,128)(2,1)S(1)}, u32[]{:S(2)}, u32[]{:S(2)}) collective-permute-start(bf16[256,1024]{1,0:T(8,128)(2,1)S(1)} %maximum_select_fusion.refs_0_.refs_7_), channel_id=1, source_target_pairs={{0,1},{1,2},{2,3},{3,0},{4,5},{5,6},{6,7},{7,4},{8,9},{9,10},{10,1... | collective-permute-start | bytes 1572872 | tf_op jit(solution)/shard_map/ppermute | solution.py:292
  48.6 17.4 %collective-permute-start.9 = (bf16[256,1024]{1,0:T(8,128)(2,1)S(1)}, bf16[256,1024]{1,0:T(8,128)(2,1)S(1)}, u32[]{:S(2)}, u32[]{:S(2)}) collective-permute-start(bf16[256,1024]{1,0:T(8,128)(2,1)S(1)} %maximum_select_fusion.refs_0_.refs_7_), channel_id=1, source_target_pairs={{0,3},{1,0},{2,1},{3,2},{4,7},{5,4},{6,5},{7,6},{8,11},{9,8},{10,9... | collective-permute-start | bytes 1572872 | tf_op jit(solution)/shard_map/ppermute | solution.py:296
  50.9 24.9 %all-to-all-start.3 = ((bf16[32,56,128]{2,1,0:T(8,128)(2,1)}), bf16[32,56,128]{2,1,0:T(8,128)(2,1)}, u32[]{:S(2)}, u32[]{:S(2)}) async-start(bf16[32,56,128]{2,1,0:T(8,128)(2,1)} %pad_maximum_fusion), calls=%async_computation.3 | async-start | bytes 917504 | tf_op jit(solution)/shard_map/all_to_all | solution.py:284
  65.6 7.6 %collective-permute-start.11 = (bf16[128,1024]{1,0:T(8,128)(2,1)S(1)}, bf16[128,1024]{1,0:T(8,128)(2,1)S(1)}, u32[]{:S(2)}, u32[]{:S(2)}) collective-permute-start(bf16[128,1024]{1,0:T(8,128)(2,1)S(1)} %slice.98), channel_id=1, source_target_pairs={{0,1},{1,2},{2,3},{3,0},{4,5},{5,6},{6,7},{7,4},{8,9},{9,10},{10,1... | collective-permute-start | bytes 786440 | tf_op jit(solution)/shard_map/ppermute | solution.py:292
  66.0 9.9 %collective-permute-start.12 = (bf16[128,1024]{1,0:T(8,128)(2,1)S(1)}, bf16[128,1024]{1,0:T(8,128)(2,1)}, u32[]{:S(2)}, u32[]{:S(2)}) collective-permute-start(bf16[128,1024]{1,0:T(8,128)(2,1)S(1)} %slice.99), channel_id=1, source_target_pairs={{0,3},{1,0},{2,1},{3,2},{4,7},{5,4},{6,5},{7,6},{8,11},{9,8},{10,9... | collective-permute-start | bytes 786440 | tf_op jit(solution)/shard_map/ppermute | solution.py:296
  68.7 3.3 %collective-permute-start.2 = (bf16[4,256]{1,0:T(4,128)(2,1)S(1)}, bf16[4,256]{1,0:T(4,128)(2,1)S(1)}, u32[]{:S(2)}, u32[]{:S(2)}) collective-permute-start(bf16[4,256]{1,0:T(4,128)(2,1)S(1)} %get-tuple-element.91), channel_id=1, source_target_pairs={{0,4},{4,0},{1,5},{5,1},{2,6},{6,2},{3,7},{7,3},{8,12},{12,8},{9,1... | collective-permute-start | bytes 6152 | tf_op jit(solution)/shard_map/ppermute | solution.py:288
  72.0 7.5 %collective-permute-start.13 = (bf16[256,1024]{1,0:T(8,128)(2,1)S(1)}, bf16[256,1024]{1,0:T(8,128)(2,1)S(1)}, u32[]{:S(2)}, u32[]{:S(2)}) collective-permute-start(bf16[256,1024]{1,0:T(8,128)(2,1)S(1)} %maximum_select_fusion.refs_0_.refs_7_), channel_id=1, source_target_pairs={{0,4},{4,0},{1,5},{5,1},{2,6},{6,2},{3,7},{7,3},{8,12},{12,8},{9,1... | collective-permute-start | bytes 1572872 | tf_op jit(solution)/shard_map/ppermute | solution.py:288
  72.3 7.1 %collective-permute-start.17 = (bf16[256,1024]{1,0:T(8,128)(2,1)S(1)}, bf16[256,1024]{1,0:T(8,128)(2,1)S(1)}, u32[]{:S(2)}, u32[]{:S(2)}) collective-permute-start(bf16[256,1024]{1,0:T(8,128)(2,1)S(1)} %collective-permute-done.10.refs_4_.refs_11_), channel_id=1, source_target_pairs={{0,4},{4,0},{1,5},{5,1},{2,6},{6,2},{3,7},{7,3},{8,12},{12,8},{9,1... | collective-permute-start | bytes 1572872 | tf_op jit(solution)/shard_map/ppermute | solution.py:288
  72.5 7.0 %collective-permute-start.14 = (bf16[256,1024]{1,0:T(8,128)(2,1)S(1)}, bf16[256,1024]{1,0:T(8,128)(2,1)S(1)}, u32[]{:S(2)}, u32[]{:S(2)}) collective-permute-start(bf16[256,1024]{1,0:T(8,128)(2,1)S(1)} %collective-permute-done.9.refs_1_.refs_8_), channel_id=1, source_target_pairs={{0,4},{4,0},{1,5},{5,1},{2,6},{6,2},{3,7},{7,3},{8,12},{12,8},{9,1... | collective-permute-start | bytes 1572872 | tf_op jit(solution)/shard_map/ppermute | solution.py:288
  73.3 6.2 %collective-permute-start.15 = (bf16[128,1024]{1,0:T(8,128)(2,1)S(1)}, bf16[128,1024]{1,0:T(8,128)(2,1)}, u32[]{:S(2)}, u32[]{:S(2)}) collective-permute-start(bf16[128,1024]{1,0:T(8,128)(2,1)S(1)} %collective-permute-done.11.refs_2_.refs_9_), channel_id=1, source_target_pairs={{0,4},{4,0},{1,5},{5,1},{2,6},{6,2},{3,7},{7,3},{8,12},{12,8},{9,1... | collective-permute-start | bytes 786440 | tf_op jit(solution)/shard_map/ppermute | solution.py:288
  75.8 3.6 %collective-permute-start.16 = (bf16[128,1024]{1,0:T(8,128)(2,1)}, bf16[128,1024]{1,0:T(8,128)(2,1)}, u32[]{:S(2)}, u32[]{:S(2)}) collective-permute-start(bf16[128,1024]{1,0:T(8,128)(2,1)} %collective-permute-done.12.refs_3_.refs_10_), channel_id=1, source_target_pairs={{0,4},{4,0},{1,5},{5,1},{2,6},{6,2},{3,7},{7,3},{8,12},{12,8},{9,1... | collective-permute-start | bytes 786440 | tf_op jit(solution)/shard_map/ppermute | solution.py:288
  81.9 8.9 %all-to-all-start.1 = ((bf16[4,4,4096]{2,1,0:T(4,128)(2,1)}), bf16[4,4,4096]{2,1,0:T(4,128)(2,1)}, u32[]{:S(2)}, u32[]{:S(2)}) async-start(bf16[4,4,4096]{2,1,0:T(4,128)(2,1)} %copy-done.4), calls=%async_computation.1 | async-start | bytes 262144 | tf_op jit(solution)/shard_map/all_to_all | solution.py:284
  92.4 16.1 %all-to-all-start.2 = ((bf16[8,4,4096]{2,1,0:T(4,128)(2,1)}), bf16[8,4,4096]{2,1,0:T(4,128)(2,1)}, u32[]{:S(2)}, u32[]{:S(2)}) async-start(bf16[8,4,4096]{2,1,0:T(4,128)(2,1)} %copy-done.2), calls=%async_computation.2 | async-start | bytes 524288 | tf_op jit(solution)/shard_map/all_to_all | solution.py:284
  142.8 12.7 %all-to-all-start.7 = ((bf16[8,4,4096]{2,1,0:T(4,128)(2,1)}), bf16[8,4,4096]{2,1,0:T(4,128)(2,1)S(1)}, u32[]{:S(2)}, u32[]{:S(2)}) async-start(bf16[8,4,4096]{2,1,0:T(4,128)(2,1)} %middle.5), calls=%async_computation.7 | async-start | bytes 524288 | tf_op jit(solution)/shard_map/all_to_all | solution.py:284
  147.3 22.0 %collective-permute-start.18 = (f32[10240]{0:T(1024)S(1)}, f32[10240]{0:T(1024)S(1)}, u32[]{:S(2)}, u32[]{:S(2)}) collective-permute-start(f32[10240]{0:T(1024)S(1)} %slice.105), channel_id=1, source_target_pairs={{0,4},{4,0},{1,5},{5,1},{2,6},{6,2},{3,7},{7,3},{8,12},{12,8},{9,1... | collective-permute-start | bytes 122888 | tf_op jit(solution)/shard_map/ppermute | solution.py:288
  157.1 17.4 %all-to-all-start.8 = ((f32[8,4,1024]{2,1,0:T(4,128)}), f32[8,4,1024]{2,1,0:T(4,128)S(1)}, u32[]{:S(2)}, u32[]{:S(2)}) async-start(f32[8,4,1024]{2,1,0:T(4,128)} %last.1), calls=%async_computation.8 | async-start | bytes 262144 | tf_op jit(solution)/shard_map/all_to_all | solution.py:284
  (12 other events, 42.2 us)

commit v5 on v4

v5 whole, which is shorter than its diff:
```python
import functools
import math

import jax
import jax.numpy as jnp
from jax import lax
from jax.experimental import pallas as pl
from jax.experimental.pallas import tpu as pltpu
from jax.sharding import Mesh
from jax.sharding import PartitionSpec as P

BLOCK = 128
SLOTS = 32
NS = SLOTS * BLOCK
LAMBDAS = 8
FOLDS = 4
FITS = LAMBDAS * FOLDS
HALF = FITS // 2
OWN = 4
SHARE = NS // 4
EACH = SHARE // BLOCK
ITERS = 3
PLANE = ("z", "y")
PARTS = 32
MBLK = 3
ROWS = 256
PART = ROWS // 2
PEAK = MBLK * BLOCK

f32 = jnp.float32
bf16 = jnp.bfloat16
LAST = (((1,), (1,)), ((), ()))
WHOLE = pl.BlockSpec(memory_space=pltpu.VMEM)
ROOM = pltpu.CompilerParams(vmem_limit_bytes=12 * 2**20)


def pick_kernel(
    block_ref,
    source_ref,
    centers_ref,
    scales_ref,
    warm_ref,
    own,
    right,
    far_a,
    far_b,
    left,
    fit_ref,
    wide_ref,
    local_ref,
    state_ref,
    scale_rows,
    center_rows,
    local_rows,
    scaled_ref,
    sem,
):
    place = lax.axis_index("x")
    local_blocks = source_ref.shape[1] // BLOCK
    slots = [lax.rem(place * EACH + r, SLOTS) for r in range(SLOTS)]
    blocks = [block_ref[slot] for slot in slots]
    for r, block in enumerate(blocks):
        pltpu.make_async_copy(scales_ref.at[block], scale_rows.at[r], sem.at[0]).start()
        pltpu.make_async_copy(centers_ref.at[block], center_rows.at[r], sem.at[1]).start()
    pltpu.make_async_copy(
        centers_ref.at[pl.ds(place * local_blocks, local_blocks)], local_rows, sem.at[7]
    ).start()
    relative = [block - place * local_blocks for block in blocks]
    moves = (
        (own, 0, 0, ROWS),
        (right, 1, 0, ROWS),
        (far_a, 2, 0, PART),
        (far_b, 2, PART, PART),
        (left, 3, 0, ROWS),
    )
    for k, (target, turn, first, height) in enumerate(moves):
        for i in range(EACH):
            local = jnp.clip(relative[turn * EACH + i], 0, local_blocks - 1)
            pltpu.make_async_copy(
                source_ref.at[
                    pl.ds(first, height), pl.ds(pl.multiple_of(local * BLOCK, BLOCK), BLOCK)
                ],
                target.at[:, pl.ds(i * BLOCK, BLOCK)],
                sem.at[2 + k],
            ).start()
    pltpu.make_async_copy(scales_ref.at[pl.ds(0, SLOTS)], scale_rows, sem.at[0]).wait()
    pltpu.make_async_copy(centers_ref.at[pl.ds(0, SLOTS)], center_rows, sem.at[1]).wait()
    moments = jnp.zeros((FITS, BLOCK), f32)
    group = lax.axis_index("core") * (HALF // OWN) + place
    for r in range(SLOTS):
        lane = pl.ds(r * BLOCK, BLOCK)
        scale = scale_rows[r]
        center = center_rows[r]
        wide_ref[0:1, lane] = scale
        wide_ref[1:2, lane] = center
        mine = (relative[r] >= 0) & (relative[r] < local_blocks)
        coef = warm_ref[:, pl.ds(pl.multiple_of(slots[r] * BLOCK, BLOCK), BLOCK)]
        start = jnp.zeros((OWN, BLOCK), f32)
        for q in range(FITS // OWN):
            start = jnp.where(group == q, coef[q * OWN : (q + 1) * OWN], start)
        state_ref[:OWN, lane] = start
        state_ref[OWN:, lane] = start
        coef = scale * coef * jnp.where(mine, 1.0, 0.0)
        moments = moments + center * coef
        scaled_ref[:, lane] = coef.astype(bf16)
    shift = jnp.sum(moments, axis=1, keepdims=True)
    pltpu.make_async_copy(
        centers_ref.at[pl.ds(0, local_blocks)], local_rows, sem.at[7]
    ).wait()
    for r in range(local_blocks):
        local_ref[:, r * BLOCK : (r + 1) * BLOCK] = local_rows[r]
    for k, (target, turn, first, height) in enumerate(moves):
        pltpu.make_async_copy(
            source_ref.at[pl.ds(0, height), pl.ds(0, SHARE)], target, sem.at[2 + k]
        ).wait()

    def dot(turn, piece):
        return lax.dot_general(
            scaled_ref[:, turn * SHARE : (turn + 1) * SHARE],
            piece[...],
            LAST,
            preferred_element_type=f32,
        )

    far = jnp.concatenate([dot(2, far_a), dot(2, far_b)], axis=1)
    fit = (dot(0, own) + dot(1, right) + far + dot(3, left) - shift).astype(bf16)
    for x in range(4):
        fit_ref[x] = fit


def pick_blocks(blocks, dosage, centers, scales, warm):
    tall = jax.ShapeDtypeStruct((ROWS, SHARE), bf16)
    flat = jax.ShapeDtypeStruct((PART, SHARE), bf16)
    far = pl.BlockSpec(memory_space=pltpu.HBM)
    return pl.pallas_call(
        pick_kernel,
        in_specs=[pl.BlockSpec(memory_space=pltpu.SMEM), far, far, far, WHOLE],
        out_specs=[WHOLE] * 9,
        out_shape=[
            tall,
            tall,
            flat,
            flat,
            tall,
            jax.ShapeDtypeStruct((4, FITS, ROWS), bf16),
            jax.ShapeDtypeStruct((2, NS), f32),
            jax.ShapeDtypeStruct((1, dosage.shape[1]), f32),
            jax.ShapeDtypeStruct((2 * OWN, NS), f32),
        ],
        scratch_shapes=[
            pltpu.VMEM((SLOTS, 1, BLOCK), f32),
            pltpu.VMEM((SLOTS, 1, BLOCK), f32),
            pltpu.VMEM((dosage.shape[1] // BLOCK, 1, BLOCK), f32),
            pltpu.VMEM((FITS, NS), bf16),
            pltpu.SemaphoreType.DMA((8,)),
        ],
        compiler_params=ROOM,
        name="pick_blocks",
    )(blocks, dosage, centers, scales, warm)


def send_gradient(residuals, wide_ref, pieces, extra_ref, out_ref):
    sums = sum(jnp.sum(part.astype(f32), axis=1, keepdims=True) for part in residuals)

    def half(residual, group):
        own, right, far_a, far_b, left = (piece[...] for piece in group)

        def dot(part, piece):
            return jnp.dot(part, piece, preferred_element_type=f32)

        far = dot(residual[:, :PART], far_a) + dot(residual[:, PART:], far_b)
        return [dot(residual, own), dot(residual, right), far, dot(residual, left)]

    both = zip(half(residuals[0], pieces[:5]), half(residuals[1], pieces[5:]))
    for j, (near, other) in enumerate(both):
        lane = pl.ds(j * SHARE, SHARE)
        piece = (near + other - wide_ref[1:2, lane] * sums).astype(bf16)
        for y in range(4):
            out_ref[y, :, lane] = piece
    if extra_ref is not None:
        for y in range(4):
            out_ref[y, :, NS:] = extra_ref[...]


def first_kernel(residual_ref, other_ref, wide_ref, *refs):
    send_gradient([residual_ref[...], other_ref[...]], wide_ref, refs[:10], None, refs[10])


def first_sweep(residual, other, wide, pieces):
    return pl.pallas_call(
        first_kernel,
        in_specs=[WHOLE] * 13,
        out_specs=WHOLE,
        out_shape=jax.ShapeDtypeStruct((4, OWN, NS), bf16),
        compiler_params=ROOM,
        name="first_sweep",
    )(residual, other, wide, *pieces)


def settle_kernel(
    local_blocks, penalty_ref, step_ref, arrived_ref, scales_ref, extra_ref, column_ref, rows, sem
):
    core = lax.axis_index("core")
    place = lax.axis_index("x")
    slot = lax.axis_index("z") * 4 + lax.axis_index("y")
    for i in range(MBLK):
        block = jnp.minimum(slot * MBLK + i, local_blocks - 1) + place * local_blocks
        pltpu.make_async_copy(scales_ref.at[block], rows.at[i], sem).start()
    first = arrived_ref[0].astype(f32)
    for source in range(1, PARTS):
        first = first + arrived_ref[source].astype(f32)
    edge = MBLK * HALF
    totals = first[edge : edge + 1] + first[edge + 1 : edge + 2]
    row = lax.broadcasted_iota(jnp.int32, (HALF, BLOCK), 0)
    lane = lax.broadcasted_iota(jnp.int32, (HALF, BLOCK), 1)
    counts = jnp.sum(jnp.where(lane == row % FOLDS, totals, 0.0), axis=1, keepdims=True)
    limit = jnp.zeros((HALF, BLOCK), f32)
    for q in range(HALF // FOLDS):
        limit = jnp.where(row // FOLDS == q, penalty_ref[core * (HALF // FOLDS) + q], limit)
    pltpu.make_async_copy(scales_ref.at[pl.ds(0, MBLK)], rows, sem).wait()
    few = lax.broadcasted_iota(jnp.int32, (OWN, BLOCK), 0)
    for i in range(MBLK):
        kkt = rows[i] * first[i * HALF : (i + 1) * HALF] / counts
        peak = jnp.max(jnp.abs(kkt) / limit, axis=0, keepdims=True)
        high = peak.astype(bf16).astype(f32)
        both = jnp.where(few == 0, high, jnp.where(few == 1, peak - high, 0.0))
        extra_ref[:, i * BLOCK : (i + 1) * BLOCK] = both.astype(bf16)
    step = jnp.zeros((OWN, BLOCK), f32)
    for j in range(OWN):
        step = jnp.where(few == j, step_ref[core * HALF + place * OWN + j], step)
    threshold = step * penalty_ref[core * (HALF // FOLDS) + place]
    few_lane = lane[:OWN]
    column_ref[...] = jnp.where(
        few_lane == 0, step, jnp.where(few_lane == 1, threshold, counts[:OWN])
    )


def settle(local_blocks, penalty, step_size, arrived, scales):
    small = pl.BlockSpec(memory_space=pltpu.SMEM)
    return pl.pallas_call(
        functools.partial(settle_kernel, local_blocks),
        in_specs=[small, small, WHOLE, pl.BlockSpec(memory_space=pltpu.HBM)],
        out_specs=[WHOLE] * 2,
        out_shape=[
            jax.ShapeDtypeStruct((OWN, PEAK), bf16),
            jax.ShapeDtypeStruct((OWN, BLOCK), f32),
        ],
        scratch_shapes=[pltpu.VMEM((MBLK, 1, BLOCK), f32), pltpu.SemaphoreType.DMA],
        compiler_params=ROOM,
        name="settle",
    )(penalty, step_size, arrived, scales)


def middle_kernel(got_ref, out_ref):
    total = got_ref[0, :, :NS].astype(f32)
    for y in range(1, 4):
        total = total + got_ref[y, :, :NS].astype(f32)
    total = total.astype(bf16)
    for z in range(8):
        out_ref[z, :, :NS] = total
        if got_ref.shape[2] > NS:
            for y in range(4):
                out_ref[z, :, NS + y * PEAK : NS + (y + 1) * PEAK] = got_ref[y, :, NS:]


def middle(got):
    width = NS + 4 * (got.shape[2] - NS)
    return pl.pallas_call(
        middle_kernel,
        in_specs=[WHOLE],
        out_specs=WHOLE,
        out_shape=jax.ShapeDtypeStruct((8, OWN, width), bf16),
        compiler_params=ROOM,
        name="middle",
    )(got)


def prox(got_ref, state_ref, wide_ref, column_ref, factor):
    total = got_ref[0, :, :NS].astype(f32)
    for z in range(1, 8):
        total = total + got_ref[z, :, :NS].astype(f32)
    step, threshold, counts = (column_ref[:, i : i + 1] for i in range(3))
    moved = state_ref[:OWN] + step * (wide_ref[0:1] * total / counts)
    current = moved - jnp.clip(moved, -threshold, threshold)
    return current + factor * (current - state_ref[OWN:]), current


def sweep_kernel(factor, has_extra, *refs):
    got_ref, state_ref, wide_ref, column_ref, samples_ref, other_ref = refs[:6]
    pieces = refs[6:16]
    extra_ref = refs[16] if has_extra else None
    out_ref, next_ref = refs[-2:]
    point, current = prox(got_ref, state_ref, wide_ref, column_ref, factor)
    next_ref[:OWN] = point
    next_ref[OWN:] = current
    weighted = wide_ref[0:1] * point
    shift = jnp.sum(wide_ref[1:2] * weighted, axis=1, keepdims=True)
    scaled = weighted.astype(bf16)

    def dot(turn, piece):
        return lax.dot_general(
            scaled[:, turn * SHARE : (turn + 1) * SHARE],
            piece[...],
            LAST,
            preferred_element_type=f32,
        )

    def half(ref, group):
        own, right, far_a, far_b, left = group
        far = jnp.concatenate([dot(2, far_a), dot(2, far_b)], axis=1)
        fitted = dot(0, own) + dot(1, right) + far + dot(3, left) - shift
        fold = lax.broadcasted_iota(jnp.int32, (OWN, ROWS), 0).astype(f32)
        weight = jnp.where(ref[1:2] != fold, 1.0, 0.0)
        return (weight * (ref[0:1] - fitted)).astype(bf16)

    residuals = [half(samples_ref, pieces[:5]), half(other_ref, pieces[5:])]
    send_gradient(residuals, wide_ref, pieces, extra_ref, out_ref)


def sweep(factor, extra, *operands):
    width = NS if extra is None else NS + PEAK
    more = () if extra is None else (extra,)
    return pl.pallas_call(
        functools.partial(sweep_kernel, factor, extra is not None),
        in_specs=[WHOLE] * (len(operands) + len(more)),
        out_specs=[WHOLE] * 2,
        out_shape=[
            jax.ShapeDtypeStruct((4, OWN, width), bf16),
            jax.ShapeDtypeStruct((2 * OWN, NS), f32),
        ],
        compiler_params=ROOM,
        name="sweep",
    )(*operands, *more)


def last_kernel(got_ref, state_ref, wide_ref, column_ref, out_ref):
    current = prox(got_ref, state_ref, wide_ref, column_ref, 0.0)[1]
    for turn in range(4):
        piece = current[:, turn * SHARE : (turn + 1) * SHARE]
        spot = lax.rem(lax.axis_index("x") + turn, 4)
        out_ref[spot] = piece
        out_ref[spot + 4] = piece


def last(got, state, wide, columns):
    return pl.pallas_call(
        last_kernel,
        in_specs=[WHOLE] * 4,
        out_specs=WHOLE,
        out_shape=jax.ShapeDtypeStruct((8, OWN, SHARE), f32),
        compiler_params=ROOM,
        name="last",
    )(got, state, wide, columns)


def exchange(value, axis):
    return lax.all_to_all(value, axis, 0, 0, tiled=True)


def swap(value):
    return lax.ppermute(value, "core", [(0, 1), (1, 0)])


def onward(value):
    return lax.ppermute(value, "x", [(i, (i + 1) % 4) for i in range(4)])


def backward(value):
    return lax.ppermute(value, "x", [(i, (i + 3) % 4) for i in range(4)])


def turned(value, count, axis):
    twice = jnp.concatenate([value, value], axis=axis)
    return lax.dynamic_slice_in_dim(twice, count, value.shape[axis], axis)


def lanes(wide):
    return wide.reshape(wide.shape[0], -1, BLOCK).transpose(1, 0, 2)


def shards(
    dosage, centers, scales, phenotype, fold_ids, strong_blocks, warm_start, penalty, step_size
):
    rows, local_width = dosage.shape
    local_blocks = local_width // BLOCK
    core = lax.axis_index("core")
    place = lax.axis_index("x")
    first_fit = core * HALF + place * OWN
    other_fit = (1 - core) * HALF + place * OWN
    ahead = place * EACH

    warm = warm_start.T
    scale_rows = scales.reshape(-1, 1, BLOCK)
    own, right, far_a, far_b, left, fit_part, wide, local_centers, state = pick_blocks(
        strong_blocks, dosage, centers.reshape(-1, 1, BLOCK), scale_rows, warm
    )

    fit_part, phenotype, fold_ids = lax.optimization_barrier((fit_part, phenotype, fold_ids))
    samples = jnp.stack([phenotype, fold_ids.astype(f32)])
    samples_other = swap(samples)
    via_left = onward(far_a)
    via_right = backward(far_b)
    from_left = onward(right)
    from_right = backward(left)
    fitted = exchange(fit_part, "x")
    fitted, via_left, via_right = lax.optimization_barrier((fitted, via_left, via_right))
    far_a = onward(via_left)
    far_b = backward(via_right)

    fit_folds = (jnp.arange(FITS, dtype=jnp.int32) % FOLDS).astype(f32)
    weights = (samples[1:] != fit_folds[:, None]).astype(f32)
    fitted = jnp.sum(fitted.astype(f32), axis=0)
    residual = (weights * (samples[:1] - fitted)).astype(bf16)
    column_sums = jnp.sum(residual.astype(f32), axis=1, keepdims=True)
    residual_own = lax.dynamic_slice_in_dim(residual, first_fit, OWN, 0)
    residual_other = swap(lax.dynamic_slice_in_dim(residual, other_fit, OWN, 0))

    cross = jnp.dot(residual, dosage, preferred_element_type=f32) - (
        local_centers * column_sums
    )
    keep = lax.dynamic_slice_in_dim(cross, core * HALF, HALF, 0)
    give = lax.dynamic_slice_in_dim(cross, (1 - core) * HALF, HALF, 0)
    summed = (keep + swap(give.astype(bf16)).astype(f32)).astype(bf16)
    padded = jnp.concatenate(
        [lanes(summed), jnp.zeros((PARTS * MBLK - local_blocks, HALF, BLOCK), bf16)], axis=0
    ).reshape(PARTS, MBLK * HALF, BLOCK)
    near = jnp.concatenate([samples, samples_other], axis=1)
    near_weights = (near[1:] != fit_folds[:FOLDS, None]).astype(f32)
    tally_rows = jnp.zeros((8, BLOCK), f32)
    tally_rows = tally_rows.at[0, :FOLDS].set(jnp.sum(near_weights[:, :rows], axis=1))
    tally_rows = tally_rows.at[1, :FOLDS].set(jnp.sum(near_weights[:, rows:], axis=1))
    message = jnp.concatenate(
        [padded, jnp.broadcast_to(tally_rows.astype(bf16)[None], (PARTS, 8, BLOCK))], axis=1
    )
    owner = jnp.repeat(turned(strong_blocks, ahead, 0)[:EACH] // local_blocks, BLOCK)[None, :]
    share = jnp.where(owner == (place + 3) % 4, from_left, own)
    share = jnp.where(owner == (place + 1) % 4, from_right, share)
    share = jnp.where(
        owner == (place + 2) % 4, jnp.concatenate([far_a, far_b], axis=0), share
    )
    arrived = exchange(message, PLANE)
    share_left = onward(share)
    share_right = backward(share)
    share_other = swap(share)
    far_a = onward(share_left[:PART])
    far_b = backward(share_right[PART:])
    strong = [share, share_right, far_a, far_b, share_left]
    strong += [share_other] + [swap(piece) for piece in strong[1:]]
    strong = lax.optimization_barrier(tuple(strong))

    sent = first_sweep(residual_own, residual_other, wide, strong)
    sent, arrived = lax.optimization_barrier((sent, arrived))
    extra, columns = settle(local_blocks, penalty, step_size, arrived, scale_rows)

    got = exchange(middle(exchange(sent, "y")), "z")
    momentum = 1.0
    margin = None
    for round in range(1, ITERS):
        following = (1.0 + math.sqrt(1.0 + 4.0 * momentum * momentum)) / 2.0
        factor = (momentum - 1.0) / following
        sent, state = sweep(
            factor,
            extra if round == 1 else None,
            got,
            state,
            wide,
            columns,
            samples,
            samples_other,
            *strong,
        )
        got = exchange(middle(exchange(sent, "y")), "z")
        momentum = following
        if round == 1:
            peaks = got[:, :2, NS:].astype(f32)
            peaks = jnp.sum(peaks, axis=1).reshape(PARTS * PEAK)[:local_width]
            margin = jnp.maximum(peaks, swap(peaks))
    leaving = last(got, state, wide, columns)
    landed = exchange(leaving, ("core", "x"))
    return (margin, landed.reshape(FITS, SHARE).T)


def solution(mesh):
    cube = Mesh(mesh.devices.reshape(8, 4, 2, 4), ("z", "y", "core", "x"))
    samp = ("z", "y", "core")
    return jax.shard_map(
        shards,
        mesh=cube,
        in_specs=(P(samp, "x"), P(), P(), P(samp), P(samp), P(), P(), P(), P()),
        out_specs=(P("x"), P("x", None)),
        check_vma=False,
    )
```

time: 177 us -> 172 us (0.972)
  blocking collectives: 27.4 us -> 37.2 us
  local copies, waits for them, and re-layouts: 19.5 us -> 13.2 us
  other arithmetic: 11.1 us -> 5.76 us
  starting transfers between devices: 69.8 us -> 67.9 us
    all_to_all x3 -> x4, blocking collectives: 27.4 us -> 37.2 us  [exchange(): return lax.all_to_all(value, axis, 0, 0, tiled=True)]
    all_to_all x6 -> x5, waiting for transfers between devices: 18.5 us -> 13.9 us  [exchange(): return lax.all_to_all(value, axis, 0, 0, tiled=True)]
    ppermute x5, waiting for transfers between devices: 10 us -> 13 us  [onward(): return lax.ppermute(value, 'x', [(i, (i + 1) % 4) for i in range(4)])]
    dynamic_slice x5 -> x1, local copies, waits for them, and re-layouts: 2.72 us -> 0.01 us  [shards(): residual_other = swap(lax.dynamic_slice_in_dim(residual, other_fit, OWN, 0))]
    unnamed x42 -> x36, local copies, waits for them, and re-layouts: 8.57 us -> 11.2 us
    concatenate x5 -> x0, other arithmetic: 2.17 us -> none  [the longest x1 0.76 us: shards(): columns = jnp.concatenate([step, threshold, counts], axis=1)]
    broadcast_in_dim x4 -> x0, local copies, waits for them, and re-layouts: 2.04 us -> none  [the longest x1 1.31 us: shards(): counts = (first[edge] + first[edge + 1])[:FOLDS, None]]
    all_to_all x6 -> x5, starting transfers between devices: 39.5 us -> 37.9 us  [exchange(): return lax.all_to_all(value, axis, 0, 0, tiled=True)]
  transfers between devices with their start and end apart: 25 -> 24, of which waited for: 8 -> 8; matrix products, arithmetic and copies ran while one was open for 13% -> 6% of each run, Pallas kernels for 2% -> 2%
where the time goes in v5:
time: 172 us; the launch traced here: 171 us
  starting transfers between devices  67.9 us (39%)
  blocking collectives  37.2 us (22%)
  waiting for transfers between devices  28.1 us (16%)
  Pallas kernels  14.1 us (8%)
  local copies, waits for them, and re-layouts  13.2 us (8%)
  other arithmetic  5.76 us (3%)
  matrix products  3.5 us (2%)
    all_to_all x5, starting transfers between devices, exchange(): return lax.all_to_all(value, axis, 0, 0, tiled=True)  37.9 us
    all_to_all x4, blocking collectives, exchange(): return lax.all_to_all(value, axis, 0, 0, tiled=True)  37.2 us
    ppermute x9, starting transfers between devices, swap(): return lax.ppermute(value, 'core', [(0, 1), (1, 0)])  17.2 us
    all_to_all x5, waiting for transfers between devices, exchange(): return lax.all_to_all(value, axis, 0, 0, tiled=True)  13.9 us
    ppermute x5, waiting for transfers between devices, onward(): return lax.ppermute(value, 'x', [(i, (i + 1) % 4) for i in range(4)])  13 us
    unnamed x36, local copies, waits for them, and re-layouts  11.2 us
    ppermute x5, starting transfers between devices, backward(): return lax.ppermute(value, 'x', [(i, (i + 3) % 4) for i in range(4)])  10.4 us
    pallas_call x2, Pallas kernels, sweep(): pl.pallas_call(functools.partial(sweep_kernel, factor, extra is not None)...  6.19 us
  transfers between devices with their start and end apart: 24, of which 8 were waited for; matrix products, arithmetic and copies ran while one was open for 6% of the time, Pallas kernels for 2%

profile of v5, /device:TPU:1, one launch (start us, length us, event | category | flops | bytes accessed | tf_op | source)
XLA Modules:
  0.0 170.6 jit_solution(15178547107530306831)
XLA Ops:
  0.6 2.5 %copy-done = bf16[256,10240]{1,0:T(8,128)(2,1)S(1)} copy-done((bf16[256,10240]{1,0:T(8,128)(2,1)S(1)}, bf16[256,10240]{1,0:T(8,128)(2,1)}, u32[]{:S(2)}) %copy-start) | copy-done | bytes 5242904
  6.7 3.3 %pick_blocks.1 = (bf16[256,1024]{1,0:T(8,128)(2,1)S(1)}, bf16[256,1024]{1,0:T(8,128)(2,1)S(1)}, bf16[128,1024]{1,0:T(8,128)(2,1)S(1)}, bf16[128,1024]{1,0:T(8,12...) custom-call(s32[32]{0:T(128)S(1)} %copy-done.12, ...), custom_call_target="tpu_custom_call" | custom-call | tf_op jit(solution)/shard_map/pick_blocks/pallas_call | solution.py:135
  10.6 4.8 %all-to-all-start = ((bf16[4,32,256]{2,1,0:T(8,128)(2,1)}), bf16[4,32,256]{2,1,0:T(8,128)(2,1)S(1)}, u32[]{:S(2)}, u32[]{:S(2)}) async-start(bf16[4,32,256]{2,1,0:T(8,128)(2,1)} %get-tuple-element.62), calls=%async_computation | async-start | bytes 131072 | tf_op jit(solution)/shard_map/all_to_all | solution.py:357
  15.5 1.5 collective-permute-start
  16.9 1.2 collective-permute-start.1
  18.2 2.4 %collective-permute-start.17 = (f32[2,256]{1,0:T(2,128)S(1)}, f32[2,256]{1,0:T(2,128)S(1)}, u32[]{:S(2)}, u32[]{:S(2)}) collective-permute-start(f32[2,256]{1,0:T(2,128)S(1)} %pad_maximum_fusion.3.refs_4_), channel_id=1, source_target_pairs={{0,4},{4,0},{1,5},{5,1},{2,6},{6,2},{3,7},{7,3},{8,12},{12,8},{9,1... | collective-permute-start | bytes 6152 | tf_op jit(solution)/shard_map/ppermute | solution.py:361
  20.6 1.6 collective-permute-start.5
  22.6 1.5 collective-permute-done
  24.9 2.2 %collective-permute-start.4 = (bf16[128,1024]{1,0:T(8,128)(2,1)}, bf16[128,1024]{1,0:T(8,128)(2,1)}, u32[]{:S(2)}, u32[]{:S(2)}) collective-permute-start(bf16[128,1024]{1,0:T(8,128)(2,1)} %collective-permute-done.1), channel_id=1, source_target_pairs={{0,3},{1,0},{2,1},{3,2},{4,7},{5,4},{6,5},{7,6},{8,11},{9,8},{10,9... | collective-permute-start | bytes 786440 | tf_op jit(solution)/shard_map/ppermute | solution.py:369
  27.0 3.5 %convolution_subtract_fusion = f32[32,10240]{1,0:T(8,128)S(1)} fusion(bf16[32,256]{1,0:T(8,128)(2,1)S(1)} %get-tuple-element.95, bf16[256,10240]{1,0:T(8,128)(2,1)} %source_ref.1, f32[32]{0:T(128)S(1)} %get-tuple-element.94, f32[10240]{0:T(1024)S(1)} %bitcast.31), kind=kOutput, calls=%fused_computation | convolution fusion | flops 168427520 | bytes 6611072 | tf_op jit(solution)/shard_map/dot_general | solution.py:418
  31.3 4.9 %collective-permute-start.16 = (bf16[16,10240]{1,0:T(8,128)(2,1)}, bf16[16,10240]{1,0:T(8,128)(2,1)}, u32[]{:S(2)}, u32[]{:S(2)}) collective-permute-start(bf16[16,10240]{1,0:T(8,128)(2,1)} %dynamic-slice_convert_fusion), channel_id=1, source_target_pairs={{0,4},{4,0},{1,5},{5,1},{2,6},{6,2},{3,7},{7,3},{8,12},{12,8},{9,1... | collective-permute-start | bytes 983048 | tf_op jit(solution)/shard_map/ppermute | solution.py:361
  36.5 5.6 %collective-permute-done.3 = bf16[128,1024]{1,0:T(8,128)(2,1)S(1)} collective-permute-done((bf16[128,1024]{1,0:T(8,128)(2,1)}, bf16[128,1024]{1,0:T(8,128)(2,1)S(1)}, u32[]{:S(2)}, u32[]{:S(2)}) %collective-permute-start.3) | collective-permute-done | bytes 262176 | tf_op jit(solution)/shard_map/ppermute | solution.py:365
  42.8 1.7 %maximum_select_fusion.refs_0_.refs_6_ = bf16[256,1024]{1,0:T(8,128)(2,1)S(1)} fusion(bf16[128,1024]{1,0:T(8,128)(2,1)} %collective-permute-done.4, bf16[128,1024]{1,0:T(8,128)(2,1)} %copy-done.15, bf16[256,1024]{1,0:T(8,128)(2,1)} %collective-permute-done.5, bf16[256,1024]{1,0:T(8,128)(2,1)} %collective-permute-done.6, ...), kind=kLoop, calls=%fused_computation.3 | loop fusion | flops 1835008 | bytes 2624512 | tf_op jit(solution)/shard_map/jit(_where)/select_n | solution.py:438
  44.7 2.7 %collective-permute-start.7 = (bf16[256,1024]{1,0:T(8,128)(2,1)S(1)}, bf16[256,1024]{1,0:T(8,128)(2,1)S(1)}, u32[]{:S(2)}, u32[]{:S(2)}) collective-permute-start(bf16[256,1024]{1,0:T(8,128)(2,1)S(1)} %maximum_select_fusion.refs_0_.refs_6_), channel_id=1, source_target_pairs={{0,3},{1,0},{2,1},{3,2},{4,7},{5,4},{6,5},{7,6},{8,11},{9,8},{10,9... | collective-permute-start | bytes 1572872 | tf_op jit(solution)/shard_map/ppermute | solution.py:369
  49.3 11.5 %all-to-all-start.1 = ((bf16[32,56,128]{2,1,0:T(8,128)(2,1)}), bf16[32,56,128]{2,1,0:T(8,128)(2,1)}, u32[]{:S(2)}, u32[]{:S(2)}) async-start(bf16[32,56,128]{2,1,0:T(8,128)(2,1)} %pad_maximum_fusion), calls=%async_computation.1 | async-start | bytes 917504 | tf_op jit(solution)/shard_map/all_to_all | solution.py:357
  60.7 1.8 %collective-permute-start.11 = (bf16[256,1024]{1,0:T(8,128)(2,1)S(1)}, bf16[256,1024]{1,0:T(8,128)(2,1)S(1)}, u32[]{:S(2)}, u32[]{:S(2)}) collective-permute-start(bf16[256,1024]{1,0:T(8,128)(2,1)S(1)} %maximum_select_fusion.refs_0_.refs_6_), channel_id=1, source_target_pairs={{0,4},{4,0},{1,5},{5,1},{2,6},{6,2},{3,7},{7,3},{8,12},{12,8},{9,1... | collective-permute-start | bytes 1572872 | tf_op jit(solution)/shard_map/ppermute | solution.py:361
  63.5 2.6 %collective-permute-start.10 = (bf16[128,1024]{1,0:T(8,128)(2,1)S(1)}, bf16[128,1024]{1,0:T(8,128)(2,1)}, u32[]{:S(2)}, u32[]{:S(2)}) collective-permute-start(bf16[128,1024]{1,0:T(8,128)(2,1)S(1)} %slice.72), channel_id=1, source_target_pairs={{0,3},{1,0},{2,1},{3,2},{4,7},{5,4},{6,5},{7,6},{8,11},{9,8},{10,9... | collective-permute-start | bytes 786440 | tf_op jit(solution)/shard_map/ppermute | solution.py:369
  66.1 5.9 %collective-permute-done.9.refs_2_.refs_8_ = bf16[128,1024]{1,0:T(8,128)(2,1)S(1)} collective-permute-done((bf16[128,1024]{1,0:T(8,128)(2,1)S(1)}, bf16[128,1024]{1,0:T(8,128)(2,1)S(1)}, u32[]{:S(2)}, u32[]{:S(2)}) %collective-permute-start.9) | collective-permute-done | bytes 262176 | tf_op jit(solution)/shard_map/ppermute | solution.py:365
  74.7 1.8 %first_sweep.1 = bf16[4,4,4096]{2,1,0:T(4,128)(2,1)S(1)} custom-call(bf16[4,256]{1,0:T(4,128)(2,1)S(1)} %get-tuple-element.99.residual_ref, bf16[4,256]{1,0:T(4,128)(2,1)S(1)} %collective-permute-done.2.other_ref, f32[2,4096]{1,0:T(2,128)S(1)} %get-tuple-element.66.wide_ref.refs_2_, bf16[256,1024]{1,0:T(8,128)(2,1)S(1)} %maximum_select_fusion.refs_0_.refs_6_, ...), custom_call_target="tpu_custom_call" | custom-call | tf_op jit(solution)/shard_map/first_sweep/pallas_call | solution.py:190
  77.1 9.1 %all_to_all.45.got_ref = bf16[4,4,4096]{2,1,0:T(4,128)(2,1)S(1)} all-to-all(bf16[4,4,4096]{2,1,0:T(4,128)(2,1)} %copy-done.6), channel_id=1, replica_groups=mesh['z'=8,'y'=4,'core'=2,'x'=4] {'y'}, dimensions={0} | all-to-all | bytes 262144 | tf_op jit(solution)/shard_map/all_to_all | solution.py:357
  86.9 6.4 %all-to-all-start.3 = ((bf16[8,4,4096]{2,1,0:T(4,128)(2,1)}), bf16[8,4,4096]{2,1,0:T(4,128)(2,1)}, u32[]{:S(2)}, u32[]{:S(2)}) async-start(bf16[8,4,4096]{2,1,0:T(4,128)(2,1)} %copy-done.2), calls=%async_computation.3 | async-start | bytes 524288 | tf_op jit(solution)/shard_map/all_to_all | solution.py:357
  95.4 7.3 %all-to-all-done.3.refs_0_ = bf16[8,4,4096]{2,1,0:T(4,128)(2,1)} async-done(((bf16[8,4,4096]{2,1,0:T(4,128)(2,1)}), bf16[8,4,4096]{2,1,0:T(4,128)(2,1)}, u32[]{:S(2)}, u32[]{:S(2)}) %all-to-all-start.3) | async-done | bytes 262176 | tf_op jit(solution)/shard_map/all_to_all | solution.py:357
  103.6 3.1 %sweep.2 = (bf16[4,4,4480]{2,1,0:T(4,128)(2,1)S(1)}, f32[8,4096]{1,0:T(8,128)S(1)}) custom-call(bf16[8,4,4096]{2,1,0:T(4,128)(2,1)} %all-to-all-done.3.refs_0_, f32[8,4096]{1,0:T(8,128)S(1)} %copy-done.9, f32[2,4096]{1,0:T(2,128)S(1)} %get-tuple-element.66.wide_ref.refs_2_, f32[4,128]{1,0:T(4,128)S(1)} %get-tuple-element.86.refs_3_.column_ref, ...), custom_call_target="tpu_custom_call" | custom-call | tf_op jit(solution)/shard_map/sweep/pallas_call | solution.py:323
  106.7 7.4 %all_to_all.46.got_ref = bf16[4,4,4480]{2,1,0:T(4,128)(2,1)S(1)} all-to-all(bf16[4,4,4480]{2,1,0:T(4,128)(2,1)S(1)} %get-tuple-element.88), channel_id=1, replica_groups=mesh['z'=8,'y'=4,'core'=2,'x'=4] {'y'}, dimensions={0} | all-to-all | bytes 286720 | tf_op jit(solution)/shard_map/all_to_all | solution.py:357
  114.2 13.4 %all_to_all.47.refs_0_ = bf16[8,4,5632]{2,1,0:T(4,128)(2,1)S(1)} all-to-all(bf16[8,4,5632]{2,1,0:T(4,128)(2,1)S(1)} %middle.4), channel_id=1, replica_groups=mesh['z'=8,'y'=4,'core'=2,'x'=4] {'z'}, dimensions={0} | all-to-all | bytes 720896 | tf_op jit(solution)/shard_map/all_to_all | solution.py:357
  127.6 3.1 %sweep.3 = (bf16[4,4,4096]{2,1,0:T(4,128)(2,1)S(1)}, f32[8,4096]{1,0:T(8,128)S(1)}) custom-call(bf16[8,4,5632]{2,1,0:T(4,128)(2,1)S(1)} %all_to_all.47.refs_0_, f32[8,4096]{1,0:T(8,128)S(1)} %get-tuple-element.89.refs_1_, f32[2,4096]{1,0:T(2,128)S(1)} %get-tuple-element.66.wide_ref.refs_2_, f32[4,128]{1,0:T(4,128)S(1)} %get-tuple-element.86.refs_3_.column_ref, ...), custom_call_target="tpu_custom_call" | custom-call | tf_op jit(solution)/shard_map/sweep/pallas_call | solution.py:323
  131.4 7.3 %all_to_all.48.got_ref = bf16[4,4,4096]{2,1,0:T(4,128)(2,1)S(1)} all-to-all(bf16[4,4,4096]{2,1,0:T(4,128)(2,1)S(1)} %get-tuple-element.90), channel_id=1, replica_groups=mesh['z'=8,'y'=4,'core'=2,'x'=4] {'y'}, dimensions={0} | all-to-all | bytes 262144 | tf_op jit(solution)/shard_map/all_to_all | solution.py:357
  139.5 3.4 %all-to-all-start.7 = ((bf16[8,4,4096]{2,1,0:T(4,128)(2,1)}), bf16[8,4,4096]{2,1,0:T(4,128)(2,1)S(1)}, u32[]{:S(2)}, u32[]{:S(2)}) async-start(bf16[8,4,4096]{2,1,0:T(4,128)(2,1)} %middle.5), calls=%async_computation.7 | async-start | bytes 524288 | tf_op jit(solution)/shard_map/all_to_all | solution.py:357
  143.9 6.2 %collective-permute-start.18 = (f32[10240]{0:T(1024)S(1)}, f32[10240]{0:T(1024)S(1)}, u32[]{:S(2)}, u32[]{:S(2)}) collective-permute-start(f32[10240]{0:T(1024)S(1)} %slice.76), channel_id=1, source_target_pairs={{0,4},{4,0},{1,5},{5,1},{2,6},{6,2},{3,7},{7,3},{8,12},{12,8},{9,1... | collective-permute-start | bytes 122888 | tf_op jit(solution)/shard_map/ppermute | solution.py:361
  150.1 2.0 %all-to-all-done.7.got_ref = bf16[8,4,4096]{2,1,0:T(4,128)(2,1)S(1)} async-done(((bf16[8,4,4096]{2,1,0:T(4,128)(2,1)}), bf16[8,4,4096]{2,1,0:T(4,128)(2,1)S(1)}, u32[]{:S(2)}, u32[]{:S(2)}) %all-to-all-start.7) | async-done | bytes 262176 | tf_op jit(solution)/shard_map/all_to_all | solution.py:357
  152.9 11.8 %all-to-all-start.8 = ((f32[8,4,1024]{2,1,0:T(4,128)}), f32[8,4,1024]{2,1,0:T(4,128)S(1)}, u32[]{:S(2)}, u32[]{:S(2)}) async-start(f32[8,4,1024]{2,1,0:T(4,128)} %last.1), calls=%async_computation.8 | async-start | bytes 262144 | tf_op jit(solution)/shard_map/all_to_all | solution.py:357
  165.3 4.6 %all-to-all-done.8 = f32[8,4,1024]{2,1,0:T(4,128)S(1)} async-done(((f32[8,4,1024]{2,1,0:T(4,128)}), f32[8,4,1024]{2,1,0:T(4,128)S(1)}, u32[]{:S(2)}, u32[]{:S(2)}) %all-to-all-start.8) | async-done | bytes 131104 | tf_op jit(solution)/shard_map/all_to_all | solution.py:357
  (96 shorter events, 21.7 us)
Async XLA Ops:
  0.6 2.5 %copy-start = (bf16[256,10240]{1,0:T(8,128)(2,1)S(1)}, bf16[256,10240]{1,0:T(8,128)(2,1)}, u32[]{:S(2)}) copy-start(bf16[256,10240]{1,0:T(8,128)(2,1)} %source_ref.1) | copy-start | bytes 15728644
  4.0 1.0 copy-start.5
  6.7 11.5 %copy-start.17 = (s32[256]{0:T(256)S(1)}, s32[256]{0:T(256)}, u32[]{:S(2)}) copy-start(s32[256]{0:T(256)} %param.17) | copy-start | bytes 3076
  6.7 11.5 %copy-start.16 = (f32[256]{0:T(256)S(1)}, f32[256]{0:T(256)}, u32[]{:S(2)}) copy-start(f32[256]{0:T(256)} %param.16) | copy-start | bytes 3076
  10.6 12.0 %all-to-all-start = ((bf16[4,32,256]{2,1,0:T(8,128)(2,1)}), bf16[4,32,256]{2,1,0:T(8,128)(2,1)S(1)}, u32[]{:S(2)}, u32[]{:S(2)}) async-start(bf16[4,32,256]{2,1,0:T(8,128)(2,1)} %get-tuple-element.62), calls=%async_computation | async-start | bytes 131072 | tf_op jit(solution)/shard_map/all_to_all | solution.py:357
  15.5 8.6 %collective-permute-start = (bf16[128,1024]{1,0:T(8,128)(2,1)S(1)}, bf16[128,1024]{1,0:T(8,128)(2,1)}, u32[]{:S(2)}, u32[]{:S(2)}) collective-permute-start(bf16[128,1024]{1,0:T(8,128)(2,1)S(1)} %get-tuple-element.63), channel_id=1, source_target_pairs={{0,1},{1,2},{2,3},{3,0},{4,5},{5,6},{6,7},{7,4},{8,9},{9,10},{10,1... | collective-permute-start | bytes 786440 | tf_op jit(solution)/shard_map/ppermute | solution.py:365
  16.9 7.2 %collective-permute-start.1 = (bf16[128,1024]{1,0:T(8,128)(2,1)S(1)}, bf16[128,1024]{1,0:T(8,128)(2,1)}, u32[]{:S(2)}, u32[]{:S(2)}) collective-permute-start(bf16[128,1024]{1,0:T(8,128)(2,1)S(1)} %get-tuple-element.64), channel_id=1, source_target_pairs={{0,3},{1,0},{2,1},{3,2},{4,7},{5,4},{6,5},{7,6},{8,11},{9,8},{10,9... | collective-permute-start | bytes 786440 | tf_op jit(solution)/shard_map/ppermute | solution.py:369
  18.2 4.3 %collective-permute-start.17 = (f32[2,256]{1,0:T(2,128)S(1)}, f32[2,256]{1,0:T(2,128)S(1)}, u32[]{:S(2)}, u32[]{:S(2)}) collective-permute-start(f32[2,256]{1,0:T(2,128)S(1)} %pad_maximum_fusion.3.refs_4_), channel_id=1, source_target_pairs={{0,4},{4,0},{1,5},{5,1},{2,6},{6,2},{3,7},{7,3},{8,12},{12,8},{9,1... | collective-permute-start | bytes 6152 | tf_op jit(solution)/shard_map/ppermute | solution.py:361
  20.6 21.6 %collective-permute-start.5 = (bf16[256,1024]{1,0:T(8,128)(2,1)S(1)}, bf16[256,1024]{1,0:T(8,128)(2,1)}, u32[]{:S(2)}, u32[]{:S(2)}) collective-permute-start(bf16[256,1024]{1,0:T(8,128)(2,1)S(1)} %get-tuple-element.69), channel_id=1, source_target_pairs={{0,3},{1,0},{2,1},{3,2},{4,7},{5,4},{6,5},{7,6},{8,11},{9,8},{10,9... | collective-permute-start | bytes 1572872 | tf_op jit(solution)/shard_map/ppermute | solution.py:369
  22.2 20.0 %collective-permute-start.6 = (bf16[256,1024]{1,0:T(8,128)(2,1)S(1)}, bf16[256,1024]{1,0:T(8,128)(2,1)}, u32[]{:S(2)}, u32[]{:S(2)}) collective-permute-start(bf16[256,1024]{1,0:T(8,128)(2,1)S(1)} %get-tuple-element.70), channel_id=1, source_target_pairs={{0,1},{1,2},{2,3},{3,0},{4,5},{5,6},{6,7},{7,4},{8,9},{9,10},{10,1... | collective-permute-start | bytes 1572872 | tf_op jit(solution)/shard_map/ppermute | solution.py:365
  24.3 17.8 %collective-permute-start.3 = (bf16[128,1024]{1,0:T(8,128)(2,1)}, bf16[128,1024]{1,0:T(8,128)(2,1)S(1)}, u32[]{:S(2)}, u32[]{:S(2)}) collective-permute-start(bf16[128,1024]{1,0:T(8,128)(2,1)} %collective-permute-done), channel_id=1, source_target_pairs={{0,1},{1,2},{2,3},{3,0},{4,5},{5,6},{6,7},{7,4},{8,9},{9,10},{10,1... | collective-permute-start | bytes 786440 | tf_op jit(solution)/shard_map/ppermute | solution.py:365
  24.9 17.3 %collective-permute-start.4 = (bf16[128,1024]{1,0:T(8,128)(2,1)}, bf16[128,1024]{1,0:T(8,128)(2,1)}, u32[]{:S(2)}, u32[]{:S(2)}) collective-permute-start(bf16[128,1024]{1,0:T(8,128)(2,1)} %collective-permute-done.1), channel_id=1, source_target_pairs={{0,3},{1,0},{2,1},{3,2},{4,7},{5,4},{6,5},{7,6},{8,11},{9,8},{10,9... | collective-permute-start | bytes 786440 | tf_op jit(solution)/shard_map/ppermute | solution.py:369
  31.3 16.0 %collective-permute-start.16 = (bf16[16,10240]{1,0:T(8,128)(2,1)}, bf16[16,10240]{1,0:T(8,128)(2,1)}, u32[]{:S(2)}, u32[]{:S(2)}) collective-permute-start(bf16[16,10240]{1,0:T(8,128)(2,1)} %dynamic-slice_convert_fusion), channel_id=1, source_target_pairs={{0,4},{4,0},{1,5},{5,1},{2,6},{6,2},{3,7},{7,3},{8,12},{12,8},{9,1... | collective-permute-start | bytes 983048 | tf_op jit(solution)/shard_map/ppermute | solution.py:361
  44.6 18.0 %collective-permute-start.8 = (bf16[256,1024]{1,0:T(8,128)(2,1)S(1)}, bf16[256,1024]{1,0:T(8,128)(2,1)S(1)}, u32[]{:S(2)}, u32[]{:S(2)}) collective-permute-start(bf16[256,1024]{1,0:T(8,128)(2,1)S(1)} %maximum_select_fusion.refs_0_.refs_6_), channel_id=1, source_target_pairs={{0,1},{1,2},{2,3},{3,0},{4,5},{5,6},{6,7},{7,4},{8,9},{9,10},{10,1... | collective-permute-start | bytes 1572872 | tf_op jit(solution)/shard_map/ppermute | solution.py:365
  44.7 18.2 %collective-permute-start.7 = (bf16[256,1024]{1,0:T(8,128)(2,1)S(1)}, bf16[256,1024]{1,0:T(8,128)(2,1)S(1)}, u32[]{:S(2)}, u32[]{:S(2)}) collective-permute-start(bf16[256,1024]{1,0:T(8,128)(2,1)S(1)} %maximum_select_fusion.refs_0_.refs_6_), channel_id=1, source_target_pairs={{0,3},{1,0},{2,1},{3,2},{4,7},{5,4},{6,5},{7,6},{8,11},{9,8},{10,9... | collective-permute-start | bytes 1572872 | tf_op jit(solution)/shard_map/ppermute | solution.py:369
  49.3 27.9 %all-to-all-start.1 = ((bf16[32,56,128]{2,1,0:T(8,128)(2,1)}), bf16[32,56,128]{2,1,0:T(8,128)(2,1)}, u32[]{:S(2)}, u32[]{:S(2)}) async-start(bf16[32,56,128]{2,1,0:T(8,128)(2,1)} %pad_maximum_fusion), calls=%async_computation.1 | async-start | bytes 917504 | tf_op jit(solution)/shard_map/all_to_all | solution.py:357
  60.7 12.0 %collective-permute-start.11 = (bf16[256,1024]{1,0:T(8,128)(2,1)S(1)}, bf16[256,1024]{1,0:T(8,128)(2,1)S(1)}, u32[]{:S(2)}, u32[]{:S(2)}) collective-permute-start(bf16[256,1024]{1,0:T(8,128)(2,1)S(1)} %maximum_select_fusion.refs_0_.refs_6_), channel_id=1, source_target_pairs={{0,4},{4,0},{1,5},{5,1},{2,6},{6,2},{3,7},{7,3},{8,12},{12,8},{9,1... | collective-permute-start | bytes 1572872 | tf_op jit(solution)/shard_map/ppermute | solution.py:361
  62.6 9.4 %collective-permute-start.9 = (bf16[128,1024]{1,0:T(8,128)(2,1)S(1)}, bf16[128,1024]{1,0:T(8,128)(2,1)S(1)}, u32[]{:S(2)}, u32[]{:S(2)}) collective-permute-start(bf16[128,1024]{1,0:T(8,128)(2,1)S(1)} %slice.71), channel_id=1, source_target_pairs={{0,1},{1,2},{2,3},{3,0},{4,5},{5,6},{6,7},{7,4},{8,9},{9,10},{10,1... | collective-permute-start | bytes 786440 | tf_op jit(solution)/shard_map/ppermute | solution.py:365
  62.9 10.5 %collective-permute-start.12 = (bf16[256,1024]{1,0:T(8,128)(2,1)S(1)}, bf16[256,1024]{1,0:T(8,128)(2,1)S(1)}, u32[]{:S(2)}, u32[]{:S(2)}) collective-permute-start(bf16[256,1024]{1,0:T(8,128)(2,1)S(1)} %collective-permute-done.7.refs_1_.refs_7_), channel_id=1, source_target_pairs={{0,4},{4,0},{1,5},{5,1},{2,6},{6,2},{3,7},{7,3},{8,12},{12,8},{9,1... | collective-permute-start | bytes 1572872 | tf_op jit(solution)/shard_map/ppermute | solution.py:361
  63.0 10.4 %collective-permute-start.15 = (bf16[256,1024]{1,0:T(8,128)(2,1)S(1)}, bf16[256,1024]{1,0:T(8,128)(2,1)S(1)}, u32[]{:S(2)}, u32[]{:S(2)}) collective-permute-start(bf16[256,1024]{1,0:T(8,128)(2,1)S(1)} %collective-permute-done.8.refs_4_.refs_10_), channel_id=1, source_target_pairs={{0,4},{4,0},{1,5},{5,1},{2,6},{6,2},{3,7},{7,3},{8,12},{12,8},{9,1... | collective-permute-start | bytes 1572872 | tf_op jit(solution)/shard_map/ppermute | solution.py:361
  63.5 9.3 %collective-permute-start.10 = (bf16[128,1024]{1,0:T(8,128)(2,1)S(1)}, bf16[128,1024]{1,0:T(8,128)(2,1)}, u32[]{:S(2)}, u32[]{:S(2)}) collective-permute-start(bf16[128,1024]{1,0:T(8,128)(2,1)S(1)} %slice.72), channel_id=1, source_target_pairs={{0,3},{1,0},{2,1},{3,2},{4,7},{5,4},{6,5},{7,6},{8,11},{9,8},{10,9... | collective-permute-start | bytes 786440 | tf_op jit(solution)/shard_map/ppermute | solution.py:369
  72.0 2.1 %collective-permute-start.13 = (bf16[128,1024]{1,0:T(8,128)(2,1)S(1)}, bf16[128,1024]{1,0:T(8,128)(2,1)}, u32[]{:S(2)}, u32[]{:S(2)}) collective-permute-start(bf16[128,1024]{1,0:T(8,128)(2,1)S(1)} %collective-permute-done.9.refs_2_.refs_8_), channel_id=1, source_target_pairs={{0,4},{4,0},{1,5},{5,1},{2,6},{6,2},{3,7},{7,3},{8,12},{12,8},{9,1... | collective-permute-start | bytes 786440 | tf_op jit(solution)/shard_map/ppermute | solution.py:361
  72.8 1.9 %collective-permute-start.14 = (bf16[128,1024]{1,0:T(8,128)(2,1)}, bf16[128,1024]{1,0:T(8,128)(2,1)}, u32[]{:S(2)}, u32[]{:S(2)}) collective-permute-start(bf16[128,1024]{1,0:T(8,128)(2,1)} %collective-permute-done.10.refs_3_.refs_9_), channel_id=1, source_target_pairs={{0,4},{4,0},{1,5},{5,1},{2,6},{6,2},{3,7},{7,3},{8,12},{12,8},{9,1... | collective-permute-start | bytes 786440 | tf_op jit(solution)/shard_map/ppermute | solution.py:361
  72.8 1.9 %collective-permute-start.2 = (bf16[4,256]{1,0:T(4,128)(2,1)S(1)}, bf16[4,256]{1,0:T(4,128)(2,1)S(1)}, u32[]{:S(2)}, u32[]{:S(2)}) collective-permute-start(bf16[4,256]{1,0:T(4,128)(2,1)S(1)} %get-tuple-element.98), channel_id=1, source_target_pairs={{0,4},{4,0},{1,5},{5,1},{2,6},{6,2},{3,7},{7,3},{8,12},{12,8},{9,1... | collective-permute-start | bytes 6152 | tf_op jit(solution)/shard_map/ppermute | solution.py:361
  74.6 18.6 %copy-start.13 = (f32[8]{0:T(128)S(1)}, f32[8]{0:T(128)}, u32[]{:S(2)}) copy-start(f32[8]{0:T(128)} %penalty_ref.1) | copy-start | bytes 100
  74.6 18.6 %copy-start.14 = (f32[32]{0:T(128)S(1)}, f32[32]{0:T(128)}, u32[]{:S(2)}) copy-start(f32[32]{0:T(128)} %step_ref.1) | copy-start | bytes 388
  86.9 15.8 %all-to-all-start.3 = ((bf16[8,4,4096]{2,1,0:T(4,128)(2,1)}), bf16[8,4,4096]{2,1,0:T(4,128)(2,1)}, u32[]{:S(2)}, u32[]{:S(2)}) async-start(bf16[8,4,4096]{2,1,0:T(4,128)(2,1)} %copy-done.2), calls=%async_computation.3 | async-start | bytes 524288 | tf_op jit(solution)/shard_map/all_to_all | solution.py:357
  127.6 3.1 %copy-start.1 = (bf16[8,4,5632]{2,1,0:T(4,128)(2,1)}, bf16[8,4,5632]{2,1,0:T(4,128)(2,1)S(1)}, u32[]{:S(2)}) copy-start(bf16[8,4,5632]{2,1,0:T(4,128)(2,1)S(1)} %all_to_all.47.refs_0_) | copy-start | bytes 1081348
  131.4 20.7 %copy-start.11 = (f32[8,4096]{1,0:T(8,128)S(1)}, f32[8,4096]{1,0:T(8,128)}, u32[]{:S(2)}) copy-start(f32[8,4096]{1,0:T(8,128)} %copy-done.10) | copy-start | bytes 393220
  139.5 12.7 %all-to-all-start.7 = ((bf16[8,4,4096]{2,1,0:T(4,128)(2,1)}), bf16[8,4,4096]{2,1,0:T(4,128)(2,1)S(1)}, u32[]{:S(2)}, u32[]{:S(2)}) async-start(bf16[8,4,4096]{2,1,0:T(4,128)(2,1)} %middle.5), calls=%async_computation.7 | async-start | bytes 524288 | tf_op jit(solution)/shard_map/all_to_all | solution.py:357
  143.9 20.8 %collective-permute-start.18 = (f32[10240]{0:T(1024)S(1)}, f32[10240]{0:T(1024)S(1)}, u32[]{:S(2)}, u32[]{:S(2)}) collective-permute-start(f32[10240]{0:T(1024)S(1)} %slice.76), channel_id=1, source_target_pairs={{0,4},{4,0},{1,5},{5,1},{2,6},{6,2},{3,7},{7,3},{8,12},{12,8},{9,1... | collective-permute-start | bytes 122888 | tf_op jit(solution)/shard_map/ppermute | solution.py:361
  152.9 17.0 %all-to-all-start.8 = ((f32[8,4,1024]{2,1,0:T(4,128)}), f32[8,4,1024]{2,1,0:T(4,128)S(1)}, u32[]{:S(2)}, u32[]{:S(2)}) async-start(f32[8,4,1024]{2,1,0:T(4,128)} %last.1), calls=%async_computation.8 | async-start | bytes 262144 | tf_op jit(solution)/shard_map/all_to_all | solution.py:357
  (10 other events, 7.7 us)

commit v6 on v5

--- a/solution.py
+++ b/solution.py
@@ -8,6 +8,7 @@
 from jax.experimental.pallas import tpu as pltpu
 from jax.sharding import Mesh
 from jax.sharding import PartitionSpec as P
+
 
 BLOCK = 128
 SLOTS = 32
@@ -39,7 +40,7 @@
     source_ref,
     centers_ref,
     scales_ref,
-    warm_ref,
+    source_warm_ref,
     own,
     right,
     far_a,
@@ -53,12 +54,15 @@
     center_rows,
     local_rows,
     scaled_ref,
+    warm_ref,
     sem,
 ):
     place = lax.axis_index("x")
     local_blocks = source_ref.shape[1] // BLOCK
     slots = [lax.rem(place * EACH + r, SLOTS) for r in range(SLOTS)]
     blocks = [block_ref[slot] for slot in slots]
+    warm_copy = pltpu.make_async_copy(source_warm_ref, warm_ref, sem.at[8])
+    warm_copy.start()
     for r, block in enumerate(blocks):
         pltpu.make_async_copy(scales_ref.at[block], scale_rows.at[r], sem.at[0]).start()
         pltpu.make_async_copy(centers_ref.at[block], center_rows.at[r], sem.at[1]).start()
@@ -85,6 +89,7 @@
             ).start()
     pltpu.make_async_copy(scales_ref.at[pl.ds(0, SLOTS)], scale_rows, sem.at[0]).wait()
     pltpu.make_async_copy(centers_ref.at[pl.ds(0, SLOTS)], center_rows, sem.at[1]).wait()
+    warm_copy.wait()
     moments = jnp.zeros((FITS, BLOCK), f32)
     group = lax.axis_index("core") * (HALF // OWN) + place
     for r in range(SLOTS):
@@ -134,7 +139,7 @@
     far = pl.BlockSpec(memory_space=pltpu.HBM)
     return pl.pallas_call(
         pick_kernel,
-        in_specs=[pl.BlockSpec(memory_space=pltpu.SMEM), far, far, far, WHOLE],
+        in_specs=[pl.BlockSpec(memory_space=pltpu.SMEM), far, far, far, far],
         out_specs=[WHOLE] * 9,
         out_shape=[
             tall,
@@ -152,9 +157,9 @@
             pltpu.VMEM((SLOTS, 1, BLOCK), f32),
             pltpu.VMEM((dosage.shape[1] // BLOCK, 1, BLOCK), f32),
             pltpu.VMEM((FITS, NS), bf16),
-            pltpu.SemaphoreType.DMA((8,)),
+            pltpu.VMEM((FITS, NS), f32),
+            pltpu.SemaphoreType.DMA((9,)),
         ],
-        compiler_params=ROOM,
         name="pick_blocks",
     )(blocks, dosage, centers, scales, warm)
 
@@ -403,7 +408,6 @@
     from_left = onward(right)
     from_right = backward(left)
     fitted = exchange(fit_part, "x")
-    fitted, via_left, via_right = lax.optimization_barrier((fitted, via_left, via_right))
     far_a = onward(via_left)
     far_b = backward(via_right)
 
@@ -435,9 +439,7 @@
     owner = jnp.repeat(turned(strong_blocks, ahead, 0)[:EACH] // local_blocks, BLOCK)[None, :]
     share = jnp.where(owner == (place + 3) % 4, from_left, own)
     share = jnp.where(owner == (place + 1) % 4, from_right, share)
-    share = jnp.where(
-        owner == (place + 2) % 4, jnp.concatenate([far_a, far_b], axis=0), share
-    )
+    share = jnp.where(owner == (place + 2) % 4, jnp.concatenate([far_a, far_b], axis=0), share)
     arrived = exchange(message, PLANE)
     share_left = onward(share)
     share_right = backward(share)

time: 172 us -> 168 us (0.977)
  local copies, waits for them, and re-layouts: 13.2 us -> 6.61 us
  waiting for transfers between devices: 28.1 us -> 34.2 us
  starting transfers between devices: 67.9 us -> 62.1 us
  Pallas kernels: 14.1 us -> 17.2 us
    unnamed x36 -> x32, local copies, waits for them, and re-layouts: 11.2 us -> 4.67 us
    ppermute x5, waiting for transfers between devices: 13 us -> 19.1 us  [onward(): return lax.ppermute(value, 'x', [(i, (i + 1) % 4) for i in range(4)])]
    ppermute x9, starting transfers between devices: 17.2 us -> 13.6 us  [swap(): return lax.ppermute(value, 'core', [(0, 1), (1, 0)])]
    pallas_call x1, Pallas kernels: 3.33 us -> 6.49 us  [pick_blocks(): pl.pallas_call(pick_kernel, in_specs=[pl.BlockSpec(memory_space=pltpu.SME...]
    all_to_all x5, starting transfers between devices: 37.9 us -> 35.9 us  [exchange(): return lax.all_to_all(value, axis, 0, 0, tiled=True)]
where the time goes in v6:
time: 168 us; the launch traced here: 167 us
  starting transfers between devices  62.1 us (37%)
  blocking collectives  37.2 us (22%)
  waiting for transfers between devices  34.2 us (20%)
  Pallas kernels  17.2 us (10%)
  local copies, waits for them, and re-layouts  6.61 us (4%)
  other arithmetic  5.46 us (3%)
  matrix products  3.56 us (2%)
    all_to_all x4, blocking collectives, exchange(): return lax.all_to_all(value, axis, 0, 0, tiled=True)  37.2 us
    all_to_all x5, starting transfers between devices, exchange(): return lax.all_to_all(value, axis, 0, 0, tiled=True)  35.9 us
    ppermute x5, waiting for transfers between devices, onward(): return lax.ppermute(value, 'x', [(i, (i + 1) % 4) for i in range(4)])  19.1 us
    all_to_all x5, waiting for transfers between devices, exchange(): return lax.all_to_all(value, axis, 0, 0, tiled=True)  13.9 us
    ppermute x9, starting transfers between devices, swap(): return lax.ppermute(value, 'core', [(0, 1), (1, 0)])  13.6 us
    ppermute x5, starting transfers between devices, backward(): return lax.ppermute(value, 'x', [(i, (i + 3) % 4) for i in range(4)])  10.3 us
    pallas_call x1, Pallas kernels, pick_blocks(): pl.pallas_call(pick_kernel, in_specs=[pl.BlockSpec(memory_space=pltpu.SME...  6.49 us
    pallas_call x2, Pallas kernels, sweep(): pl.pallas_call(functools.partial(sweep_kernel, factor, extra is not None)...  6.2 us
  transfers between devices with their start and end apart: 24, of which 8 were waited for; matrix products, arithmetic and copies ran while one was open for 6% of the time, Pallas kernels for 2%

profile of v6, /device:TPU:1, one launch (start us, length us, event | category | flops | bytes accessed | tf_op | source)
XLA Modules:
  0.0 167.3 jit_solution(2347831430436271540)
XLA Ops:
  0.7 6.5 %pick_blocks.1 = (bf16[256,1024]{1,0:T(8,128)(2,1)}, bf16[256,1024]{1,0:T(8,128)(2,1)}, bf16[128,1024]{1,0:T(8,128)(2,1)}, bf16[128,1024]{1,0:T(8,128)(2,1)}, bf...) custom-call(s32[32]{0:T(128)} %block_ref.1, ...), custom_call_target="tpu_custom_call" | custom-call | tf_op jit(solution)/shard_map/pick_blocks/pallas_call | solution.py:140
  7.2 4.2 %all-to-all-start = ((bf16[4,32,256]{2,1,0:T(8,128)(2,1)}), bf16[4,32,256]{2,1,0:T(8,128)(2,1)S(1)}, u32[]{:S(2)}, u32[]{:S(2)}) async-start(bf16[4,32,256]{2,1,0:T(8,128)(2,1)} %get-tuple-element.59), calls=%async_computation | async-start | bytes 131072 | tf_op jit(solution)/shard_map/all_to_all | solution.py:362
  11.4 2.4 %collective-permute-start.17 = (f32[2,256]{1,0:T(2,128)S(1)}, f32[2,256]{1,0:T(2,128)S(1)}, u32[]{:S(2)}, u32[]{:S(2)}) collective-permute-start(f32[2,256]{1,0:T(2,128)S(1)} %pad_maximum_fusion.3.refs_4_), channel_id=1, source_target_pairs={{0,4},{4,0},{1,5},{5,1},{2,6},{6,2},{3,7},{7,3},{8,12},{12,8},{9,1... | collective-permute-start | bytes 6152 | tf_op jit(solution)/shard_map/ppermute | solution.py:366
  13.8 1.7 %collective-permute-start.1 = (bf16[128,1024]{1,0:T(8,128)(2,1)}, bf16[128,1024]{1,0:T(8,128)(2,1)}, u32[]{:S(2)}, u32[]{:S(2)}) collective-permute-start(bf16[128,1024]{1,0:T(8,128)(2,1)} %get-tuple-element.61), channel_id=1, source_target_pairs={{0,1},{1,2},{2,3},{3,0},{4,5},{5,6},{6,7},{7,4},{8,9},{9,10},{10,1... | collective-permute-start | bytes 786440 | tf_op jit(solution)/shard_map/ppermute | solution.py:370
  15.5 1.2 collective-permute-start.3
  16.7 1.5 collective-permute-start.5
  18.8 3.6 %convolution_subtract_fusion = f32[32,10240]{1,0:T(8,128)S(1)} fusion(bf16[32,256]{1,0:T(8,128)(2,1)S(1)} %get-tuple-element.89, bf16[256,10240]{1,0:T(8,128)(2,1)} %source_ref.1, f32[32]{0:T(128)S(1)} %get-tuple-element.88, f32[10240]{0:T(1024)} %bitcast.33), kind=kOutput, calls=%fused_computation | convolution fusion | flops 168427520 | bytes 6611072 | tf_op jit(solution)/shard_map/dot_general | solution.py:422
  22.4 1.6 collective-permute-done.1
  24.0 2.7 %collective-permute-start.4 = (bf16[128,1024]{1,0:T(8,128)(2,1)}, bf16[128,1024]{1,0:T(8,128)(2,1)S(1)}, u32[]{:S(2)}, u32[]{:S(2)}) collective-permute-start(bf16[128,1024]{1,0:T(8,128)(2,1)} %collective-permute-done.3), channel_id=1, source_target_pairs={{0,3},{1,0},{2,1},{3,2},{4,7},{5,4},{6,5},{7,6},{8,11},{9,8},{10,9... | collective-permute-start | bytes 786440 | tf_op jit(solution)/shard_map/ppermute | solution.py:374
  27.4 1.4 collective-permute-start.16
  29.2 11.6 %collective-permute-done.2 = bf16[128,1024]{1,0:T(8,128)(2,1)S(1)} collective-permute-done((bf16[128,1024]{1,0:T(8,128)(2,1)}, bf16[128,1024]{1,0:T(8,128)(2,1)S(1)}, u32[]{:S(2)}, u32[]{:S(2)}) %collective-permute-start.2) | collective-permute-done | bytes 262176 | tf_op jit(solution)/shard_map/ppermute | solution.py:370
  41.6 1.4 maximum_select_fusion.refs_0_.refs_6_
  43.4 2.3 %collective-permute-start.7 = (bf16[256,1024]{1,0:T(8,128)(2,1)S(1)}, bf16[256,1024]{1,0:T(8,128)(2,1)S(1)}, u32[]{:S(2)}, u32[]{:S(2)}) collective-permute-start(bf16[256,1024]{1,0:T(8,128)(2,1)S(1)} %maximum_select_fusion.refs_0_.refs_6_), channel_id=1, source_target_pairs={{0,3},{1,0},{2,1},{3,2},{4,7},{5,4},{6,5},{7,6},{8,11},{9,8},{10,9... | collective-permute-start | bytes 1572872 | tf_op jit(solution)/shard_map/ppermute | solution.py:374
  47.7 10.0 %all-to-all-start.1 = ((bf16[32,56,128]{2,1,0:T(8,128)(2,1)}), bf16[32,56,128]{2,1,0:T(8,128)(2,1)}, u32[]{:S(2)}, u32[]{:S(2)}) async-start(bf16[32,56,128]{2,1,0:T(8,128)(2,1)} %pad_maximum_fusion), calls=%async_computation.1 | async-start | bytes 917504 | tf_op jit(solution)/shard_map/all_to_all | solution.py:362
  57.7 1.6 collective-permute-start.11
  60.2 2.6 %collective-permute-start.10 = (bf16[128,1024]{1,0:T(8,128)(2,1)S(1)}, bf16[128,1024]{1,0:T(8,128)(2,1)}, u32[]{:S(2)}, u32[]{:S(2)}) collective-permute-start(bf16[128,1024]{1,0:T(8,128)(2,1)S(1)} %slice.72), channel_id=1, source_target_pairs={{0,3},{1,0},{2,1},{3,2},{4,7},{5,4},{6,5},{7,6},{8,11},{9,8},{10,9... | collective-permute-start | bytes 786440 | tf_op jit(solution)/shard_map/ppermute | solution.py:374
  62.8 5.9 %collective-permute-done.9.refs_2_.refs_8_ = bf16[128,1024]{1,0:T(8,128)(2,1)S(1)} collective-permute-done((bf16[128,1024]{1,0:T(8,128)(2,1)S(1)}, bf16[128,1024]{1,0:T(8,128)(2,1)S(1)}, u32[]{:S(2)}, u32[]{:S(2)}) %collective-permute-start.9) | collective-permute-done | bytes 262176 | tf_op jit(solution)/shard_map/ppermute | solution.py:370
  71.4 1.8 %first_sweep.1 = bf16[4,4,4096]{2,1,0:T(4,128)(2,1)S(1)} custom-call(bf16[4,256]{1,0:T(4,128)(2,1)S(1)} %get-tuple-element.93.residual_ref, bf16[4,256]{1,0:T(4,128)(2,1)S(1)} %collective-permute-done.other_ref, f32[2,4096]{1,0:T(2,128)S(1)} %copy-done.3, bf16[256,1024]{1,0:T(8,128)(2,1)S(1)} %maximum_select_fusion.refs_0_.refs_6_, ...), custom_call_target="tpu_custom_call" | custom-call | tf_op jit(solution)/shard_map/first_sweep/pallas_call | solution.py:195
  73.8 9.0 %all_to_all.45.got_ref = bf16[4,4,4096]{2,1,0:T(4,128)(2,1)S(1)} all-to-all(bf16[4,4,4096]{2,1,0:T(4,128)(2,1)} %copy-done.4), channel_id=1, replica_groups=mesh['z'=8,'y'=4,'core'=2,'x'=4] {'y'}, dimensions={0} | all-to-all | bytes 262144 | tf_op jit(solution)/shard_map/all_to_all | solution.py:362
  83.6 6.4 %all-to-all-start.3 = ((bf16[8,4,4096]{2,1,0:T(4,128)(2,1)}), bf16[8,4,4096]{2,1,0:T(4,128)(2,1)}, u32[]{:S(2)}, u32[]{:S(2)}) async-start(bf16[8,4,4096]{2,1,0:T(4,128)(2,1)} %copy-done.1), calls=%async_computation.3 | async-start | bytes 524288 | tf_op jit(solution)/shard_map/all_to_all | solution.py:362
  90.9 1.2 settle.1
  92.1 7.3 %all-to-all-done.3.refs_0_ = bf16[8,4,4096]{2,1,0:T(4,128)(2,1)} async-done(((bf16[8,4,4096]{2,1,0:T(4,128)(2,1)}), bf16[8,4,4096]{2,1,0:T(4,128)(2,1)}, u32[]{:S(2)}, u32[]{:S(2)}) %all-to-all-start.3) | async-done | bytes 262176 | tf_op jit(solution)/shard_map/all_to_all | solution.py:362
  100.4 3.1 %sweep.2 = (bf16[4,4,4480]{2,1,0:T(4,128)(2,1)S(1)}, f32[8,4096]{1,0:T(8,128)S(1)}) custom-call(bf16[8,4,4096]{2,1,0:T(4,128)(2,1)} %all-to-all-done.3.refs_0_, f32[8,4096]{1,0:T(8,128)S(1)} %copy-done.5, f32[2,4096]{1,0:T(2,128)S(1)} %copy-done.3, f32[4,128]{1,0:T(4,128)S(1)} %get-tuple-element.80.refs_3_.column_ref, ...), custom_call_target="tpu_custom_call" | custom-call | tf_op jit(solution)/shard_map/sweep/pallas_call | solution.py:328
  103.4 7.4 %all_to_all.46.got_ref = bf16[4,4,4480]{2,1,0:T(4,128)(2,1)S(1)} all-to-all(bf16[4,4,4480]{2,1,0:T(4,128)(2,1)S(1)} %get-tuple-element.82), channel_id=1, replica_groups=mesh['z'=8,'y'=4,'core'=2,'x'=4] {'y'}, dimensions={0} | all-to-all | bytes 286720 | tf_op jit(solution)/shard_map/all_to_all | solution.py:362
  110.9 13.4 %all_to_all.47.refs_0_ = bf16[8,4,5632]{2,1,0:T(4,128)(2,1)S(1)} all-to-all(bf16[8,4,5632]{2,1,0:T(4,128)(2,1)S(1)} %middle.4), channel_id=1, replica_groups=mesh['z'=8,'y'=4,'core'=2,'x'=4] {'z'}, dimensions={0} | all-to-all | bytes 720896 | tf_op jit(solution)/shard_map/all_to_all | solution.py:362
  124.3 3.1 %sweep.3 = (bf16[4,4,4096]{2,1,0:T(4,128)(2,1)S(1)}, f32[8,4096]{1,0:T(8,128)S(1)}) custom-call(bf16[8,4,5632]{2,1,0:T(4,128)(2,1)S(1)} %all_to_all.47.refs_0_, f32[8,4096]{1,0:T(8,128)S(1)} %get-tuple-element.83.refs_1_, f32[2,4096]{1,0:T(2,128)S(1)} %copy-done.3, f32[4,128]{1,0:T(4,128)S(1)} %get-tuple-element.80.refs_3_.column_ref, ...), custom_call_target="tpu_custom_call" | custom-call | tf_op jit(solution)/shard_map/sweep/pallas_call | solution.py:328
  128.1 7.3 %all_to_all.48.got_ref = bf16[4,4,4096]{2,1,0:T(4,128)(2,1)S(1)} all-to-all(bf16[4,4,4096]{2,1,0:T(4,128)(2,1)S(1)} %get-tuple-element.84), channel_id=1, replica_groups=mesh['z'=8,'y'=4,'core'=2,'x'=4] {'y'}, dimensions={0} | all-to-all | bytes 262144 | tf_op jit(solution)/shard_map/all_to_all | solution.py:362
  136.2 3.4 %all-to-all-start.7 = ((bf16[8,4,4096]{2,1,0:T(4,128)(2,1)}), bf16[8,4,4096]{2,1,0:T(4,128)(2,1)S(1)}, u32[]{:S(2)}, u32[]{:S(2)}) async-start(bf16[8,4,4096]{2,1,0:T(4,128)(2,1)} %middle.5), calls=%async_computation.7 | async-start | bytes 524288 | tf_op jit(solution)/shard_map/all_to_all | solution.py:362
  140.7 6.2 %collective-permute-start.18 = (f32[10240]{0:T(1024)S(1)}, f32[10240]{0:T(1024)S(1)}, u32[]{:S(2)}, u32[]{:S(2)}) collective-permute-start(f32[10240]{0:T(1024)S(1)} %slice.76), channel_id=1, source_target_pairs={{0,4},{4,0},{1,5},{5,1},{2,6},{6,2},{3,7},{7,3},{8,12},{12,8},{9,1... | collective-permute-start | bytes 122888 | tf_op jit(solution)/shard_map/ppermute | solution.py:366
  146.9 2.0 %all-to-all-done.7.got_ref = bf16[8,4,4096]{2,1,0:T(4,128)(2,1)S(1)} async-done(((bf16[8,4,4096]{2,1,0:T(4,128)(2,1)}), bf16[8,4,4096]{2,1,0:T(4,128)(2,1)S(1)}, u32[]{:S(2)}, u32[]{:S(2)}) %all-to-all-start.7) | async-done | bytes 262176 | tf_op jit(solution)/shard_map/all_to_all | solution.py:362
  149.6 11.8 %all-to-all-start.8 = ((f32[8,4,1024]{2,1,0:T(4,128)}), f32[8,4,1024]{2,1,0:T(4,128)S(1)}, u32[]{:S(2)}, u32[]{:S(2)}) async-start(f32[8,4,1024]{2,1,0:T(4,128)} %last.1), calls=%async_computation.8 | async-start | bytes 262144 | tf_op jit(solution)/shard_map/all_to_all | solution.py:362
  162.1 4.6 %all-to-all-done.8 = f32[8,4,1024]{2,1,0:T(4,128)S(1)} async-done(((f32[8,4,1024]{2,1,0:T(4,128)}), f32[8,4,1024]{2,1,0:T(4,128)S(1)}, u32[]{:S(2)}, u32[]{:S(2)}) %all-to-all-start.8) | async-done | bytes 131104 | tf_op jit(solution)/shard_map/all_to_all | solution.py:362
  (92 shorter events, 16.3 us)
Async XLA Ops:
  0.6 10.8 %copy-start.14 = (s32[256]{0:T(256)S(1)}, s32[256]{0:T(256)}, u32[]{:S(2)}) copy-start(s32[256]{0:T(256)} %param.17) | copy-start | bytes 3076
  0.6 10.7 %copy-start.13 = (f32[256]{0:T(256)S(1)}, f32[256]{0:T(256)}, u32[]{:S(2)}) copy-start(f32[256]{0:T(256)} %param.16) | copy-start | bytes 3076
  0.7 17.5 %copy-start.15 = (s32[32]{0:T(128)S(1)}, s32[32]{0:T(128)}, u32[]{:S(2)}) copy-start(s32[32]{0:T(128)} %block_ref.1) | copy-start | bytes 388
  7.2 11.4 %all-to-all-start = ((bf16[4,32,256]{2,1,0:T(8,128)(2,1)}), bf16[4,32,256]{2,1,0:T(8,128)(2,1)S(1)}, u32[]{:S(2)}, u32[]{:S(2)}) async-start(bf16[4,32,256]{2,1,0:T(8,128)(2,1)} %get-tuple-element.59), calls=%async_computation | async-start | bytes 131072 | tf_op jit(solution)/shard_map/all_to_all | solution.py:362
  11.4 7.1 %collective-permute-start.17 = (f32[2,256]{1,0:T(2,128)S(1)}, f32[2,256]{1,0:T(2,128)S(1)}, u32[]{:S(2)}, u32[]{:S(2)}) collective-permute-start(f32[2,256]{1,0:T(2,128)S(1)} %pad_maximum_fusion.3.refs_4_), channel_id=1, source_target_pairs={{0,4},{4,0},{1,5},{5,1},{2,6},{6,2},{3,7},{7,3},{8,12},{12,8},{9,1... | collective-permute-start | bytes 6152 | tf_op jit(solution)/shard_map/ppermute | solution.py:366
  13.8 10.2 %collective-permute-start.1 = (bf16[128,1024]{1,0:T(8,128)(2,1)}, bf16[128,1024]{1,0:T(8,128)(2,1)}, u32[]{:S(2)}, u32[]{:S(2)}) collective-permute-start(bf16[128,1024]{1,0:T(8,128)(2,1)} %get-tuple-element.61), channel_id=1, source_target_pairs={{0,1},{1,2},{2,3},{3,0},{4,5},{5,6},{6,7},{7,4},{8,9},{9,10},{10,1... | collective-permute-start | bytes 786440 | tf_op jit(solution)/shard_map/ppermute | solution.py:370
  15.5 8.5 %collective-permute-start.3 = (bf16[128,1024]{1,0:T(8,128)(2,1)}, bf16[128,1024]{1,0:T(8,128)(2,1)}, u32[]{:S(2)}, u32[]{:S(2)}) collective-permute-start(bf16[128,1024]{1,0:T(8,128)(2,1)} %get-tuple-element.62), channel_id=1, source_target_pairs={{0,3},{1,0},{2,1},{3,2},{4,7},{5,4},{6,5},{7,6},{8,11},{9,8},{10,9... | collective-permute-start | bytes 786440 | tf_op jit(solution)/shard_map/ppermute | solution.py:374
  16.7 24.0 %collective-permute-start.5 = (bf16[256,1024]{1,0:T(8,128)(2,1)}, bf16[256,1024]{1,0:T(8,128)(2,1)S(1)}, u32[]{:S(2)}, u32[]{:S(2)}) collective-permute-start(bf16[256,1024]{1,0:T(8,128)(2,1)} %get-tuple-element.63), channel_id=1, source_target_pairs={{0,3},{1,0},{2,1},{3,2},{4,7},{5,4},{6,5},{7,6},{8,11},{9,8},{10,9... | collective-permute-start | bytes 1572872 | tf_op jit(solution)/shard_map/ppermute | solution.py:374
  18.2 22.6 %collective-permute-start.6 = (bf16[256,1024]{1,0:T(8,128)(2,1)}, bf16[256,1024]{1,0:T(8,128)(2,1)S(1)}, u32[]{:S(2)}, u32[]{:S(2)}) collective-permute-start(bf16[256,1024]{1,0:T(8,128)(2,1)} %get-tuple-element.64), channel_id=1, source_target_pairs={{0,1},{1,2},{2,3},{3,0},{4,5},{5,6},{6,7},{7,4},{8,9},{9,10},{10,1... | collective-permute-start | bytes 1572872 | tf_op jit(solution)/shard_map/ppermute | solution.py:370
  18.8 22.8 %copy-start.10 = (bf16[256,1024]{1,0:T(8,128)(2,1)S(1)}, bf16[256,1024]{1,0:T(8,128)(2,1)}, u32[]{:S(2)}) copy-start(bf16[256,1024]{1,0:T(8,128)(2,1)} %get-tuple-element.65) | copy-start | bytes 1572868
  24.0 16.7 %collective-permute-start.2 = (bf16[128,1024]{1,0:T(8,128)(2,1)}, bf16[128,1024]{1,0:T(8,128)(2,1)S(1)}, u32[]{:S(2)}, u32[]{:S(2)}) collective-permute-start(bf16[128,1024]{1,0:T(8,128)(2,1)} %collective-permute-done.1), channel_id=1, source_target_pairs={{0,1},{1,2},{2,3},{3,0},{4,5},{5,6},{6,7},{7,4},{8,9},{9,10},{10,1... | collective-permute-start | bytes 786440 | tf_op jit(solution)/shard_map/ppermute | solution.py:370
  24.0 16.7 %collective-permute-start.4 = (bf16[128,1024]{1,0:T(8,128)(2,1)}, bf16[128,1024]{1,0:T(8,128)(2,1)S(1)}, u32[]{:S(2)}, u32[]{:S(2)}) collective-permute-start(bf16[128,1024]{1,0:T(8,128)(2,1)} %collective-permute-done.3), channel_id=1, source_target_pairs={{0,3},{1,0},{2,1},{3,2},{4,7},{5,4},{6,5},{7,6},{8,11},{9,8},{10,9... | collective-permute-start | bytes 786440 | tf_op jit(solution)/shard_map/ppermute | solution.py:374
  27.4 18.3 %collective-permute-start.16 = (bf16[16,10240]{1,0:T(8,128)(2,1)}, bf16[16,10240]{1,0:T(8,128)(2,1)}, u32[]{:S(2)}, u32[]{:S(2)}) collective-permute-start(bf16[16,10240]{1,0:T(8,128)(2,1)} %dynamic-slice_convert_fusion), channel_id=1, source_target_pairs={{0,4},{4,0},{1,5},{5,1},{2,6},{6,2},{3,7},{7,3},{8,12},{12,8},{9,1... | collective-permute-start | bytes 983048 | tf_op jit(solution)/shard_map/ppermute | solution.py:366
  43.0 16.3 %collective-permute-start.8 = (bf16[256,1024]{1,0:T(8,128)(2,1)S(1)}, bf16[256,1024]{1,0:T(8,128)(2,1)S(1)}, u32[]{:S(2)}, u32[]{:S(2)}) collective-permute-start(bf16[256,1024]{1,0:T(8,128)(2,1)S(1)} %maximum_select_fusion.refs_0_.refs_6_), channel_id=1, source_target_pairs={{0,1},{1,2},{2,3},{3,0},{4,5},{5,6},{6,7},{7,4},{8,9},{9,10},{10,1... | collective-permute-start | bytes 1572872 | tf_op jit(solution)/shard_map/ppermute | solution.py:370
  43.4 16.1 %collective-permute-start.7 = (bf16[256,1024]{1,0:T(8,128)(2,1)S(1)}, bf16[256,1024]{1,0:T(8,128)(2,1)S(1)}, u32[]{:S(2)}, u32[]{:S(2)}) collective-permute-start(bf16[256,1024]{1,0:T(8,128)(2,1)S(1)} %maximum_select_fusion.refs_0_.refs_6_), channel_id=1, source_target_pairs={{0,3},{1,0},{2,1},{3,2},{4,7},{5,4},{6,5},{7,6},{8,11},{9,8},{10,9... | collective-permute-start | bytes 1572872 | tf_op jit(solution)/shard_map/ppermute | solution.py:374
  46.8 24.5 %copy-start.3 = (f32[2,4096]{1,0:T(2,128)S(1)}, f32[2,4096]{1,0:T(2,128)}, u32[]{:S(2)}) copy-start(f32[2,4096]{1,0:T(2,128)} %get-tuple-element.60.wide_ref.refs_2_) | copy-start | bytes 98308
  47.7 26.2 %all-to-all-start.1 = ((bf16[32,56,128]{2,1,0:T(8,128)(2,1)}), bf16[32,56,128]{2,1,0:T(8,128)(2,1)}, u32[]{:S(2)}, u32[]{:S(2)}) async-start(bf16[32,56,128]{2,1,0:T(8,128)(2,1)} %pad_maximum_fusion), calls=%async_computation.1 | async-start | bytes 917504 | tf_op jit(solution)/shard_map/all_to_all | solution.py:362
  57.7 11.8 %collective-permute-start.11 = (bf16[256,1024]{1,0:T(8,128)(2,1)S(1)}, bf16[256,1024]{1,0:T(8,128)(2,1)S(1)}, u32[]{:S(2)}, u32[]{:S(2)}) collective-permute-start(bf16[256,1024]{1,0:T(8,128)(2,1)S(1)} %maximum_select_fusion.refs_0_.refs_6_), channel_id=1, source_target_pairs={{0,4},{4,0},{1,5},{5,1},{2,6},{6,2},{3,7},{7,3},{8,12},{12,8},{9,1... | collective-permute-start | bytes 1572872 | tf_op jit(solution)/shard_map/ppermute | solution.py:366
  59.3 9.4 %collective-permute-start.9 = (bf16[128,1024]{1,0:T(8,128)(2,1)S(1)}, bf16[128,1024]{1,0:T(8,128)(2,1)S(1)}, u32[]{:S(2)}, u32[]{:S(2)}) collective-permute-start(bf16[128,1024]{1,0:T(8,128)(2,1)S(1)} %slice.71), channel_id=1, source_target_pairs={{0,1},{1,2},{2,3},{3,0},{4,5},{5,6},{6,7},{7,4},{8,9},{9,10},{10,1... | collective-permute-start | bytes 786440 | tf_op jit(solution)/shard_map/ppermute | solution.py:370
  59.6 10.5 %collective-permute-start.12 = (bf16[256,1024]{1,0:T(8,128)(2,1)S(1)}, bf16[256,1024]{1,0:T(8,128)(2,1)S(1)}, u32[]{:S(2)}, u32[]{:S(2)}) collective-permute-start(bf16[256,1024]{1,0:T(8,128)(2,1)S(1)} %collective-permute-done.7.refs_1_.refs_7_), channel_id=1, source_target_pairs={{0,4},{4,0},{1,5},{5,1},{2,6},{6,2},{3,7},{7,3},{8,12},{12,8},{9,1... | collective-permute-start | bytes 1572872 | tf_op jit(solution)/shard_map/ppermute | solution.py:366
  59.7 10.4 %collective-permute-start.15 = (bf16[256,1024]{1,0:T(8,128)(2,1)S(1)}, bf16[256,1024]{1,0:T(8,128)(2,1)S(1)}, u32[]{:S(2)}, u32[]{:S(2)}) collective-permute-start(bf16[256,1024]{1,0:T(8,128)(2,1)S(1)} %collective-permute-done.8.refs_4_.refs_10_), channel_id=1, source_target_pairs={{0,4},{4,0},{1,5},{5,1},{2,6},{6,2},{3,7},{7,3},{8,12},{12,8},{9,1... | collective-permute-start | bytes 1572872 | tf_op jit(solution)/shard_map/ppermute | solution.py:366
  60.2 9.3 %collective-permute-start.10 = (bf16[128,1024]{1,0:T(8,128)(2,1)S(1)}, bf16[128,1024]{1,0:T(8,128)(2,1)}, u32[]{:S(2)}, u32[]{:S(2)}) collective-permute-start(bf16[128,1024]{1,0:T(8,128)(2,1)S(1)} %slice.72), channel_id=1, source_target_pairs={{0,3},{1,0},{2,1},{3,2},{4,7},{5,4},{6,5},{7,6},{8,11},{9,8},{10,9... | collective-permute-start | bytes 786440 | tf_op jit(solution)/shard_map/ppermute | solution.py:374
  68.7 2.1 %collective-permute-start.13 = (bf16[128,1024]{1,0:T(8,128)(2,1)S(1)}, bf16[128,1024]{1,0:T(8,128)(2,1)}, u32[]{:S(2)}, u32[]{:S(2)}) collective-permute-start(bf16[128,1024]{1,0:T(8,128)(2,1)S(1)} %collective-permute-done.9.refs_2_.refs_8_), channel_id=1, source_target_pairs={{0,4},{4,0},{1,5},{5,1},{2,6},{6,2},{3,7},{7,3},{8,12},{12,8},{9,1... | collective-permute-start | bytes 786440 | tf_op jit(solution)/shard_map/ppermute | solution.py:366
  69.5 1.9 %collective-permute-start.14 = (bf16[128,1024]{1,0:T(8,128)(2,1)}, bf16[128,1024]{1,0:T(8,128)(2,1)}, u32[]{:S(2)}, u32[]{:S(2)}) collective-permute-start(bf16[128,1024]{1,0:T(8,128)(2,1)} %collective-permute-done.10.refs_3_.refs_9_), channel_id=1, source_target_pairs={{0,4},{4,0},{1,5},{5,1},{2,6},{6,2},{3,7},{7,3},{8,12},{12,8},{9,1... | collective-permute-start | bytes 786440 | tf_op jit(solution)/shard_map/ppermute | solution.py:366
  69.5 1.9 %collective-permute-start = (bf16[4,256]{1,0:T(4,128)(2,1)S(1)}, bf16[4,256]{1,0:T(4,128)(2,1)S(1)}, u32[]{:S(2)}, u32[]{:S(2)}) collective-permute-start(bf16[4,256]{1,0:T(4,128)(2,1)S(1)} %get-tuple-element.92), channel_id=1, source_target_pairs={{0,4},{4,0},{1,5},{5,1},{2,6},{6,2},{3,7},{7,3},{8,12},{12,8},{9,1... | collective-permute-start | bytes 6152 | tf_op jit(solution)/shard_map/ppermute | solution.py:366
  71.4 18.6 %copy-start.8 = (f32[8]{0:T(128)S(1)}, f32[8]{0:T(128)}, u32[]{:S(2)}) copy-start(f32[8]{0:T(128)} %penalty_ref.1) | copy-start | bytes 100
  71.4 18.6 %copy-start.9 = (f32[32]{0:T(128)S(1)}, f32[32]{0:T(128)}, u32[]{:S(2)}) copy-start(f32[32]{0:T(128)} %step_ref.1) | copy-start | bytes 388
  83.6 15.8 %all-to-all-start.3 = ((bf16[8,4,4096]{2,1,0:T(4,128)(2,1)}), bf16[8,4,4096]{2,1,0:T(4,128)(2,1)}, u32[]{:S(2)}, u32[]{:S(2)}) async-start(bf16[8,4,4096]{2,1,0:T(4,128)(2,1)} %copy-done.1), calls=%async_computation.3 | async-start | bytes 524288 | tf_op jit(solution)/shard_map/all_to_all | solution.py:362
  128.1 20.8 %copy-start.7 = (f32[8,4096]{1,0:T(8,128)S(1)}, f32[8,4096]{1,0:T(8,128)}, u32[]{:S(2)}) copy-start(f32[8,4096]{1,0:T(8,128)} %copy-done.6) | copy-start | bytes 393220
  136.2 12.7 %all-to-all-start.7 = ((bf16[8,4,4096]{2,1,0:T(4,128)(2,1)}), bf16[8,4,4096]{2,1,0:T(4,128)(2,1)S(1)}, u32[]{:S(2)}, u32[]{:S(2)}) async-start(bf16[8,4,4096]{2,1,0:T(4,128)(2,1)} %middle.5), calls=%async_computation.7 | async-start | bytes 524288 | tf_op jit(solution)/shard_map/all_to_all | solution.py:362
  140.7 20.8 %collective-permute-start.18 = (f32[10240]{0:T(1024)S(1)}, f32[10240]{0:T(1024)S(1)}, u32[]{:S(2)}, u32[]{:S(2)}) collective-permute-start(f32[10240]{0:T(1024)S(1)} %slice.76), channel_id=1, source_target_pairs={{0,4},{4,0},{1,5},{5,1},{2,6},{6,2},{3,7},{7,3},{8,12},{12,8},{9,1... | collective-permute-start | bytes 122888 | tf_op jit(solution)/shard_map/ppermute | solution.py:366
  149.6 17.0 %all-to-all-start.8 = ((f32[8,4,1024]{2,1,0:T(4,128)}), f32[8,4,1024]{2,1,0:T(4,128)S(1)}, u32[]{:S(2)}, u32[]{:S(2)}) async-start(f32[8,4,1024]{2,1,0:T(4,128)} %last.1), calls=%async_computation.8 | async-start | bytes 262144 | tf_op jit(solution)/shard_map/all_to_all | solution.py:362
  (8 other events, 8.5 us)
